TPU v7x, 256 devices: a whole 4x4x8 slice. The times are simulated.
256 devices in a mesh: cells: 64 (over x_lo, y, z), tracers: 4 (over x_hi, core).
Axes of the slice: x: 4 (x_hi: 2, x_lo: 2; x = x_hi * 2 + x_lo), y: 4, z: 8, core: 2. Of those that a mesh axis runs over, the one named last changes fastest.
Arguments:
- pulses: float32 [4096, 256, 128], P('tracers', 'cells'), may hold values from -6 to 6
- wind_x: float32 [256, 128], P('cells'), may hold values from -0.24 to 0.24
- wind_y: float32 [256, 128], P('cells'), may hold values from -0.24 to 0.24
- obs_tile: int32 [8192, 1], P('cells'), may hold values from 0 to 63; in each aligned block of 128 rows (0 to 127, 128 to 255, ...) at most 4 rows name the same one
- obs_weight: bfloat16 [8192, 512], P('cells'), may hold values from 0.099609375 to 10
- obs_precision: bfloat16 [8192], P('cells'), may hold values from 0.0029907227 to 0.099609375
Outputs:
- gram: float32 [4096, 4096], P('cells', 'tracers')
Inputs may be any that keep to these rules, and one draw needn't show every extreme that they name: `obs_tile`: among the rows of one index of cells no tile is named by more than 4 rows, a bound that some block reaches of them.
All inputs are finite; a program needn't handle non-finite values.
Results may differ from a plain program's by a relative error of at most 0.0031.
Values may be sent and summed in bfloat16 or wider, within the bound.
No kernel may reach another device: no remote copies, remote signals or barrier semaphores. Data moves between devices by JAX's collectives and lax.ppermute only.
A program may use at most 64 MiB of HBM per device.

v0:
```python
import jax
import jax.numpy as jnp
from jax import lax
from jax.experimental import pallas as pl
from jax.experimental.pallas import tpu as pltpu
from jax.sharding import Mesh, PartitionSpec as P


STEPS = 3
GRANT = 16 * 1024 * 1024
CAP = 4
XY = ("xl", "y")
CELLS = ("xl", "y", "z")
TRACERS = ("xh", "core")
PLANE = XY + TRACERS


def shifted(value, axis, steps):
    count = lax.axis_size(axis)
    return lax.ppermute(value, axis, [(i, (i + steps) % count) for i in range(count)])


def exchanged(value, axis):
    return lax.all_to_all(value, axis, split_axis=0, concat_axis=0, tiled=True)


def edge_rows(pulse_ref, wind_x_ref, wind_y_ref, first_ref, last_ref):
    count = pulse_ref.shape[0] // 4
    rows = [pulse_ref[pl.ds(r, count, 4), :].astype(jnp.bfloat16) for r in range(4)]
    for r in range(STEPS):
        first_ref[r * count : (r + 1) * count] = rows[r]
        last_ref[r * count : (r + 1) * count] = rows[r + 1]
    winds = jnp.concatenate([wind_x_ref[...], wind_y_ref[...]], axis=0)
    coarse = winds.astype(jnp.bfloat16)
    fine = (winds - coarse.astype(jnp.float32)).astype(jnp.bfloat16)
    both = jnp.concatenate([coarse.astype(jnp.float32), fine.astype(jnp.float32)], axis=0)
    first_ref[STEPS * count :] = both.astype(jnp.bfloat16)
    last_ref[STEPS * count :] = both.astype(jnp.bfloat16)


def edges(pulses, wind_x, wind_y):
    tracers = pulses.shape[0] // 4
    shape = jax.ShapeDtypeStruct((STEPS * tracers + 16, 128), jnp.bfloat16)
    return pl.pallas_call(
        edge_rows,
        out_shape=[shape, shape],
        compiler_params=pltpu.CompilerParams(vmem_limit_bytes=GRANT),
        name="edges",
    )(pulses, wind_x, wind_y)


PIECE = 16


def transport_body(
    pulse_ref, a0, a1, a2, a_winds, b0, b1, b2, b_winds, wind_x_ref, wind_y_ref, out_ref, coef_ref
):
    count = out_ref.shape[0]

    @pl.when(pl.program_id(0) == 0)
    def _():
        above = a_winds[...].astype(jnp.float32)
        below = b_winds[...].astype(jnp.float32)
        above = above[0:8] + above[8:16]
        below = below[0:8] + below[8:16]
        wind_x = jnp.concatenate([above[2:4], wind_x_ref[...], below[0:2]], axis=0)
        wind_y = jnp.concatenate([above[6:8], wind_y_ref[...], below[4:6]], axis=0)
        next_y = jnp.concatenate([above[7:8], wind_y_ref[...], below[4:7]], axis=0)
        gain_x, loss_x = jnp.maximum(wind_x, 0.0), jnp.minimum(wind_x, 0.0)
        gain_y, loss_y = jnp.maximum(wind_y, 0.0), jnp.minimum(wind_y, 0.0)
        keep = 1.0 + loss_x - pltpu.roll(gain_x, 127, 1) + loss_y - jnp.maximum(next_y, 0.0)
        parts = [
            keep, gain_x, -pltpu.roll(loss_x, 127, 1), gain_y, -jnp.minimum(next_y, 0.0)
        ]
        for k, part in enumerate(parts):
            for w in range(8):
                coef_ref[k * 8 + w] = jnp.broadcast_to(part[w : w + 1], (PIECE, 128))

    for piece in range(count // PIECE):
        at = piece * PIECE
        field = (
            [ref[at : at + PIECE].astype(jnp.float32) for ref in (a0, a1, a2)]
            + [pulse_ref[pl.ds(4 * at + r, PIECE, 4), :] for r in range(4)]
            + [ref[at : at + PIECE].astype(jnp.float32) for ref in (b0, b1, b2)]
        )
        for step in range(STEPS):
            new = []
            for i in range(len(field) - 2):
                w = step + i
                here = field[i + 1]
                new.append(
                    coef_ref[w] * here
                    + coef_ref[8 + w] * pltpu.roll(here, 1, 1)
                    + coef_ref[16 + w] * pltpu.roll(here, 127, 1)
                    + coef_ref[24 + w] * field[i]
                    + coef_ref[32 + w] * field[i + 2]
                )
            field = new
        for r in range(4):
            out_ref[at : at + PIECE, r * 128 : (r + 1) * 128] = field[r].astype(jnp.bfloat16)


def transport(pulses, above, below, wind_x, wind_y, block=256):
    tracers = pulses.shape[0] // 4
    steps = tracers // block
    halo = [
        pl.BlockSpec((block, 128), lambda i, r=r: (r * steps + i, 0)) for r in range(STEPS)
    ] + [pl.BlockSpec((16, 128), lambda i: (STEPS * tracers // 16, 0))]
    wind = pl.BlockSpec((4, 128), lambda i: (0, 0))
    return pl.pallas_call(
        transport_body,
        grid=(steps,),
        in_specs=[pl.BlockSpec((4 * block, 128), lambda i: (i, 0))] + halo + halo + [wind, wind],
        out_specs=pl.BlockSpec((block, 512), lambda i: (i, 0)),
        out_shape=jax.ShapeDtypeStruct((tracers, 512), jnp.bfloat16),
        scratch_shapes=[pltpu.VMEM((40, PIECE, 128), jnp.float32)],
        compiler_params=pltpu.CompilerParams(vmem_limit_bytes=GRANT),
        name="transport",
    )(pulses, *[above] * 4, *[below] * 4, wind_x, wind_y)


def jacobian_body(rows_ref, low_ref, high_ref, out_ref, full_ref):
    @pl.when(pl.program_id(0) == 0)
    def _():
        count, width = rows_ref.shape
        mine = rows_ref[...].astype(jnp.float32).reshape(count // 8, 8, width)
        swap = pltpu.roll(mine, 4, 1)
        top = lax.broadcasted_iota(jnp.int32, mine.shape, 1) < 4
        left = jnp.where(top, mine, swap).reshape(count, width)
        right = jnp.where(top, swap, mine).reshape(count, width)
        full_ref[:, :width] = left.astype(jnp.bfloat16)
        full_ref[:, width:] = right.astype(jnp.bfloat16)

    dims = (((1,), (1,)), ((), ()))
    full = full_ref[...]
    low = lax.dot_general(full, low_ref[...], dims, preferred_element_type=jnp.float32)
    high = lax.dot_general(full, high_ref[...], dims, preferred_element_type=jnp.float32)
    row = lax.broadcasted_iota(jnp.int32, low.shape, 0)
    out_ref[...] = jnp.where((row & 4) == 0, low, high).astype(jnp.bfloat16)


def jacobian(rows, sampled, block=256):
    tracers = sampled.shape[0]
    count, width = rows.shape
    steps = tracers // 2 // block
    return pl.pallas_call(
        jacobian_body,
        grid=(steps,),
        in_specs=[
            pl.BlockSpec((count, width), lambda i: (0, 0)),
            pl.BlockSpec((block, 512), lambda i: (i, 0)),
            pl.BlockSpec((block, 512), lambda i: (steps + i, 0)),
        ],
        out_specs=pl.BlockSpec((count, block), lambda i: (0, i)),
        out_shape=jax.ShapeDtypeStruct((count, tracers // 2), jnp.bfloat16),
        scratch_shapes=[pltpu.VMEM((count, 2 * width), jnp.bfloat16)],
        compiler_params=pltpu.CompilerParams(vmem_limit_bytes=GRANT),
        name="jacobian",
    )(rows, sampled, sampled)


def gram_body(place_ref, same_ref, cross_ref, across_ref, other_ref, *refs):
    cols, out_ref, rows_ref, cols_ref = refs[:-3], refs[-3], refs[-2], refs[-1]
    block = same_ref.shape[0]

    @pl.when(pl.program_id(0) == 0)
    def _():
        parts = [same_ref[...], cross_ref[...]]
        for ref in (across_ref, other_ref):
            parts += [ref[s : s + block] for s in range(0, ref.shape[0], block)]
        for k, part in enumerate(parts):
            at = pl.multiple_of(place_ref[k] * block, block)
            rows_ref[:, pl.ds(at, block)] = part.T

    for k, ref in enumerate(cols):
        at = pl.multiple_of(place_ref[8 + k] * block, block)
        cols_ref[pl.ds(at, block), :] = ref[...]
    out_ref[...] = lax.dot_general(
        rows_ref[...], cols_ref[...], (((1,), (0,)), ((), ())), preferred_element_type=jnp.float32
    ).astype(jnp.bfloat16)


def gram_tile(place, same, cross, across, other, cols, block=256):
    obs, tracers = cols[0].shape
    width = same.shape[1]
    whole = lambda v: pl.BlockSpec(v.shape, lambda i: (0, 0))
    return pl.pallas_call(
        gram_body,
        grid=(tracers // block,),
        in_specs=[pl.BlockSpec(memory_space=pltpu.SMEM)]
        + [whole(v) for v in (same, cross, across, other)]
        + [pl.BlockSpec((obs, block), lambda i: (0, i))] * len(cols),
        out_specs=pl.BlockSpec((width, block), lambda i: (0, i)),
        out_shape=jax.ShapeDtypeStruct((width, tracers), jnp.bfloat16),
        scratch_shapes=[
            pltpu.VMEM((width, len(cols) * obs), jnp.bfloat16),
            pltpu.VMEM((len(cols) * obs, block), jnp.bfloat16),
        ],
        compiler_params=pltpu.CompilerParams(vmem_limit_bytes=GRANT),
        name="gram",
    )(place, same, cross, across, other, *cols)


def on_device(pulses, wind_x, wind_y, obs_tile, obs_weight, obs_precision):
    tracers = pulses.shape[0]
    cells = lax.axis_size(CELLS)
    obs = obs_tile.shape[0]
    half = tracers // 2
    pulses = pulses.reshape(tracers * 4, 128)

    first, last = edges(pulses, wind_x, wind_y)
    above = shifted(last, CELLS, 1)
    below = shifted(first, CELLS, -1)
    sampled = transport(pulses, above, below, wind_x, wind_y)

    tile = obs_tile[:, 0]
    order = jnp.arange(obs)
    earlier = (tile[:, None] == tile[None, :]) & (order[None, :] < order[:, None])
    slot = 2 * CAP * tile + jnp.sum(earlier.astype(jnp.int32), axis=1)
    lanes = jnp.arange(2 * CAP * cells)[None, :]
    chosen = [(slot[:, None] + CAP * h == lanes).astype(jnp.bfloat16) for h in range(2)]
    wide = obs_weight.astype(jnp.float32)
    averaging = (wide / jnp.sum(wide, axis=1, keepdims=True)).astype(jnp.bfloat16)
    split = obs_weight.shape[1] // 2
    rows_out = lax.dot_general(
        jnp.concatenate(chosen, axis=0),
        jnp.concatenate([averaging[:, :split], averaging[:, split:]], axis=0),
        (((0,), (0,)), ((), ())),
        preferred_element_type=jnp.float32,
    ).astype(jnp.bfloat16)
    rows_in = exchanged(rows_out.reshape(cells, 2 * CAP, split), CELLS)

    jac_tile = jacobian(rows_in.reshape(cells * 2 * CAP, split), sampled)
    jac_back = exchanged(jac_tile.reshape(cells, 2 * CAP, half), CELLS)
    jac_back = jac_back.reshape(cells * 2 * CAP, half)
    jac = [
        lax.dot_general(
            c, jac_back, (((1,), (0,)), ((), ())), preferred_element_type=jnp.float32
        )
        for c in chosen
    ]
    precision = obs_precision.astype(jnp.float32)[:, None]
    weighted = jnp.concatenate([precision * j for j in jac], axis=1).astype(jnp.bfloat16)
    low, high = [j.astype(jnp.bfloat16) for j in jac]

    group = lax.axis_size(XY)
    peers = lax.axis_size(TRACERS)
    here = lax.axis_index(XY)
    odd = here % 2
    pairs = [(i // peers, i % peers) for i in range(group * peers)]
    to_same = [(a * peers + q, (2 * q + a % 2) * peers + a // 2) for a, q in pairs]
    to_cross = [(a * peers + q, (2 * q + 1 - a % 2) * peers + a // 2) for a, q in pairs]
    same = lax.ppermute(jnp.where(odd == 0, low, high), PLANE, to_same)
    cross = lax.ppermute(jnp.where(odd == 0, high, low), PLANE, to_cross)
    across = shifted(jnp.concatenate([same, cross], axis=0), "xh", 1)
    other = shifted(jnp.concatenate([same, cross, across], axis=0), "core", 1)

    beside = shifted(weighted, "xl", 1)
    deep = lax.axis_size("y")
    cols = [weighted, beside]
    for value in (weighted, beside):
        for d in range(1, deep):
            cols.append(shifted(value, "y", d))
    xl, y = lax.axis_index("xl"), lax.axis_index("y")
    owners = [here, (1 - xl) * deep + y]
    owners += [xl * deep + (y - d) % deep for d in range(1, deep)]
    owners += [(1 - xl) * deep + (y - d) % deep for d in range(1, deep)]
    tracer = lax.axis_index(TRACERS)
    row_owners = [2 * (tracer ^ flip) + (odd ^ s) for flip in (0, 2, 1, 3) for s in (0, 1)]
    place = jnp.stack(row_owners + owners).astype(jnp.int32)

    partial = gram_tile(place, same, cross, across, other, cols)
    depth = lax.axis_size("z")
    parts = exchanged(partial.reshape(depth, half // depth, tracers), "z")
    return jnp.sum(parts.astype(jnp.float32), axis=0)


def solution(mesh):
    fine = Mesh(mesh.devices.reshape(2, 4, 8, 2, 2), CELLS + TRACERS)
    placed = (
        P(TRACERS, CELLS, None),
        P(CELLS, None),
        P(CELLS, None),
        P(CELLS, None),
        P(CELLS, None),
        P(CELLS),
    )
    return jax.shard_map(
        on_device, mesh=fine, in_specs=placed, out_specs=P(CELLS, TRACERS), check_vma=False
    )
```

profile of v0, /device:TPU:4, one launch (start us, length us, event | category | flops | bytes accessed | tf_op | source)
XLA Modules:
  0.0 153.0 jit_solution(11413589582710862413)
XLA Ops:
  0.0 0.0 copy-start.7
  0.0 0.0 copy-start
  0.0 1.6 %copy-done = f32[1024,4,128]{2,1,0:T(4,128)S(1)} copy-done((f32[1024,4,128]{2,1,0:T(4,128)S(1)}, f32[1024,4,128]{2,1,0:T(4,128)}, u32[]{:S(2)}) %copy-start) | copy-done | bytes 2097176
  1.6 0.0 copy-start.2
  1.6 0.7 copy-done.2
  2.3 0.0 copy-start.4
  2.3 0.7 copy-done.4
  3.0 0.0 copy-start.6
  3.0 0.0 copy-start.3
  3.0 0.0 copy-start.5
  3.0 1.1 edges.1
  4.1 1.9 %collective-permute-start = (bf16[3088,128]{1,0:T(8,128)(2,1)}, bf16[3088,128]{1,0:T(8,128)(2,1)S(1)}, u32[]{:S(2)}, u32[]{:S(2)}) collective-permute-start(bf16[3088,128]{1,0:T(8,128)(2,1)} %get-tuple-element.7), channel_id=1, source_target_pairs={{0,4},{4,8},{8,12},{12,16},{16,20},{20,24},{24,28},{28,32},{32,36}... | collective-permute-start | bytes 2371592 | tf_op jit(solution)/shard_map/ppermute | solution.py:20
  6.0 7.0 %collective-permute-start.1 = (bf16[3088,128]{1,0:T(8,128)(2,1)S(1)}, bf16[3088,128]{1,0:T(8,128)(2,1)S(1)}, u32[]{:S(2)}, u32[]{:S(2)}) collective-permute-start(bf16[3088,128]{1,0:T(8,128)(2,1)S(1)} %get-tuple-element.8), channel_id=1, source_target_pairs={{0,252},{4,0},{8,4},{12,8},{16,12},{20,16},{24,20},{28,24},{32,28}... | collective-permute-start | bytes 2371592 | tf_op jit(solution)/shard_map/ppermute | solution.py:20
  13.0 0.0 copy-done.7
  13.0 0.2 convert_reduce_fusion.2
  13.2 0.0 copy-done.6
  13.2 0.1 convert_reduce_fusion.1
  13.3 0.1 fusion.8
  13.4 0.1 iota_compare_fusion
  13.6 1.1 fusion
  14.6 7.0 %all-to-all-start = ((bf16[64,8,256]{2,1,0:T(8,128)(2,1)}), bf16[64,8,256]{2,1,0:T(8,128)(2,1)S(1)}, u32[]{:S(2)}, u32[]{:S(2)}) async-start(bf16[64,8,256]{2,1,0:T(8,128)(2,1)} %fusion), calls=%async_computation | async-start | bytes 524288 | tf_op jit(solution)/shard_map/all_to_all | solution.py:24
  21.7 10.9 %collective-permute-done.a0.a1.a2.a_winds = bf16[3088,128]{1,0:T(8,128)(2,1)S(1)} collective-permute-done((bf16[3088,128]{1,0:T(8,128)(2,1)}, bf16[3088,128]{1,0:T(8,128)(2,1)S(1)}, u32[]{:S(2)}, u32[]{:S(2)}) %collective-permute-start) | collective-permute-done | bytes 790560 | tf_op jit(solution)/shard_map/ppermute | solution.py:20
  32.5 1.9 %collective-permute-done.1.b0.b1.b2.b_winds = bf16[3088,128]{1,0:T(8,128)(2,1)S(1)} collective-permute-done((bf16[3088,128]{1,0:T(8,128)(2,1)S(1)}, bf16[3088,128]{1,0:T(8,128)(2,1)S(1)}, u32[]{:S(2)}, u32[]{:S(2)}) %collective-permute-start.1) | collective-permute-done | bytes 790560 | tf_op jit(solution)/shard_map/ppermute | solution.py:20
  34.5 0.0 copy-done.3
  34.5 0.0 copy-done.5
  34.5 0.0 copy-start.1
  34.5 1.6 %copy-done.1 = f32[1024,4,128]{2,1,0:T(4,128)S(1)} copy-done((f32[1024,4,128]{2,1,0:T(4,128)S(1)}, f32[1024,4,128]{2,1,0:T(4,128)}, u32[]{:S(2)}) %copy-start.1) | copy-done | bytes 2097176
  36.1 10.3 %transport.1.low_ref.high_ref = bf16[1024,512]{1,0:T(8,128)(2,1)S(1)} custom-call(f32[4096,128]{1,0:T(8,128)S(1)} %bitcast.41, bf16[3088,128]{1,0:T(8,128)(2,1)S(1)} %collective-permute-done.a0.a1.a2.a_winds, bf16[3088,128]{1,0:T(8,128)(2,1)S(1)} %collective-permute-done.a0.a1.a2.a_winds, bf16[3088,128]{1,0:T(8,128)(2,1)S(1)} %collective-permute-done.a0.a1.a2.a_winds, ...), custom_call_target="tpu_custom_call" | custom-call | tf_op jit(solution)/shard_map/transport/pallas_call | solution.py:110
  46.3 0.0 all-to-all-done
  46.3 1.8 %jacobian.1 = bf16[512,512]{1,0:T(8,128)(2,1)} custom-call(bf16[512,256]{1,0:T(8,128)(2,1)S(1)} %bitcast.43, bf16[1024,512]{1,0:T(8,128)(2,1)S(1)} %transport.1.low_ref.high_ref, bf16[1024,512]{1,0:T(8,128)(2,1)S(1)} %transport.1.low_ref.high_ref), custom_call_target="tpu_custom_call" | custom-call | tf_op jit(solution)/shard_map/jacobian/pallas_call | solution.py:146
  48.2 0.0 copy-start.8
  48.2 9.1 %all-to-all-start.1 = ((bf16[64,8,512]{2,1,0:T(8,128)(2,1)}), bf16[64,8,512]{2,1,0:T(8,128)(2,1)S(1)}, u32[]{:S(2)}, u32[]{:S(2)}) async-start(bf16[64,8,512]{2,1,0:T(8,128)(2,1)} %bitcast.23), calls=%async_computation.1 | async-start | bytes 1048576 | tf_op jit(solution)/shard_map/all_to_all | solution.py:24
  57.3 17.1 %all-to-all-done.1 = bf16[64,8,512]{2,1,0:T(8,128)(2,1)S(1)} async-done(((bf16[64,8,512]{2,1,0:T(8,128)(2,1)}), bf16[64,8,512]{2,1,0:T(8,128)(2,1)S(1)}, u32[]{:S(2)}, u32[]{:S(2)}) %all-to-all-start.1) | async-done | bytes 524320 | tf_op jit(solution)/shard_map/all_to_all | solution.py:24
  74.4 0.3 fusion.3
  74.6 0.3 broadcast_select_fusion
  74.9 1.2 collective-permute-start.3
  76.1 2.8 %collective-permute-start.2 = (bf16[128,512]{1,0:T(8,128)(2,1)S(1)}, bf16[128,512]{1,0:T(8,128)(2,1)S(1)}, u32[]{:S(2)}, u32[]{:S(2)}) collective-permute-start(bf16[128,512]{1,0:T(8,128)(2,1)S(1)} %get-tuple-element.10), channel_id=1, source_target_pairs={{0,0},{1,64},{2,128},{3,192},{32,32},{33,96},{34,160},{35,224},{64... | collective-permute-start | bytes 393224 | tf_op jit(solution)/shard_map/ppermute | solution.py:253
  79.0 0.0 copy-done.8
  79.0 2.2 %collective-permute-done.3.cross_ref = bf16[128,512]{1,0:T(8,128)(2,1)S(1)} collective-permute-done((bf16[128,512]{1,0:T(8,128)(2,1)S(1)}, bf16[128,512]{1,0:T(8,128)(2,1)S(1)}, u32[]{:S(2)}, u32[]{:S(2)}) %collective-permute-start.3) | collective-permute-done | bytes 131104 | tf_op jit(solution)/shard_map/ppermute | solution.py:254
  81.2 3.2 %collective-permute-done.2.same_ref = bf16[128,512]{1,0:T(8,128)(2,1)S(1)} collective-permute-done((bf16[128,512]{1,0:T(8,128)(2,1)S(1)}, bf16[128,512]{1,0:T(8,128)(2,1)S(1)}, u32[]{:S(2)}, u32[]{:S(2)}) %collective-permute-start.2) | collective-permute-done | bytes 131104 | tf_op jit(solution)/shard_map/ppermute | solution.py:253
  84.4 0.1 collective-permute-start.4
  84.5 0.1 multiply_convert_fusion.1
  84.6 2.5 %collective-permute-start.9 = (bf16[128,1024]{1,0:T(8,128)(2,1)S(1)}, bf16[128,1024]{1,0:T(8,128)(2,1)S(1)}, u32[]{:S(2)}, u32[]{:S(2)}) collective-permute-start(bf16[128,1024]{1,0:T(8,128)(2,1)S(1)} %pad_maximum_fusion.2.refs_0_), channel_id=1, source_target_pairs={{0,96},{32,0},{64,32},{96,64},{1,97},{33,1},{65,33},{97,65},{2,98}... | collective-permute-start | bytes 786440 | tf_op jit(solution)/shard_map/ppermute | solution.py:20
  87.1 1.9 %collective-permute-start.8 = (bf16[128,1024]{1,0:T(8,128)(2,1)S(1)}, bf16[128,1024]{1,0:T(8,128)(2,1)S(1)}, u32[]{:S(2)}, u32[]{:S(2)}) collective-permute-start(bf16[128,1024]{1,0:T(8,128)(2,1)S(1)} %pad_maximum_fusion.2.refs_0_), channel_id=1, source_target_pairs={{0,64},{32,96},{64,0},{96,32},{1,65},{33,97},{65,1},{97,33},{2,66}... | collective-permute-start | bytes 786440 | tf_op jit(solution)/shard_map/ppermute | solution.py:20
  89.0 1.7 %collective-permute-start.6 = (bf16[128,1024]{1,0:T(8,128)(2,1)S(1)}, bf16[128,1024]{1,0:T(8,128)(2,1)S(1)}, u32[]{:S(2)}, u32[]{:S(2)}) collective-permute-start(bf16[128,1024]{1,0:T(8,128)(2,1)S(1)} %pad_maximum_fusion.2.refs_0_), channel_id=1, source_target_pairs={{0,128},{128,0},{1,129},{129,1},{2,130},{130,2},{3,131},{131,3},{4... | collective-permute-start | bytes 786440 | tf_op jit(solution)/shard_map/ppermute | solution.py:20
  90.7 1.9 %collective-permute-done.4.across_ref = bf16[256,512]{1,0:T(8,128)(2,1)S(1)} collective-permute-done((bf16[256,512]{1,0:T(8,128)(2,1)S(1)}, bf16[256,512]{1,0:T(8,128)(2,1)S(1)}, u32[]{:S(2)}, u32[]{:S(2)}) %collective-permute-start.4) | collective-permute-done | bytes 262176 | tf_op jit(solution)/shard_map/ppermute | solution.py:20
  92.6 0.8 pad_maximum_fusion
  93.4 3.8 %collective-permute-start.5 = (bf16[512,512]{1,0:T(8,128)(2,1)}, bf16[512,512]{1,0:T(8,128)(2,1)S(1)}, u32[]{:S(2)}, u32[]{:S(2)}) collective-permute-start(bf16[512,512]{1,0:T(8,128)(2,1)} %pad_maximum_fusion), channel_id=1, source_target_pairs={{0,1},{1,0},{2,3},{3,2},{4,5},{5,4},{6,7},{7,6},{8,9},{9,8},{10,11... | collective-permute-start | bytes 1572872 | tf_op jit(solution)/shard_map/ppermute | solution.py:20
  97.2 0.0 collective-permute-start.7
  97.2 0.5 collective-permute-done.6.refs_1_
  97.7 2.8 %collective-permute-start.12 = (bf16[128,1024]{1,0:T(8,128)(2,1)S(1)}, bf16[128,1024]{1,0:T(8,128)(2,1)S(1)}, u32[]{:S(2)}, u32[]{:S(2)}) collective-permute-start(bf16[128,1024]{1,0:T(8,128)(2,1)S(1)} %collective-permute-done.6.refs_1_), channel_id=1, source_target_pairs={{0,96},{32,0},{64,32},{96,64},{1,97},{33,1},{65,33},{97,65},{2,98}... | collective-permute-start | bytes 786440 | tf_op jit(solution)/shard_map/ppermute | solution.py:20
  100.5 0.0 collective-permute-done.9.refs_4_
  100.5 1.1 collective-permute-start.11
  101.6 0.0 collective-permute-done.8.refs_3_
  101.6 1.9 %collective-permute-start.10 = (bf16[128,1024]{1,0:T(8,128)(2,1)S(1)}, bf16[128,1024]{1,0:T(8,128)(2,1)S(1)}, u32[]{:S(2)}, u32[]{:S(2)}) collective-permute-start(bf16[128,1024]{1,0:T(8,128)(2,1)S(1)} %collective-permute-done.6.refs_1_), channel_id=1, source_target_pairs={{0,32},{32,64},{64,96},{96,0},{1,33},{33,65},{65,97},{97,1},{2,34}... | collective-permute-start | bytes 786440 | tf_op jit(solution)/shard_map/ppermute | solution.py:20
  103.5 0.1 stack.67.place_ref
  103.6 9.6 %collective-permute-done.7.refs_2_ = bf16[128,1024]{1,0:T(8,128)(2,1)S(1)} collective-permute-done((bf16[128,1024]{1,0:T(8,128)(2,1)S(1)}, bf16[128,1024]{1,0:T(8,128)(2,1)S(1)}, u32[]{:S(2)}, u32[]{:S(2)}) %collective-permute-start.7) | collective-permute-done | bytes 262176 | tf_op jit(solution)/shard_map/ppermute | solution.py:20
  113.2 0.0 collective-permute-done.12.refs_7_
  113.2 0.0 collective-permute-done.11.refs_6_
  113.2 4.6 %collective-permute-done.10.refs_5_ = bf16[128,1024]{1,0:T(8,128)(2,1)S(1)} collective-permute-done((bf16[128,1024]{1,0:T(8,128)(2,1)S(1)}, bf16[128,1024]{1,0:T(8,128)(2,1)S(1)}, u32[]{:S(2)}, u32[]{:S(2)}) %collective-permute-start.10) | collective-permute-done | bytes 262176 | tf_op jit(solution)/shard_map/ppermute | solution.py:20
  117.9 0.0 collective-permute-done.5.other_ref
  117.9 3.3 %gram.1 = bf16[512,1024]{1,0:T(8,128)(2,1)S(1)} custom-call(s32[16]{0:T(128)S(1)} %stack.67.place_ref, bf16[128,512]{1,0:T(8,128)(2,1)S(1)} %collective-permute-done.2.same_ref, bf16[128,512]{1,0:T(8,128)(2,1)S(1)} %collective-permute-done.3.cross_ref, bf16[256,512]{1,0:T(8,128)(2,1)S(1)} %collective-permute-done.4.across_ref, ...), custom_call_target="tpu_custom_call" | custom-call | tf_op jit(solution)/shard_map/gram/pallas_call | solution.py:187
  121.2 31.0 %all_to_all.15 = bf16[8,64,1024]{2,1,0:T(8,128)(2,1)S(1)} all-to-all(bf16[8,64,1024]{2,1,0:T(8,128)(2,1)S(1)} %bitcast.42), channel_id=1, replica_groups=mesh['xl'=2,'y'=4,'z'=8,'xh'=2,'core'=2] {'z'}, dimensions={0} | all-to-all | bytes 2097152 | tf_op jit(solution)/shard_map/all_to_all | solution.py:24
  152.2 0.9 convert_reduce_fusion
  (5 shorter events, 0.1 us)
Async XLA Ops:
  0.0 13.0 %copy-start.7 = (s32[128,1]{0,1:T(1,128)S(1)}, s32[128,1]{0,1:T(1,128)}, u32[]{:S(2)}) copy-start(s32[128,1]{0,1:T(1,128)} %param.9) | copy-start | bytes 1540
  0.0 1.6 %copy-start = (f32[1024,4,128]{2,1,0:T(4,128)S(1)}, f32[1024,4,128]{2,1,0:T(4,128)}, u32[]{:S(2)}) copy-start(f32[1024,4,128]{2,1,0:T(4,128)} %param.6) | copy-start | bytes 6291460
  1.6 0.7 copy-start.2
  2.3 0.7 copy-start.4
  3.0 10.2 %copy-start.6 = (bf16[128,512]{1,0:T(8,128)(2,1)S(1)}, bf16[128,512]{1,0:T(8,128)(2,1)}, u32[]{:S(2)}) copy-start(bf16[128,512]{1,0:T(8,128)(2,1)} %param.10) | copy-start | bytes 393220
  3.0 31.5 %copy-start.3 = (f32[4,128]{1,0:T(4,128)S(1)}, f32[4,128]{1,0:T(4,128)}, u32[]{:S(2)}) copy-start(f32[4,128]{1,0:T(4,128)} %wind_x_ref.3) | copy-start | bytes 6148
  3.0 31.5 %copy-start.5 = (f32[4,128]{1,0:T(4,128)S(1)}, f32[4,128]{1,0:T(4,128)}, u32[]{:S(2)}) copy-start(f32[4,128]{1,0:T(4,128)} %wind_y_ref.3) | copy-start | bytes 6148
  4.1 28.5 %collective-permute-start = (bf16[3088,128]{1,0:T(8,128)(2,1)}, bf16[3088,128]{1,0:T(8,128)(2,1)S(1)}, u32[]{:S(2)}, u32[]{:S(2)}) collective-permute-start(bf16[3088,128]{1,0:T(8,128)(2,1)} %get-tuple-element.7), channel_id=1, source_target_pairs={{0,4},{4,8},{8,12},{12,16},{16,20},{20,24},{24,28},{28,32},{32,36}... | collective-permute-start | bytes 2371592 | tf_op jit(solution)/shard_map/ppermute | solution.py:20
  6.0 28.5 %collective-permute-start.1 = (bf16[3088,128]{1,0:T(8,128)(2,1)S(1)}, bf16[3088,128]{1,0:T(8,128)(2,1)S(1)}, u32[]{:S(2)}, u32[]{:S(2)}) collective-permute-start(bf16[3088,128]{1,0:T(8,128)(2,1)S(1)} %get-tuple-element.8), channel_id=1, source_target_pairs={{0,252},{4,0},{8,4},{12,8},{16,12},{20,16},{24,20},{28,24},{32,28}... | collective-permute-start | bytes 2371592 | tf_op jit(solution)/shard_map/ppermute | solution.py:20
  14.6 31.7 %all-to-all-start = ((bf16[64,8,256]{2,1,0:T(8,128)(2,1)}), bf16[64,8,256]{2,1,0:T(8,128)(2,1)S(1)}, u32[]{:S(2)}, u32[]{:S(2)}) async-start(bf16[64,8,256]{2,1,0:T(8,128)(2,1)} %fusion), calls=%async_computation | async-start | bytes 524288 | tf_op jit(solution)/shard_map/all_to_all | solution.py:24
  34.5 1.6 %copy-start.1 = (f32[1024,4,128]{2,1,0:T(4,128)S(1)}, f32[1024,4,128]{2,1,0:T(4,128)}, u32[]{:S(2)}) copy-start(f32[1024,4,128]{2,1,0:T(4,128)} %param.6) | copy-start | bytes 6291460
  48.2 30.8 %copy-start.8 = (bf16[128]{0:T(256)(128)(2,1)S(1)}, bf16[128]{0:T(256)(128)(2,1)}, u32[]{:S(2)}) copy-start(bf16[128]{0:T(256)(128)(2,1)} %param.11) | copy-start | bytes 772
  48.2 26.2 %all-to-all-start.1 = ((bf16[64,8,512]{2,1,0:T(8,128)(2,1)}), bf16[64,8,512]{2,1,0:T(8,128)(2,1)S(1)}, u32[]{:S(2)}, u32[]{:S(2)}) async-start(bf16[64,8,512]{2,1,0:T(8,128)(2,1)} %bitcast.23), calls=%async_computation.1 | async-start | bytes 1048576 | tf_op jit(solution)/shard_map/all_to_all | solution.py:24
  74.9 6.3 %collective-permute-start.3 = (bf16[128,512]{1,0:T(8,128)(2,1)S(1)}, bf16[128,512]{1,0:T(8,128)(2,1)S(1)}, u32[]{:S(2)}, u32[]{:S(2)}) collective-permute-start(bf16[128,512]{1,0:T(8,128)(2,1)S(1)} %get-tuple-element.9), channel_id=1, source_target_pairs={{0,32},{1,96},{2,160},{3,224},{32,0},{33,64},{34,128},{35,192},{64... | collective-permute-start | bytes 393224 | tf_op jit(solution)/shard_map/ppermute | solution.py:254
  76.1 8.2 %collective-permute-start.2 = (bf16[128,512]{1,0:T(8,128)(2,1)S(1)}, bf16[128,512]{1,0:T(8,128)(2,1)S(1)}, u32[]{:S(2)}, u32[]{:S(2)}) collective-permute-start(bf16[128,512]{1,0:T(8,128)(2,1)S(1)} %get-tuple-element.10), channel_id=1, source_target_pairs={{0,0},{1,64},{2,128},{3,192},{32,32},{33,96},{34,160},{35,224},{64... | collective-permute-start | bytes 393224 | tf_op jit(solution)/shard_map/ppermute | solution.py:253
  84.4 8.2 %collective-permute-start.4 = (bf16[256,512]{1,0:T(8,128)(2,1)S(1)}, bf16[256,512]{1,0:T(8,128)(2,1)S(1)}, u32[]{:S(2)}, u32[]{:S(2)}) collective-permute-start(bf16[256,512]{1,0:T(8,128)(2,1)S(1)} %pad_maximum_fusion.1), channel_id=1, source_target_pairs={{0,2},{2,0},{1,3},{3,1},{4,6},{6,4},{5,7},{7,5},{8,10},{10,8},{9,1... | collective-permute-start | bytes 786440 | tf_op jit(solution)/shard_map/ppermute | solution.py:20
  84.6 15.8 %collective-permute-start.9 = (bf16[128,1024]{1,0:T(8,128)(2,1)S(1)}, bf16[128,1024]{1,0:T(8,128)(2,1)S(1)}, u32[]{:S(2)}, u32[]{:S(2)}) collective-permute-start(bf16[128,1024]{1,0:T(8,128)(2,1)S(1)} %pad_maximum_fusion.2.refs_0_), channel_id=1, source_target_pairs={{0,96},{32,0},{64,32},{96,64},{1,97},{33,1},{65,33},{97,65},{2,98}... | collective-permute-start | bytes 786440 | tf_op jit(solution)/shard_map/ppermute | solution.py:20
  87.1 14.5 %collective-permute-start.8 = (bf16[128,1024]{1,0:T(8,128)(2,1)S(1)}, bf16[128,1024]{1,0:T(8,128)(2,1)S(1)}, u32[]{:S(2)}, u32[]{:S(2)}) collective-permute-start(bf16[128,1024]{1,0:T(8,128)(2,1)S(1)} %pad_maximum_fusion.2.refs_0_), channel_id=1, source_target_pairs={{0,64},{32,96},{64,0},{96,32},{1,65},{33,97},{65,1},{97,33},{2,66}... | collective-permute-start | bytes 786440 | tf_op jit(solution)/shard_map/ppermute | solution.py:20
  89.0 8.7 %collective-permute-start.6 = (bf16[128,1024]{1,0:T(8,128)(2,1)S(1)}, bf16[128,1024]{1,0:T(8,128)(2,1)S(1)}, u32[]{:S(2)}, u32[]{:S(2)}) collective-permute-start(bf16[128,1024]{1,0:T(8,128)(2,1)S(1)} %pad_maximum_fusion.2.refs_0_), channel_id=1, source_target_pairs={{0,128},{128,0},{1,129},{129,1},{2,130},{130,2},{3,131},{131,3},{4... | collective-permute-start | bytes 786440 | tf_op jit(solution)/shard_map/ppermute | solution.py:20
  93.4 24.5 %collective-permute-start.5 = (bf16[512,512]{1,0:T(8,128)(2,1)}, bf16[512,512]{1,0:T(8,128)(2,1)S(1)}, u32[]{:S(2)}, u32[]{:S(2)}) collective-permute-start(bf16[512,512]{1,0:T(8,128)(2,1)} %pad_maximum_fusion), channel_id=1, source_target_pairs={{0,1},{1,0},{2,3},{3,2},{4,5},{5,4},{6,7},{7,6},{8,9},{9,8},{10,11... | collective-permute-start | bytes 1572872 | tf_op jit(solution)/shard_map/ppermute | solution.py:20
  97.2 16.0 %collective-permute-start.7 = (bf16[128,1024]{1,0:T(8,128)(2,1)S(1)}, bf16[128,1024]{1,0:T(8,128)(2,1)S(1)}, u32[]{:S(2)}, u32[]{:S(2)}) collective-permute-start(bf16[128,1024]{1,0:T(8,128)(2,1)S(1)} %pad_maximum_fusion.2.refs_0_), channel_id=1, source_target_pairs={{0,32},{32,64},{64,96},{96,0},{1,33},{33,65},{65,97},{97,1},{2,34}... | collective-permute-start | bytes 786440 | tf_op jit(solution)/shard_map/ppermute | solution.py:20
  97.7 15.5 %collective-permute-start.12 = (bf16[128,1024]{1,0:T(8,128)(2,1)S(1)}, bf16[128,1024]{1,0:T(8,128)(2,1)S(1)}, u32[]{:S(2)}, u32[]{:S(2)}) collective-permute-start(bf16[128,1024]{1,0:T(8,128)(2,1)S(1)} %collective-permute-done.6.refs_1_), channel_id=1, source_target_pairs={{0,96},{32,0},{64,32},{96,64},{1,97},{33,1},{65,33},{97,65},{2,98}... | collective-permute-start | bytes 786440 | tf_op jit(solution)/shard_map/ppermute | solution.py:20
  100.5 12.8 %collective-permute-start.11 = (bf16[128,1024]{1,0:T(8,128)(2,1)S(1)}, bf16[128,1024]{1,0:T(8,128)(2,1)S(1)}, u32[]{:S(2)}, u32[]{:S(2)}) collective-permute-start(bf16[128,1024]{1,0:T(8,128)(2,1)S(1)} %collective-permute-done.6.refs_1_), channel_id=1, source_target_pairs={{0,64},{32,96},{64,0},{96,32},{1,65},{33,97},{65,1},{97,33},{2,66}... | collective-permute-start | bytes 786440 | tf_op jit(solution)/shard_map/ppermute | solution.py:20
  101.6 16.3 %collective-permute-start.10 = (bf16[128,1024]{1,0:T(8,128)(2,1)S(1)}, bf16[128,1024]{1,0:T(8,128)(2,1)S(1)}, u32[]{:S(2)}, u32[]{:S(2)}) collective-permute-start(bf16[128,1024]{1,0:T(8,128)(2,1)S(1)} %collective-permute-done.6.refs_1_), channel_id=1, source_target_pairs={{0,32},{32,64},{64,96},{96,0},{1,33},{33,65},{65,97},{97,1},{2,34}... | collective-permute-start | bytes 786440 | tf_op jit(solution)/shard_map/ppermute | solution.py:20
where the time goes:
time: 156 us; the launch traced here: 153 us
  waiting for transfers between devices  51.8 us (33%)
  starting transfers between devices  44.9 us (29%)
  blocking collectives  31 us (20%)
  Pallas kernels  16.4 us (11%)
  local copies, waits for them, and re-layouts  4.68 us (3%)
  other arithmetic  2.36 us (2%)
  matrix products  1.61 us (1%)
    all_to_all x1, blocking collectives, exchanged(): return lax.all_to_all(value, axis, split_axis=0, concat_axis=0, tiled=True)  31 us
    ppermute x11, waiting for transfers between devices, shifted(): lax.ppermute(value, axis, [(i, (i + steps) % count) for i in range(count)])  29.4 us
    ppermute x11, starting transfers between devices, shifted(): lax.ppermute(value, axis, [(i, (i + steps) % count) for i in range(count)])  24.7 us
    all_to_all x2, waiting for transfers between devices, exchanged(): return lax.all_to_all(value, axis, split_axis=0, concat_axis=0, tiled=True)  17.1 us
    all_to_all x2, starting transfers between devices, exchanged(): return lax.all_to_all(value, axis, split_axis=0, concat_axis=0, tiled=True)  16.1 us
    pallas_call x1, Pallas kernels, transport(): pl.pallas_call(transport_body, grid=(steps,), in_specs=[pl.BlockSpec((4 *...  10.3 us
    unnamed x18, local copies, waits for them, and re-layouts  4.58 us
    pallas_call x1, Pallas kernels, gram_tile(): pl.pallas_call(gram_body, grid=(tracers // block,), in_specs=[pl.BlockSpe...  3.28 us
  transfers between devices with their start and end apart: 15, of which 9 were waited for; matrix products, arithmetic and copies ran while one was open for 2% of the time, Pallas kernels for 7%

commit v1 on v0

--- a/solution.py
+++ b/solution.py
@@ -24,37 +24,40 @@
     return lax.all_to_all(value, axis, split_axis=0, concat_axis=0, tiled=True)
 
 
-def edge_rows(pulse_ref, wind_x_ref, wind_y_ref, first_ref, last_ref):
-    count = pulse_ref.shape[0] // 4
-    rows = [pulse_ref[pl.ds(r, count, 4), :].astype(jnp.bfloat16) for r in range(4)]
-    for r in range(STEPS):
-        first_ref[r * count : (r + 1) * count] = rows[r]
-        last_ref[r * count : (r + 1) * count] = rows[r + 1]
+def edge_rows(pulse_ref, wind_x_ref, wind_y_ref, *out_refs):
+    tracers = pulse_ref.shape[0] // 4
+    rows = [pulse_ref[pl.ds(r, tracers, 4), :].astype(jnp.bfloat16) for r in range(4)]
     winds = jnp.concatenate([wind_x_ref[...], wind_y_ref[...]], axis=0)
-    coarse = winds.astype(jnp.bfloat16)
-    fine = (winds - coarse.astype(jnp.float32)).astype(jnp.bfloat16)
-    both = jnp.concatenate([coarse.astype(jnp.float32), fine.astype(jnp.float32)], axis=0)
-    first_ref[STEPS * count :] = both.astype(jnp.bfloat16)
-    last_ref[STEPS * count :] = both.astype(jnp.bfloat16)
+    coarse = winds.astype(jnp.bfloat16).astype(jnp.float32)
+    both = jnp.concatenate([coarse, winds - coarse], axis=0).astype(jnp.bfloat16)
+    for k, (start, size) in enumerate(spans(tracers)):
+        for edge in range(2):
+            ref = out_refs[2 * k + edge]
+            for r in range(STEPS):
+                ref[r * size : (r + 1) * size] = rows[r + edge][start : start + size]
+            ref[STEPS * size :] = both
+
+
+def spans(tracers):
+    cut = tracers * 5 // 8
+    return [(0, cut), (cut, tracers - cut)]
 
 
 def edges(pulses, wind_x, wind_y):
     tracers = pulses.shape[0] // 4
-    shape = jax.ShapeDtypeStruct((STEPS * tracers + 16, 128), jnp.bfloat16)
-    return pl.pallas_call(
-        edge_rows,
-        out_shape=[shape, shape],
-        compiler_params=pltpu.CompilerParams(vmem_limit_bytes=GRANT),
-        name="edges",
-    )(pulses, wind_x, wind_y)
+    shapes = []
+    for start, size in spans(tracers):
+        shapes += [jax.ShapeDtypeStruct((STEPS * size + 16, 128), jnp.bfloat16)] * 2
+    return pl.pallas_call(edge_rows, out_shape=shapes, name="edges")(pulses, wind_x, wind_y)
 
 
 PIECE = 16
 
 
 def transport_body(
-    pulse_ref, a0, a1, a2, a_winds, b0, b1, b2, b_winds, wind_x_ref, wind_y_ref, out_ref, coef_ref
+    pulse_ref, a0, a1, a2, b0, b1, b2, a_winds, b_winds, wind_x_ref, wind_y_ref, *refs
 ):
+    out_ref, coef_ref = refs[-2:]
     count = out_ref.shape[0]
 
     @pl.when(pl.program_id(0) == 0)
@@ -100,23 +103,34 @@
             out_ref[at : at + PIECE, r * 128 : (r + 1) * 128] = field[r].astype(jnp.bfloat16)
 
 
-def transport(pulses, above, below, wind_x, wind_y, block=256):
+def transport(pulses, above, below, wind_x, wind_y, span, into=None, block=128):
     tracers = pulses.shape[0] // 4
-    steps = tracers // block
+    start, size = span
+    skip, steps = start // block, size // block
     halo = [
         pl.BlockSpec((block, 128), lambda i, r=r: (r * steps + i, 0)) for r in range(STEPS)
-    ] + [pl.BlockSpec((16, 128), lambda i: (STEPS * tracers // 16, 0))]
+    ]
+    last = [pl.BlockSpec((16, 128), lambda i: (STEPS * size // 16, 0))] * 2
     wind = pl.BlockSpec((4, 128), lambda i: (0, 0))
+    operands = [pulses, *[above] * 3, *[below] * 3, above, below, wind_x, wind_y]
+    specs = [pl.BlockSpec((4 * block, 128), lambda i: (skip + i, 0))] + halo + halo + last
+    specs += [wind, wind]
+    aliases = {}
+    if into is not None:
+        aliases = {len(operands): 0}
+        operands.append(into)
+        specs.append(pl.BlockSpec(memory_space=pl.ANY))
     return pl.pallas_call(
         transport_body,
         grid=(steps,),
-        in_specs=[pl.BlockSpec((4 * block, 128), lambda i: (i, 0))] + halo + halo + [wind, wind],
-        out_specs=pl.BlockSpec((block, 512), lambda i: (i, 0)),
+        in_specs=specs,
+        out_specs=pl.BlockSpec((block, 512), lambda i: (skip + i, 0)),
         out_shape=jax.ShapeDtypeStruct((tracers, 512), jnp.bfloat16),
         scratch_shapes=[pltpu.VMEM((40, PIECE, 128), jnp.float32)],
+        input_output_aliases=aliases,
         compiler_params=pltpu.CompilerParams(vmem_limit_bytes=GRANT),
         name="transport",
-    )(pulses, *[above] * 4, *[below] * 4, wind_x, wind_y)
+    )(*operands)
 
 
 def jacobian_body(rows_ref, low_ref, high_ref, out_ref, full_ref):
@@ -208,10 +222,13 @@
     half = tracers // 2
     pulses = pulses.reshape(tracers * 4, 128)
 
-    first, last = edges(pulses, wind_x, wind_y)
-    above = shifted(last, CELLS, 1)
-    below = shifted(first, CELLS, -1)
-    sampled = transport(pulses, above, below, wind_x, wind_y)
+    messages = edges(pulses, wind_x, wind_y)
+    halos = []
+    for k in range(2):
+        halos.append((shifted(messages[2 * k + 1], CELLS, 1), shifted(messages[2 * k], CELLS, -1)))
+    sampled = None
+    for span, (above, below) in zip(spans(tracers), halos):
+        sampled = transport(pulses, above, below, wind_x, wind_y, span, sampled)
 
     tile = obs_tile[:, 0]
     order = jnp.arange(obs)

time: 156 us -> 157 us (level)
  starting transfers between devices: 44.9 us -> 53.4 us
  waiting for transfers between devices: 51.8 us -> 45.9 us
  local copies, waits for them, and re-layouts: 4.68 us -> 0.12 us
  other arithmetic: 2.36 us -> 5.64 us
    ppermute x11 -> x13, waiting for transfers between devices: 29.4 us -> 24.2 us  [shifted(): lax.ppermute(value, axis, [(i, (i + steps) % count) for i in range(count)])]
    unnamed x18 -> x8, local copies, waits for them, and re-layouts: 4.58 us -> 0.01 us
    all_to_all x2, starting transfers between devices: 16.1 us -> 20.5 us  [exchanged(): return lax.all_to_all(value, axis, split_axis=0, concat_axis=0, tiled=True)]
    ppermute x11 -> x13, starting transfers between devices: 24.7 us -> 28.8 us  [shifted(): lax.ppermute(value, axis, [(i, (i + steps) % count) for i in range(count)])]
    pallas_call x2 -> x3, Pallas kernels: 11.3 us -> 12.5 us  [the longest x2 9.6 us: transport(): pl.pallas_call(transport_body, grid=(steps,), in_specs=specs, out_specs=p...]
  transfers between devices with their start and end apart: 15 -> 17, of which waited for: 9 -> 7; matrix products, arithmetic and copies ran while one was open for 2% -> 1% of each run, Pallas kernels for 7% -> 8%
where the time goes in v1:
time: 157 us; the launch traced here: 155 us
  starting transfers between devices  53.4 us (34%)
  waiting for transfers between devices  45.9 us (29%)
  blocking collectives  30.7 us (20%)
  Pallas kernels  17.5 us (11%)
  other arithmetic  5.64 us (4%)
  matrix products  1.61 us (1%)
    all_to_all x1, blocking collectives, exchanged(): return lax.all_to_all(value, axis, split_axis=0, concat_axis=0, tiled=True)  30.7 us
    ppermute x13, starting transfers between devices, shifted(): lax.ppermute(value, axis, [(i, (i + steps) % count) for i in range(count)])  28.8 us
    ppermute x13, waiting for transfers between devices, shifted(): lax.ppermute(value, axis, [(i, (i + steps) % count) for i in range(count)])  24.2 us
    all_to_all x2, starting transfers between devices, exchanged(): return lax.all_to_all(value, axis, split_axis=0, concat_axis=0, tiled=True)  20.5 us
    all_to_all x2, waiting for transfers between devices, exchanged(): return lax.all_to_all(value, axis, split_axis=0, concat_axis=0, tiled=True)  16.3 us
    pallas_call x2, Pallas kernels, transport(): pl.pallas_call(transport_body, grid=(steps,), in_specs=specs, out_specs=p...  9.6 us
    pallas_call x1, Pallas kernels, gram_tile(): pl.pallas_call(gram_body, grid=(tracers // block,), in_specs=[pl.BlockSpe...  3.28 us
    ppermute x1, waiting for transfers between devices, on_device(): same = lax.ppermute(jnp.where(odd == 0, low, high), PLANE, to_same)  3.16 us
  transfers between devices with their start and end apart: 17, of which 7 were waited for; matrix products, arithmetic and copies ran while one was open for 1% of the time, Pallas kernels for 8%

profile of v1, /device:TPU:4, one launch (start us, length us, event | category | flops | bytes accessed | tf_op | source)
XLA Modules:
  0.0 155.1 jit_solution(11883250029448303346)
XLA Ops:
  0.0 0.0 copy-start.2
  0.0 0.0 copy-start.1
  0.0 0.0 copy-start
  0.0 1.0 convert_reduce_fusion.2
  1.0 1.0 convert_reduce_fusion.1
  2.0 0.7 fusion.15
  2.7 1.0 fusion.8
  3.7 0.1 iota_compare_fusion
  3.9 1.1 fusion
  4.9 12.7 %all-to-all-start = ((bf16[64,8,256]{2,1,0:T(8,128)(2,1)}), bf16[64,8,256]{2,1,0:T(8,128)(2,1)S(1)}, u32[]{:S(2)}, u32[]{:S(2)}) async-start(bf16[64,8,256]{2,1,0:T(8,128)(2,1)} %fusion), calls=%async_computation | async-start | bytes 524288 | tf_op jit(solution)/shard_map/all_to_all | solution.py:24
  17.7 2.9 %edges.1 = (bf16[1936,128]{1,0:T(8,128)(2,1)}, bf16[1936,128]{1,0:T(8,128)(2,1)}, bf16[1168,128]{1,0:T(8,128)(2,1)}, bf16[1168,128]{1,0:T(8,128)(2,1)}) custom-call(f32[4096,128]{1,0:T(8,128)} %bitcast.40, f32[4,128]{1,0:T(4,128)} %wind_x_ref.5, f32[4,128]{1,0:T(4,128)} %wind_y_ref.5), custom_call_target="tpu_custom_call" | custom-call | tf_op jit(solution)/shard_map/edges/pallas_call | solution.py:51
  20.5 1.6 %collective-permute-start.2 = (bf16[1936,128]{1,0:T(8,128)(2,1)}, bf16[1936,128]{1,0:T(8,128)(2,1)S(1)}, u32[]{:S(2)}, u32[]{:S(2)}) collective-permute-start(bf16[1936,128]{1,0:T(8,128)(2,1)} %get-tuple-element.11), channel_id=1, source_target_pairs={{0,4},{4,8},{8,12},{12,16},{16,20},{20,24},{24,28},{28,32},{32,36}... | collective-permute-start | bytes 1486856 | tf_op jit(solution)/shard_map/ppermute | solution.py:20
  22.1 4.7 %collective-permute-start.3 = (bf16[1936,128]{1,0:T(8,128)(2,1)}, bf16[1936,128]{1,0:T(8,128)(2,1)S(1)}, u32[]{:S(2)}, u32[]{:S(2)}) collective-permute-start(bf16[1936,128]{1,0:T(8,128)(2,1)} %get-tuple-element.12), channel_id=1, source_target_pairs={{0,252},{4,0},{8,4},{12,8},{16,12},{20,16},{24,20},{28,24},{32,28}... | collective-permute-start | bytes 1486856 | tf_op jit(solution)/shard_map/ppermute | solution.py:20
  26.8 0.0 collective-permute-start
  26.8 6.2 %collective-permute-start.1 = (bf16[1168,128]{1,0:T(8,128)(2,1)}, bf16[1168,128]{1,0:T(8,128)(2,1)S(1)}, u32[]{:S(2)}, u32[]{:S(2)}) collective-permute-start(bf16[1168,128]{1,0:T(8,128)(2,1)} %get-tuple-element.10), channel_id=1, source_target_pairs={{0,252},{4,0},{8,4},{12,8},{16,12},{20,16},{24,20},{28,24},{32,28}... | collective-permute-start | bytes 897032 | tf_op jit(solution)/shard_map/ppermute | solution.py:20
  33.0 7.3 %collective-permute-done.2.a0.a1.a2.a_winds = bf16[1936,128]{1,0:T(8,128)(2,1)S(1)} collective-permute-done((bf16[1936,128]{1,0:T(8,128)(2,1)}, bf16[1936,128]{1,0:T(8,128)(2,1)S(1)}, u32[]{:S(2)}, u32[]{:S(2)}) %collective-permute-start.2) | collective-permute-done | bytes 495648 | tf_op jit(solution)/shard_map/ppermute | solution.py:20
  40.3 0.0 collective-permute-done.3.b0.b1.b2.b_winds
  40.3 0.0 copy-done.2
  40.3 0.0 copy-done.1
  40.3 0.0 copy-done
  40.3 6.0 %transport.2.refs_0_ = bf16[1024,512]{1,0:T(8,128)(2,1)S(1)} custom-call(f32[4096,128]{1,0:T(8,128)S(1)} %bitcast.41, bf16[1936,128]{1,0:T(8,128)(2,1)S(1)} %collective-permute-done.2.a0.a1.a2.a_winds, bf16[1936,128]{1,0:T(8,128)(2,1)S(1)} %collective-permute-done.2.a0.a1.a2.a_winds, bf16[1936,128]{1,0:T(8,128)(2,1)S(1)} %collective-permute-done.2.a0.a1.a2.a_winds, ...), custom_call_target="tpu_custom_call" | custom-call | tf_op jit(solution)/shard_map/transport/pallas_call | solution.py:123
  46.3 0.0 collective-permute-done.a0.a1.a2.a_winds
  46.4 0.0 collective-permute-done.1.b0.b1.b2.b_winds
  46.4 3.6 %transport.3.low_ref.high_ref = bf16[1024,512]{1,0:T(8,128)(2,1)S(1)} custom-call(f32[4096,128]{1,0:T(8,128)S(1)} %bitcast.42, bf16[1168,128]{1,0:T(8,128)(2,1)S(1)} %collective-permute-done.a0.a1.a2.a_winds, bf16[1168,128]{1,0:T(8,128)(2,1)S(1)} %collective-permute-done.a0.a1.a2.a_winds, ...), custom_call_target="tpu_custom_call", output_to_operand_aliasing={{}: (11, {})} | custom-call | tf_op jit(solution)/shard_map/transport/pallas_call | solution.py:123
  50.0 0.0 all-to-all-done
  50.0 1.8 %jacobian.1 = bf16[512,512]{1,0:T(8,128)(2,1)} custom-call(bf16[512,256]{1,0:T(8,128)(2,1)S(1)} %bitcast.44, bf16[1024,512]{1,0:T(8,128)(2,1)S(1)} %transport.3.low_ref.high_ref, bf16[1024,512]{1,0:T(8,128)(2,1)S(1)} %transport.3.low_ref.high_ref), custom_call_target="tpu_custom_call" | custom-call | tf_op jit(solution)/shard_map/jacobian/pallas_call | solution.py:160
  51.8 0.0 copy-start.3
  51.8 7.8 %all-to-all-start.1 = ((bf16[64,8,512]{2,1,0:T(8,128)(2,1)}), bf16[64,8,512]{2,1,0:T(8,128)(2,1)S(1)}, u32[]{:S(2)}, u32[]{:S(2)}) async-start(bf16[64,8,512]{2,1,0:T(8,128)(2,1)} %bitcast.23), calls=%async_computation.1 | async-start | bytes 1048576 | tf_op jit(solution)/shard_map/all_to_all | solution.py:24
  59.6 16.3 %all-to-all-done.1 = bf16[64,8,512]{2,1,0:T(8,128)(2,1)S(1)} async-done(((bf16[64,8,512]{2,1,0:T(8,128)(2,1)}), bf16[64,8,512]{2,1,0:T(8,128)(2,1)S(1)}, u32[]{:S(2)}, u32[]{:S(2)}) %all-to-all-start.1) | async-done | bytes 524320 | tf_op jit(solution)/shard_map/all_to_all | solution.py:24
  76.0 0.3 fusion.3
  76.2 0.3 broadcast_select_fusion
  76.5 1.2 collective-permute-start.5
  77.7 2.9 %collective-permute-start.4 = (bf16[128,512]{1,0:T(8,128)(2,1)S(1)}, bf16[128,512]{1,0:T(8,128)(2,1)S(1)}, u32[]{:S(2)}, u32[]{:S(2)}) collective-permute-start(bf16[128,512]{1,0:T(8,128)(2,1)S(1)} %get-tuple-element.14), channel_id=1, source_target_pairs={{0,0},{1,64},{2,128},{3,192},{32,32},{33,96},{34,160},{35,224},{64... | collective-permute-start | bytes 393224 | tf_op jit(solution)/shard_map/ppermute | solution.py:270
  80.6 0.0 copy-done.3
  80.6 2.2 %collective-permute-done.5.cross_ref = bf16[128,512]{1,0:T(8,128)(2,1)S(1)} collective-permute-done((bf16[128,512]{1,0:T(8,128)(2,1)S(1)}, bf16[128,512]{1,0:T(8,128)(2,1)S(1)}, u32[]{:S(2)}, u32[]{:S(2)}) %collective-permute-start.5) | collective-permute-done | bytes 131104 | tf_op jit(solution)/shard_map/ppermute | solution.py:271
  82.8 3.2 %collective-permute-done.4.same_ref = bf16[128,512]{1,0:T(8,128)(2,1)S(1)} collective-permute-done((bf16[128,512]{1,0:T(8,128)(2,1)S(1)}, bf16[128,512]{1,0:T(8,128)(2,1)S(1)}, u32[]{:S(2)}, u32[]{:S(2)}) %collective-permute-start.4) | collective-permute-done | bytes 131104 | tf_op jit(solution)/shard_map/ppermute | solution.py:270
  86.0 0.1 collective-permute-start.6
  86.1 0.1 multiply_convert_fusion.1
  86.2 2.5 %collective-permute-start.11 = (bf16[128,1024]{1,0:T(8,128)(2,1)S(1)}, bf16[128,1024]{1,0:T(8,128)(2,1)S(1)}, u32[]{:S(2)}, u32[]{:S(2)}) collective-permute-start(bf16[128,1024]{1,0:T(8,128)(2,1)S(1)} %pad_maximum_fusion.2.refs_0_), channel_id=1, source_target_pairs={{0,96},{32,0},{64,32},{96,64},{1,97},{33,1},{65,33},{97,65},{2,98}... | collective-permute-start | bytes 786440 | tf_op jit(solution)/shard_map/ppermute | solution.py:20
  88.8 1.1 collective-permute-start.10
  89.9 2.3 %collective-permute-start.8 = (bf16[128,1024]{1,0:T(8,128)(2,1)S(1)}, bf16[128,1024]{1,0:T(8,128)(2,1)S(1)}, u32[]{:S(2)}, u32[]{:S(2)}) collective-permute-start(bf16[128,1024]{1,0:T(8,128)(2,1)S(1)} %pad_maximum_fusion.2.refs_0_), channel_id=1, source_target_pairs={{0,128},{128,0},{1,129},{129,1},{2,130},{130,2},{3,131},{131,3},{4... | collective-permute-start | bytes 786440 | tf_op jit(solution)/shard_map/ppermute | solution.py:20
  92.2 2.1 %collective-permute-done.6.across_ref = bf16[256,512]{1,0:T(8,128)(2,1)S(1)} collective-permute-done((bf16[256,512]{1,0:T(8,128)(2,1)S(1)}, bf16[256,512]{1,0:T(8,128)(2,1)S(1)}, u32[]{:S(2)}, u32[]{:S(2)}) %collective-permute-start.6) | collective-permute-done | bytes 262176 | tf_op jit(solution)/shard_map/ppermute | solution.py:20
  94.3 0.8 pad_maximum_fusion
  95.1 4.4 %collective-permute-start.7 = (bf16[512,512]{1,0:T(8,128)(2,1)}, bf16[512,512]{1,0:T(8,128)(2,1)S(1)}, u32[]{:S(2)}, u32[]{:S(2)}) collective-permute-start(bf16[512,512]{1,0:T(8,128)(2,1)} %pad_maximum_fusion), channel_id=1, source_target_pairs={{0,1},{1,0},{2,3},{3,2},{4,5},{5,4},{6,7},{7,6},{8,9},{9,8},{10,11... | collective-permute-start | bytes 1572872 | tf_op jit(solution)/shard_map/ppermute | solution.py:20
  99.5 0.0 collective-permute-start.9
  99.6 0.0 collective-permute-done.8.refs_1_
  99.6 3.2 %collective-permute-start.14 = (bf16[128,1024]{1,0:T(8,128)(2,1)S(1)}, bf16[128,1024]{1,0:T(8,128)(2,1)S(1)}, u32[]{:S(2)}, u32[]{:S(2)}) collective-permute-start(bf16[128,1024]{1,0:T(8,128)(2,1)S(1)} %collective-permute-done.8.refs_1_), channel_id=1, source_target_pairs={{0,96},{32,0},{64,32},{96,64},{1,97},{33,1},{65,33},{97,65},{2,98}... | collective-permute-start | bytes 786440 | tf_op jit(solution)/shard_map/ppermute | solution.py:20
  102.8 0.0 collective-permute-done.11.refs_4_
  102.8 0.0 collective-permute-start.13
  102.8 0.0 collective-permute-done.10.refs_3_
  102.8 2.5 %collective-permute-start.12 = (bf16[128,1024]{1,0:T(8,128)(2,1)S(1)}, bf16[128,1024]{1,0:T(8,128)(2,1)S(1)}, u32[]{:S(2)}, u32[]{:S(2)}) collective-permute-start(bf16[128,1024]{1,0:T(8,128)(2,1)S(1)} %collective-permute-done.8.refs_1_), channel_id=1, source_target_pairs={{0,32},{32,64},{64,96},{96,0},{1,33},{33,65},{65,97},{97,1},{2,34}... | collective-permute-start | bytes 786440 | tf_op jit(solution)/shard_map/ppermute | solution.py:20
  105.3 0.1 stack.67.place_ref
  105.4 10.1 %collective-permute-done.9.refs_2_ = bf16[128,1024]{1,0:T(8,128)(2,1)S(1)} collective-permute-done((bf16[128,1024]{1,0:T(8,128)(2,1)S(1)}, bf16[128,1024]{1,0:T(8,128)(2,1)S(1)}, u32[]{:S(2)}, u32[]{:S(2)}) %collective-permute-start.9) | collective-permute-done | bytes 262176 | tf_op jit(solution)/shard_map/ppermute | solution.py:20
  115.6 0.0 collective-permute-done.14.refs_7_
  115.6 0.0 collective-permute-done.13.refs_6_
  115.6 4.6 %collective-permute-done.12.refs_5_ = bf16[128,1024]{1,0:T(8,128)(2,1)S(1)} collective-permute-done((bf16[128,1024]{1,0:T(8,128)(2,1)S(1)}, bf16[128,1024]{1,0:T(8,128)(2,1)S(1)}, u32[]{:S(2)}, u32[]{:S(2)}) %collective-permute-start.12) | collective-permute-done | bytes 262176 | tf_op jit(solution)/shard_map/ppermute | solution.py:20
  120.2 0.0 collective-permute-done.7.other_ref
  120.2 3.3 %gram.1 = bf16[512,1024]{1,0:T(8,128)(2,1)S(1)} custom-call(s32[16]{0:T(128)S(1)} %stack.67.place_ref, bf16[128,512]{1,0:T(8,128)(2,1)S(1)} %collective-permute-done.4.same_ref, bf16[128,512]{1,0:T(8,128)(2,1)S(1)} %collective-permute-done.5.cross_ref, bf16[256,512]{1,0:T(8,128)(2,1)S(1)} %collective-permute-done.6.across_ref, ...), custom_call_target="tpu_custom_call" | custom-call | tf_op jit(solution)/shard_map/gram/pallas_call | solution.py:201
  123.5 30.7 %all_to_all.15 = bf16[8,64,1024]{2,1,0:T(8,128)(2,1)S(1)} all-to-all(bf16[8,64,1024]{2,1,0:T(8,128)(2,1)S(1)} %bitcast.43), channel_id=1, replica_groups=mesh['xl'=2,'y'=4,'z'=8,'xh'=2,'core'=2] {'z'}, dimensions={0} | all-to-all | bytes 2097152 | tf_op jit(solution)/shard_map/all_to_all | solution.py:24
  154.2 0.9 convert_reduce_fusion
  (4 shorter events, 0.1 us)
Async XLA Ops:
  0.0 40.3 %copy-start.2 = (f32[4,128]{1,0:T(4,128)S(1)}, f32[4,128]{1,0:T(4,128)}, u32[]{:S(2)}) copy-start(f32[4,128]{1,0:T(4,128)} %wind_y_ref.5) | copy-start | bytes 6148
  0.0 40.3 %copy-start.1 = (f32[4,128]{1,0:T(4,128)S(1)}, f32[4,128]{1,0:T(4,128)}, u32[]{:S(2)}) copy-start(f32[4,128]{1,0:T(4,128)} %wind_x_ref.5) | copy-start | bytes 6148
  0.0 40.3 %copy-start = (f32[1024,4,128]{2,1,0:T(4,128)S(1)}, f32[1024,4,128]{2,1,0:T(4,128)}, u32[]{:S(2)}) copy-start(f32[1024,4,128]{2,1,0:T(4,128)} %param.6) | copy-start | bytes 6291460
  4.9 45.1 %all-to-all-start = ((bf16[64,8,256]{2,1,0:T(8,128)(2,1)}), bf16[64,8,256]{2,1,0:T(8,128)(2,1)S(1)}, u32[]{:S(2)}, u32[]{:S(2)}) async-start(bf16[64,8,256]{2,1,0:T(8,128)(2,1)} %fusion), calls=%async_computation | async-start | bytes 524288 | tf_op jit(solution)/shard_map/all_to_all | solution.py:24
  20.5 19.8 %collective-permute-start.2 = (bf16[1936,128]{1,0:T(8,128)(2,1)}, bf16[1936,128]{1,0:T(8,128)(2,1)S(1)}, u32[]{:S(2)}, u32[]{:S(2)}) collective-permute-start(bf16[1936,128]{1,0:T(8,128)(2,1)} %get-tuple-element.11), channel_id=1, source_target_pairs={{0,4},{4,8},{8,12},{12,16},{16,20},{20,24},{24,28},{28,32},{32,36}... | collective-permute-start | bytes 1486856 | tf_op jit(solution)/shard_map/ppermute | solution.py:20
  22.1 18.2 %collective-permute-start.3 = (bf16[1936,128]{1,0:T(8,128)(2,1)}, bf16[1936,128]{1,0:T(8,128)(2,1)S(1)}, u32[]{:S(2)}, u32[]{:S(2)}) collective-permute-start(bf16[1936,128]{1,0:T(8,128)(2,1)} %get-tuple-element.12), channel_id=1, source_target_pairs={{0,252},{4,0},{8,4},{12,8},{16,12},{20,16},{24,20},{28,24},{32,28}... | collective-permute-start | bytes 1486856 | tf_op jit(solution)/shard_map/ppermute | solution.py:20
  26.8 19.6 %collective-permute-start = (bf16[1168,128]{1,0:T(8,128)(2,1)}, bf16[1168,128]{1,0:T(8,128)(2,1)S(1)}, u32[]{:S(2)}, u32[]{:S(2)}) collective-permute-start(bf16[1168,128]{1,0:T(8,128)(2,1)} %get-tuple-element.9), channel_id=1, source_target_pairs={{0,4},{4,8},{8,12},{12,16},{16,20},{20,24},{24,28},{28,32},{32,36}... | collective-permute-start | bytes 897032 | tf_op jit(solution)/shard_map/ppermute | solution.py:20
  26.8 19.6 %collective-permute-start.1 = (bf16[1168,128]{1,0:T(8,128)(2,1)}, bf16[1168,128]{1,0:T(8,128)(2,1)S(1)}, u32[]{:S(2)}, u32[]{:S(2)}) collective-permute-start(bf16[1168,128]{1,0:T(8,128)(2,1)} %get-tuple-element.10), channel_id=1, source_target_pairs={{0,252},{4,0},{8,4},{12,8},{16,12},{20,16},{24,20},{28,24},{32,28}... | collective-permute-start | bytes 897032 | tf_op jit(solution)/shard_map/ppermute | solution.py:20
  51.8 28.8 %copy-start.3 = (bf16[128]{0:T(256)(128)(2,1)S(1)}, bf16[128]{0:T(256)(128)(2,1)}, u32[]{:S(2)}) copy-start(bf16[128]{0:T(256)(128)(2,1)} %param.11) | copy-start | bytes 772
  51.8 24.1 %all-to-all-start.1 = ((bf16[64,8,512]{2,1,0:T(8,128)(2,1)}), bf16[64,8,512]{2,1,0:T(8,128)(2,1)S(1)}, u32[]{:S(2)}, u32[]{:S(2)}) async-start(bf16[64,8,512]{2,1,0:T(8,128)(2,1)} %bitcast.23), calls=%async_computation.1 | async-start | bytes 1048576 | tf_op jit(solution)/shard_map/all_to_all | solution.py:24
  76.5 6.3 %collective-permute-start.5 = (bf16[128,512]{1,0:T(8,128)(2,1)S(1)}, bf16[128,512]{1,0:T(8,128)(2,1)S(1)}, u32[]{:S(2)}, u32[]{:S(2)}) collective-permute-start(bf16[128,512]{1,0:T(8,128)(2,1)S(1)} %get-tuple-element.13), channel_id=1, source_target_pairs={{0,32},{1,96},{2,160},{3,224},{32,0},{33,64},{34,128},{35,192},{64... | collective-permute-start | bytes 393224 | tf_op jit(solution)/shard_map/ppermute | solution.py:271
  77.7 8.2 %collective-permute-start.4 = (bf16[128,512]{1,0:T(8,128)(2,1)S(1)}, bf16[128,512]{1,0:T(8,128)(2,1)S(1)}, u32[]{:S(2)}, u32[]{:S(2)}) collective-permute-start(bf16[128,512]{1,0:T(8,128)(2,1)S(1)} %get-tuple-element.14), channel_id=1, source_target_pairs={{0,0},{1,64},{2,128},{3,192},{32,32},{33,96},{34,160},{35,224},{64... | collective-permute-start | bytes 393224 | tf_op jit(solution)/shard_map/ppermute | solution.py:270
  86.0 8.3 %collective-permute-start.6 = (bf16[256,512]{1,0:T(8,128)(2,1)S(1)}, bf16[256,512]{1,0:T(8,128)(2,1)S(1)}, u32[]{:S(2)}, u32[]{:S(2)}) collective-permute-start(bf16[256,512]{1,0:T(8,128)(2,1)S(1)} %pad_maximum_fusion.1), channel_id=1, source_target_pairs={{0,2},{2,0},{1,3},{3,1},{4,6},{6,4},{5,7},{7,5},{8,10},{10,8},{9,1... | collective-permute-start | bytes 786440 | tf_op jit(solution)/shard_map/ppermute | solution.py:20
  86.2 16.6 %collective-permute-start.11 = (bf16[128,1024]{1,0:T(8,128)(2,1)S(1)}, bf16[128,1024]{1,0:T(8,128)(2,1)S(1)}, u32[]{:S(2)}, u32[]{:S(2)}) collective-permute-start(bf16[128,1024]{1,0:T(8,128)(2,1)S(1)} %pad_maximum_fusion.2.refs_0_), channel_id=1, source_target_pairs={{0,96},{32,0},{64,32},{96,64},{1,97},{33,1},{65,33},{97,65},{2,98}... | collective-permute-start | bytes 786440 | tf_op jit(solution)/shard_map/ppermute | solution.py:20
  88.8 14.0 %collective-permute-start.10 = (bf16[128,1024]{1,0:T(8,128)(2,1)S(1)}, bf16[128,1024]{1,0:T(8,128)(2,1)S(1)}, u32[]{:S(2)}, u32[]{:S(2)}) collective-permute-start(bf16[128,1024]{1,0:T(8,128)(2,1)S(1)} %pad_maximum_fusion.2.refs_0_), channel_id=1, source_target_pairs={{0,64},{32,96},{64,0},{96,32},{1,65},{33,97},{65,1},{97,33},{2,66}... | collective-permute-start | bytes 786440 | tf_op jit(solution)/shard_map/ppermute | solution.py:20
  89.9 9.7 %collective-permute-start.8 = (bf16[128,1024]{1,0:T(8,128)(2,1)S(1)}, bf16[128,1024]{1,0:T(8,128)(2,1)S(1)}, u32[]{:S(2)}, u32[]{:S(2)}) collective-permute-start(bf16[128,1024]{1,0:T(8,128)(2,1)S(1)} %pad_maximum_fusion.2.refs_0_), channel_id=1, source_target_pairs={{0,128},{128,0},{1,129},{129,1},{2,130},{130,2},{3,131},{131,3},{4... | collective-permute-start | bytes 786440 | tf_op jit(solution)/shard_map/ppermute | solution.py:20
  95.1 25.1 %collective-permute-start.7 = (bf16[512,512]{1,0:T(8,128)(2,1)}, bf16[512,512]{1,0:T(8,128)(2,1)S(1)}, u32[]{:S(2)}, u32[]{:S(2)}) collective-permute-start(bf16[512,512]{1,0:T(8,128)(2,1)} %pad_maximum_fusion), channel_id=1, source_target_pairs={{0,1},{1,0},{2,3},{3,2},{4,5},{5,4},{6,7},{7,6},{8,9},{9,8},{10,11... | collective-permute-start | bytes 1572872 | tf_op jit(solution)/shard_map/ppermute | solution.py:20
  99.5 16.0 %collective-permute-start.9 = (bf16[128,1024]{1,0:T(8,128)(2,1)S(1)}, bf16[128,1024]{1,0:T(8,128)(2,1)S(1)}, u32[]{:S(2)}, u32[]{:S(2)}) collective-permute-start(bf16[128,1024]{1,0:T(8,128)(2,1)S(1)} %pad_maximum_fusion.2.refs_0_), channel_id=1, source_target_pairs={{0,32},{32,64},{64,96},{96,0},{1,33},{33,65},{65,97},{97,1},{2,34}... | collective-permute-start | bytes 786440 | tf_op jit(solution)/shard_map/ppermute | solution.py:20
  99.6 16.0 %collective-permute-start.14 = (bf16[128,1024]{1,0:T(8,128)(2,1)S(1)}, bf16[128,1024]{1,0:T(8,128)(2,1)S(1)}, u32[]{:S(2)}, u32[]{:S(2)}) collective-permute-start(bf16[128,1024]{1,0:T(8,128)(2,1)S(1)} %collective-permute-done.8.refs_1_), channel_id=1, source_target_pairs={{0,96},{32,0},{64,32},{96,64},{1,97},{33,1},{65,33},{97,65},{2,98}... | collective-permute-start | bytes 786440 | tf_op jit(solution)/shard_map/ppermute | solution.py:20
  102.8 12.8 %collective-permute-start.13 = (bf16[128,1024]{1,0:T(8,128)(2,1)S(1)}, bf16[128,1024]{1,0:T(8,128)(2,1)S(1)}, u32[]{:S(2)}, u32[]{:S(2)}) collective-permute-start(bf16[128,1024]{1,0:T(8,128)(2,1)S(1)} %collective-permute-done.8.refs_1_), channel_id=1, source_target_pairs={{0,64},{32,96},{64,0},{96,32},{1,65},{33,97},{65,1},{97,33},{2,66}... | collective-permute-start | bytes 786440 | tf_op jit(solution)/shard_map/ppermute | solution.py:20
  102.8 17.4 %collective-permute-start.12 = (bf16[128,1024]{1,0:T(8,128)(2,1)S(1)}, bf16[128,1024]{1,0:T(8,128)(2,1)S(1)}, u32[]{:S(2)}, u32[]{:S(2)}) collective-permute-start(bf16[128,1024]{1,0:T(8,128)(2,1)S(1)} %collective-permute-done.8.refs_1_), channel_id=1, source_target_pairs={{0,32},{32,64},{64,96},{96,0},{1,33},{33,65},{65,97},{97,1},{2,34}... | collective-permute-start | bytes 786440 | tf_op jit(solution)/shard_map/ppermute | solution.py:20

commit v2 on v1

--- a/solution.py
+++ b/solution.py
@@ -1,3 +1,5 @@
+import functools
+
 import jax
 import jax.numpy as jnp
 from jax import lax
@@ -55,10 +57,23 @@
 
 
 def transport_body(
-    pulse_ref, a0, a1, a2, b0, b1, b2, a_winds, b_winds, wind_x_ref, wind_y_ref, *refs
+    skip, pulse_ref, a0, a1, a2, b0, b1, b2, a_winds, b_winds, wind_x_ref, wind_y_ref, *refs
 ):
-    out_ref, coef_ref = refs[-2:]
+    out_ref, coef_ref, fetched_ref, sems = refs[-4:]
     count = out_ref.shape[0]
+    block = pl.program_id(0)
+
+    def fetch(i):
+        source = pulse_ref.at[pl.ds((skip + i) * 4 * count, 4 * count)]
+        return pltpu.make_async_copy(source, fetched_ref.at[i % 2], sems.at[i % 2])
+
+    @pl.when(block == 0)
+    def _():
+        fetch(block).start()
+
+    @pl.when(block + 1 < pl.num_programs(0))
+    def _():
+        fetch(block + 1).start()
 
     @pl.when(pl.program_id(0) == 0)
     def _():
@@ -79,11 +94,13 @@
             for w in range(8):
                 coef_ref[k * 8 + w] = jnp.broadcast_to(part[w : w + 1], (PIECE, 128))
 
+    fetch(block).wait()
+    slot = block % 2
     for piece in range(count // PIECE):
         at = piece * PIECE
         field = (
             [ref[at : at + PIECE].astype(jnp.float32) for ref in (a0, a1, a2)]
-            + [pulse_ref[pl.ds(4 * at + r, PIECE, 4), :] for r in range(4)]
+            + [fetched_ref[slot, pl.ds(4 * at + r, PIECE, 4), :] for r in range(4)]
             + [ref[at : at + PIECE].astype(jnp.float32) for ref in (b0, b1, b2)]
         )
         for step in range(STEPS):
@@ -113,7 +130,7 @@
     last = [pl.BlockSpec((16, 128), lambda i: (STEPS * size // 16, 0))] * 2
     wind = pl.BlockSpec((4, 128), lambda i: (0, 0))
     operands = [pulses, *[above] * 3, *[below] * 3, above, below, wind_x, wind_y]
-    specs = [pl.BlockSpec((4 * block, 128), lambda i: (skip + i, 0))] + halo + halo + last
+    specs = [pl.BlockSpec(memory_space=pltpu.HBM)] + halo + halo + last
     specs += [wind, wind]
     aliases = {}
     if into is not None:
@@ -121,12 +138,16 @@
         operands.append(into)
         specs.append(pl.BlockSpec(memory_space=pl.ANY))
     return pl.pallas_call(
-        transport_body,
+        functools.partial(transport_body, skip),
         grid=(steps,),
         in_specs=specs,
         out_specs=pl.BlockSpec((block, 512), lambda i: (skip + i, 0)),
         out_shape=jax.ShapeDtypeStruct((tracers, 512), jnp.bfloat16),
-        scratch_shapes=[pltpu.VMEM((40, PIECE, 128), jnp.float32)],
+        scratch_shapes=[
+            pltpu.VMEM((40, PIECE, 128), jnp.float32),
+            pltpu.VMEM((2, 4 * block, 128), jnp.float32),
+            pltpu.SemaphoreType.DMA((2,)),
+        ],
         input_output_aliases=aliases,
         compiler_params=pltpu.CompilerParams(vmem_limit_bytes=GRANT),
         name="transport",
@@ -173,42 +194,52 @@
     )(rows, sampled, sampled)
 
 
-def gram_body(place_ref, same_ref, cross_ref, across_ref, other_ref, *refs):
-    cols, out_ref, rows_ref, cols_ref = refs[:-3], refs[-3], refs[-2], refs[-1]
+def gram_body(apart, place_ref, same_ref, cross_ref, across_ref, other_ref, *refs):
+    cols, outs, scratch = refs[:8], refs[8:-3], refs[-3:]
+    rows_ref, cols_ref, sum_ref = scratch
     block = same_ref.shape[0]
-
-    @pl.when(pl.program_id(0) == 0)
-    def _():
-        parts = [same_ref[...], cross_ref[...]]
-        for ref in (across_ref, other_ref):
-            parts += [ref[s : s + block] for s in range(0, ref.shape[0], block)]
-        for k, part in enumerate(parts):
-            at = pl.multiple_of(place_ref[k] * block, block)
-            rows_ref[:, pl.ds(at, block)] = part.T
-
+    parts = [same_ref[...], cross_ref[...]]
+    for ref in (across_ref, other_ref):
+        parts += [ref[s : s + block] for s in range(0, ref.shape[0], block)]
+    for k, part in enumerate(parts):
+        at = pl.multiple_of(place_ref[k] * block, block)
+        rows_ref[:, pl.ds(at, block)] = part.T
     for k, ref in enumerate(cols):
         at = pl.multiple_of(place_ref[8 + k] * block, block)
         cols_ref[pl.ds(at, block), :] = ref[...]
-    out_ref[...] = lax.dot_general(
+    tile = lax.dot_general(
         rows_ref[...], cols_ref[...], (((1,), (0,)), ((), ())), preferred_element_type=jnp.float32
-    ).astype(jnp.bfloat16)
-
-
-def gram_tile(place, same, cross, across, other, cols, block=256):
-    obs, tracers = cols[0].shape
-    width = same.shape[1]
-    whole = lambda v: pl.BlockSpec(v.shape, lambda i: (0, 0))
+    )
+    if not apart:
+        outs[0][...] = tile.astype(jnp.bfloat16)
+        return
+    sum_ref[...] = tile
+    deep = len(outs)
+    size = tile.shape[0] // deep
+    for d, out_ref in enumerate(outs):
+        at = pl.multiple_of(((place_ref[16] + d) % deep) * size, size)
+        out_ref[...] = sum_ref[pl.ds(at, size), :].astype(out_ref.dtype)
+
+
+def gram_tile(place, same, cross, across, other, cols, apart):
+    obs, width = cols[0].shape
+    rows = same.shape[1]
+    if apart:
+        size = (rows // apart, width)
+        shapes = [jax.ShapeDtypeStruct(size, jnp.float32)]
+        shapes += [jax.ShapeDtypeStruct(size, jnp.bfloat16)] * (apart - 1)
+    else:
+        shapes = [jax.ShapeDtypeStruct((rows, width), jnp.bfloat16)]
+    whole = pl.BlockSpec(memory_space=pltpu.VMEM)
     return pl.pallas_call(
-        gram_body,
-        grid=(tracers // block,),
-        in_specs=[pl.BlockSpec(memory_space=pltpu.SMEM)]
-        + [whole(v) for v in (same, cross, across, other)]
-        + [pl.BlockSpec((obs, block), lambda i: (0, i))] * len(cols),
-        out_specs=pl.BlockSpec((width, block), lambda i: (0, i)),
-        out_shape=jax.ShapeDtypeStruct((width, tracers), jnp.bfloat16),
+        functools.partial(gram_body, apart),
+        in_specs=[pl.BlockSpec(memory_space=pltpu.SMEM)] + [whole] * (4 + len(cols)),
+        out_specs=[whole] * len(shapes),
+        out_shape=shapes,
         scratch_shapes=[
-            pltpu.VMEM((width, len(cols) * obs), jnp.bfloat16),
-            pltpu.VMEM((len(cols) * obs, block), jnp.bfloat16),
+            pltpu.VMEM((rows, len(cols) * obs), jnp.bfloat16),
+            pltpu.VMEM((len(cols) * obs, width), jnp.bfloat16),
+            pltpu.VMEM((rows, width), jnp.float32),
         ],
         compiler_params=pltpu.CompilerParams(vmem_limit_bytes=GRANT),
         name="gram",
@@ -227,6 +258,7 @@
     for k in range(2):
         halos.append((shifted(messages[2 * k + 1], CELLS, 1), shifted(messages[2 * k], CELLS, -1)))
     sampled = None
+    pulses = pltpu.with_memory_space_constraint(pulses, pltpu.HBM)
     for span, (above, below) in zip(spans(tracers), halos):
         sampled = transport(pulses, above, below, wind_x, wind_y, span, sampled)
 
@@ -257,7 +289,7 @@
         for c in chosen
     ]
     precision = obs_precision.astype(jnp.float32)[:, None]
-    weighted = jnp.concatenate([precision * j for j in jac], axis=1).astype(jnp.bfloat16)
+    weighted = [(precision * j).astype(jnp.bfloat16) for j in jac]
     low, high = [j.astype(jnp.bfloat16) for j in jac]
 
     group = lax.axis_size(XY)
@@ -272,24 +304,31 @@
     across = shifted(jnp.concatenate([same, cross], axis=0), "xh", 1)
     other = shifted(jnp.concatenate([same, cross, across], axis=0), "core", 1)
 
-    beside = shifted(weighted, "xl", 1)
     deep = lax.axis_size("y")
-    cols = [weighted, beside]
-    for value in (weighted, beside):
-        for d in range(1, deep):
-            cols.append(shifted(value, "y", d))
+    cols = []
+    for part, value in enumerate(weighted):
+        beside = shifted(value, "xl", 1)
+        cols.append([value, beside])
+        for source in (value, beside):
+            for d in range(1, deep):
+                cols[part].append(shifted(source, "y", d))
     xl, y = lax.axis_index("xl"), lax.axis_index("y")
     owners = [here, (1 - xl) * deep + y]
     owners += [xl * deep + (y - d) % deep for d in range(1, deep)]
     owners += [(1 - xl) * deep + (y - d) % deep for d in range(1, deep)]
     tracer = lax.axis_index(TRACERS)
     row_owners = [2 * (tracer ^ flip) + (odd ^ s) for flip in (0, 2, 1, 3) for s in (0, 1)]
-    place = jnp.stack(row_owners + owners).astype(jnp.int32)
-
-    partial = gram_tile(place, same, cross, across, other, cols)
+    place = jnp.stack(row_owners + owners + [lax.axis_index("z")]).astype(jnp.int32)
+
     depth = lax.axis_size("z")
-    parts = exchanged(partial.reshape(depth, half // depth, tracers), "z")
-    return jnp.sum(parts.astype(jnp.float32), axis=0)
+    tile = gram_tile(place, same, cross, across, other, cols[0], 0)[0]
+    parts = exchanged(tile.reshape(depth, half // depth, half), "z")
+    total = jnp.sum(parts.astype(jnp.float32), axis=0)
+    blocks = gram_tile(place, same, cross, across, other, cols[1], depth)
+    last = blocks[0]
+    for d in (4, 3, 5, 2, 6, 1, 7):
+        last = last + shifted(blocks[d], "z", d).astype(jnp.float32)
+    return jnp.concatenate([total, last], axis=1)
 
 
 def solution(mesh):

time: 157 us -> 161 us (1.025)
  blocking collectives: 30.7 us -> 0 us
  starting transfers between devices: 53.4 us -> 77.7 us
  waiting for transfers between devices: 45.9 us -> 56 us
  Pallas kernels: 17.5 us -> 20.2 us
    all_to_all x1 -> x0, blocking collectives: 30.7 us -> none  [exchanged(): return lax.all_to_all(value, axis, split_axis=0, concat_axis=0, tiled=True)]
    ppermute x13 -> x27, starting transfers between devices: 28.8 us -> 49.8 us  [shifted(): lax.ppermute(value, axis, [(i, (i + steps) % count) for i in range(count)])]
    ppermute x13 -> x27, waiting for transfers between devices: 24.2 us -> 33.8 us  [shifted(): lax.ppermute(value, axis, [(i, (i + steps) % count) for i in range(count)])]
    all_to_all x2 -> x3, starting transfers between devices: 20.5 us -> 23.9 us  [exchanged(): return lax.all_to_all(value, axis, split_axis=0, concat_axis=0, tiled=True)]
    pallas_call x3 -> x4, Pallas kernels: 12.9 us -> 15.5 us  [the longest x2 11.4 us: transport(): pl.pallas_call(functools.partial(transport_body, skip), grid=(steps,), in...]
    all_to_all x2 -> x3, waiting for transfers between devices: 16.3 us -> 16 us  [exchanged(): return lax.all_to_all(value, axis, split_axis=0, concat_axis=0, tiled=True)]
  transfers between devices with their start and end apart: 17 -> 32, of which waited for: 7 -> 14; matrix products, arithmetic and copies ran while one was open for 1% -> 0% of each run, Pallas kernels for 8% -> 10%
where the time goes in v2:
time: 161 us
  starting transfers between devices  77.7 us (48%)
  waiting for transfers between devices  56 us (35%)
  Pallas kernels  20.2 us (13%)
  other arithmetic  4.73 us (3%)
    ppermute x27, starting transfers between devices, shifted(): lax.ppermute(value, axis, [(i, (i + steps) % count) for i in range(count)])  49.8 us
    ppermute x27, waiting for transfers between devices, shifted(): lax.ppermute(value, axis, [(i, (i + steps) % count) for i in range(count)])  33.8 us
    all_to_all x3, starting transfers between devices, exchanged(): return lax.all_to_all(value, axis, split_axis=0, concat_axis=0, tiled=True)  23.9 us
    all_to_all x3, waiting for transfers between devices, exchanged(): return lax.all_to_all(value, axis, split_axis=0, concat_axis=0, tiled=True)  16 us
    pallas_call x2, Pallas kernels, transport(): pl.pallas_call(functools.partial(transport_body, skip), grid=(steps,), in...  11.4 us
    pallas_call x2, Pallas kernels, gram_tile(): pl.pallas_call(functools.partial(gram_body, apart), in_specs=[pl.BlockSpe...  4.12 us
    ppermute x1, waiting for transfers between devices, on_device(): same = lax.ppermute(jnp.where(odd == 0, low, high), PLANE, to_same)  3.73 us
  transfers between devices with their start and end apart: 32, of which 14 were waited for; matrix products, arithmetic and copies ran while one was open for 0% of the time, Pallas kernels for 10%

profile of v2, /device:TPU:4, one launch (start us, length us, event | category | flops | bytes accessed | tf_op | source)
XLA Modules:
  0.0 160.6 jit_solution(13421036652953506712)
XLA Ops:
  0.0 0.9 convert_reduce_fusion.2
  0.9 0.7 fusion.15
  1.6 1.0 convert_reduce_fusion.1
  2.6 1.0 fusion.8
  3.6 0.1 iota_compare_fusion
  3.8 1.1 fusion
  4.8 12.7 %all-to-all-start = ((bf16[64,8,256]{2,1,0:T(8,128)(2,1)}), bf16[64,8,256]{2,1,0:T(8,128)(2,1)S(1)}, u32[]{:S(2)}, u32[]{:S(2)}) async-start(bf16[64,8,256]{2,1,0:T(8,128)(2,1)} %fusion), calls=%async_computation | async-start | bytes 524288 | tf_op jit(solution)/shard_map/all_to_all | solution.py:26
  17.6 2.9 %edges.1 = (bf16[1936,128]{1,0:T(8,128)(2,1)}, bf16[1936,128]{1,0:T(8,128)(2,1)}, bf16[1168,128]{1,0:T(8,128)(2,1)}, bf16[1168,128]{1,0:T(8,128)(2,1)}) custom-call(f32[4096,128]{1,0:T(8,128)} %bitcast.42, f32[4,128]{1,0:T(4,128)} %wind_x_ref.5, f32[4,128]{1,0:T(4,128)} %wind_y_ref.5), custom_call_target="tpu_custom_call" | custom-call | tf_op jit(solution)/shard_map/edges/pallas_call | solution.py:53
  20.4 1.6 collective-permute-start.2
  22.0 4.7 %collective-permute-start.3 = (bf16[1936,128]{1,0:T(8,128)(2,1)}, bf16[1936,128]{1,0:T(8,128)(2,1)S(1)}, u32[]{:S(2)}, u32[]{:S(2)}) collective-permute-start(bf16[1936,128]{1,0:T(8,128)(2,1)} %get-tuple-element.20), channel_id=1, source_target_pairs={{0,252},{4,0},{8,4},{12,8},{16,12},{20,16},{24,20},{28,24},{32,28}... | collective-permute-start | bytes 1486856 | tf_op jit(solution)/shard_map/ppermute | solution.py:22
  26.7 6.2 %collective-permute-start.1 = (bf16[1168,128]{1,0:T(8,128)(2,1)}, bf16[1168,128]{1,0:T(8,128)(2,1)S(1)}, u32[]{:S(2)}, u32[]{:S(2)}) collective-permute-start(bf16[1168,128]{1,0:T(8,128)(2,1)} %get-tuple-element.18), channel_id=1, source_target_pairs={{0,252},{4,0},{8,4},{12,8},{16,12},{20,16},{24,20},{28,24},{32,28}... | collective-permute-start | bytes 897032 | tf_op jit(solution)/shard_map/ppermute | solution.py:22
  32.9 7.3 %collective-permute-done.2.a0.a1.a2.a_winds = bf16[1936,128]{1,0:T(8,128)(2,1)S(1)} collective-permute-done((bf16[1936,128]{1,0:T(8,128)(2,1)}, bf16[1936,128]{1,0:T(8,128)(2,1)S(1)}, u32[]{:S(2)}, u32[]{:S(2)}) %collective-permute-start.2) | collective-permute-done | bytes 495648 | tf_op jit(solution)/shard_map/ppermute | solution.py:22
  40.2 6.9 %transport.2.refs_0_ = bf16[1024,512]{1,0:T(8,128)(2,1)S(1)} custom-call(f32[4096,128]{1,0:T(8,128)} %bitcast.43, bf16[1936,128]{1,0:T(8,128)(2,1)S(1)} %collective-permute-done.2.a0.a1.a2.a_winds, bf16[1936,128]{1,0:T(8,128)(2,1)S(1)} %collective-permute-done.2.a0.a1.a2.a_winds, bf16[1936,128]{1,0:T(8,128)(2,1)S(1)} %collective-permute-done.2.a0.a1.a2.a_winds, ...), custom_call_target="tpu_custom_call" | custom-call | tf_op jit(solution)/shard_map/transport/pallas_call | solution.py:140
  47.1 4.5 %transport.3.low_ref.high_ref = bf16[1024,512]{1,0:T(8,128)(2,1)S(1)} custom-call(f32[4096,128]{1,0:T(8,128)} %bitcast.44, bf16[1168,128]{1,0:T(8,128)(2,1)S(1)} %collective-permute-done.a0.a1.a2.a_winds, bf16[1168,128]{1,0:T(8,128)(2,1)S(1)} %collective-permute-done.a0.a1.a2.a_winds, ...), custom_call_target="tpu_custom_call", output_to_operand_aliasing={{}: (11, {})} | custom-call | tf_op jit(solution)/shard_map/transport/pallas_call | solution.py:140
  51.7 1.8 %jacobian.1 = bf16[512,512]{1,0:T(8,128)(2,1)} custom-call(bf16[512,256]{1,0:T(8,128)(2,1)S(1)} %bitcast.41, bf16[1024,512]{1,0:T(8,128)(2,1)S(1)} %transport.3.low_ref.high_ref, bf16[1024,512]{1,0:T(8,128)(2,1)S(1)} %transport.3.low_ref.high_ref), custom_call_target="tpu_custom_call" | custom-call | tf_op jit(solution)/shard_map/jacobian/pallas_call | solution.py:181
  53.5 7.6 %all-to-all-start.1 = ((bf16[64,8,512]{2,1,0:T(8,128)(2,1)}), bf16[64,8,512]{2,1,0:T(8,128)(2,1)S(1)}, u32[]{:S(2)}, u32[]{:S(2)}) async-start(bf16[64,8,512]{2,1,0:T(8,128)(2,1)} %bitcast.24), calls=%async_computation.1 | async-start | bytes 1048576 | tf_op jit(solution)/shard_map/all_to_all | solution.py:26
  61.1 0.0 copy-start.2
  61.2 16.0 %all-to-all-done.1 = bf16[64,8,512]{2,1,0:T(8,128)(2,1)S(1)} async-done(((bf16[64,8,512]{2,1,0:T(8,128)(2,1)}), bf16[64,8,512]{2,1,0:T(8,128)(2,1)S(1)}, u32[]{:S(2)}, u32[]{:S(2)}) %all-to-all-start.1) | async-done | bytes 524320 | tf_op jit(solution)/shard_map/all_to_all | solution.py:26
  77.1 0.3 fusion.3
  77.4 0.3 broadcast_select_fusion
  77.7 2.9 %collective-permute-start.4 = (bf16[128,512]{1,0:T(8,128)(2,1)S(1)}, bf16[128,512]{1,0:T(8,128)(2,1)S(1)}, u32[]{:S(2)}, u32[]{:S(2)}) collective-permute-start(bf16[128,512]{1,0:T(8,128)(2,1)S(1)} %get-tuple-element.30), channel_id=1, source_target_pairs={{0,0},{1,64},{2,128},{3,192},{32,32},{33,96},{34,160},{35,224},{64... | collective-permute-start | bytes 393224 | tf_op jit(solution)/shard_map/ppermute | solution.py:302
  80.6 1.2 collective-permute-start.5
  81.8 3.7 %collective-permute-done.4.same_ref = bf16[128,512]{1,0:T(8,128)(2,1)S(1)} collective-permute-done((bf16[128,512]{1,0:T(8,128)(2,1)S(1)}, bf16[128,512]{1,0:T(8,128)(2,1)S(1)}, u32[]{:S(2)}, u32[]{:S(2)}) %collective-permute-start.4) | collective-permute-done | bytes 131104 | tf_op jit(solution)/shard_map/ppermute | solution.py:302
  85.5 2.5 %collective-permute-done.5.cross_ref = bf16[128,512]{1,0:T(8,128)(2,1)S(1)} collective-permute-done((bf16[128,512]{1,0:T(8,128)(2,1)S(1)}, bf16[128,512]{1,0:T(8,128)(2,1)S(1)}, u32[]{:S(2)}, u32[]{:S(2)}) %collective-permute-start.5) | collective-permute-done | bytes 131104 | tf_op jit(solution)/shard_map/ppermute | solution.py:303
  88.0 0.1 collective-permute-start.6
  88.1 10.2 %collective-permute-done.6.across_ref = bf16[256,512]{1,0:T(8,128)(2,1)S(1)} collective-permute-done((bf16[256,512]{1,0:T(8,128)(2,1)S(1)}, bf16[256,512]{1,0:T(8,128)(2,1)S(1)}, u32[]{:S(2)}, u32[]{:S(2)}) %collective-permute-start.6) | collective-permute-done | bytes 262176 | tf_op jit(solution)/shard_map/ppermute | solution.py:22
  98.4 0.4 collective-permute-start.7
  98.7 0.1 multiply_convert_fusion.1
  98.8 0.3 collective-permute-start.8
  99.2 0.2 collective-permute-start.10
  99.3 3.6 %collective-permute-start.11 = (bf16[128,512]{1,0:T(8,128)(2,1)S(1)}, bf16[128,512]{1,0:T(8,128)(2,1)S(1)}, u32[]{:S(2)}, u32[]{:S(2)}) collective-permute-start(bf16[128,512]{1,0:T(8,128)(2,1)S(1)} %get-tuple-element.35.refs_0_), channel_id=1, source_target_pairs={{0,96},{32,0},{64,32},{96,64},{1,97},{33,1},{65,33},{97,65},{2,98}... | collective-permute-start | bytes 393224 | tf_op jit(solution)/shard_map/ppermute | solution.py:22
  102.9 1.6 %collective-permute-done.8.refs_1_ = bf16[128,512]{1,0:T(8,128)(2,1)S(1)} collective-permute-done((bf16[128,512]{1,0:T(8,128)(2,1)S(1)}, bf16[128,512]{1,0:T(8,128)(2,1)S(1)}, u32[]{:S(2)}, u32[]{:S(2)}) %collective-permute-start.8) | collective-permute-done | bytes 131104 | tf_op jit(solution)/shard_map/ppermute | solution.py:22
  104.6 1.5 collective-permute-start.12
  106.0 1.0 collective-permute-done.10.refs_3_
  107.1 0.6 collective-permute-start.13
  107.6 3.2 %collective-permute-start.14 = (bf16[128,512]{1,0:T(8,128)(2,1)S(1)}, bf16[128,512]{1,0:T(8,128)(2,1)S(1)}, u32[]{:S(2)}, u32[]{:S(2)}) collective-permute-start(bf16[128,512]{1,0:T(8,128)(2,1)S(1)} %collective-permute-done.8.refs_1_), channel_id=1, source_target_pairs={{0,96},{32,0},{64,32},{96,64},{1,97},{33,1},{65,33},{97,65},{2,98}... | collective-permute-start | bytes 393224 | tf_op jit(solution)/shard_map/ppermute | solution.py:22
  110.9 0.1 stack.71.place_ref
  111.0 4.3 %collective-permute-done.12.refs_5_ = bf16[128,512]{1,0:T(8,128)(2,1)S(1)} collective-permute-done((bf16[128,512]{1,0:T(8,128)(2,1)S(1)}, bf16[128,512]{1,0:T(8,128)(2,1)S(1)}, u32[]{:S(2)}, u32[]{:S(2)}) %collective-permute-start.12) | collective-permute-done | bytes 131104 | tf_op jit(solution)/shard_map/ppermute | solution.py:22
  115.3 2.4 %gram.2 = bf16[512,512]{1,0:T(8,128)(2,1)} custom-call(s32[17]{0:T(128)S(1)} %stack.71.place_ref, bf16[128,512]{1,0:T(8,128)(2,1)S(1)} %collective-permute-done.4.same_ref, bf16[128,512]{1,0:T(8,128)(2,1)S(1)} %collective-permute-done.5.cross_ref, bf16[256,512]{1,0:T(8,128)(2,1)S(1)} %collective-permute-done.6.across_ref, ...), custom_call_target="tpu_custom_call" | custom-call | tf_op jit(solution)/shard_map/gram/pallas_call | solution.py:234
  117.7 3.5 %all-to-all-start.2 = ((bf16[8,64,512]{2,1,0:T(8,128)(2,1)}), bf16[8,64,512]{2,1,0:T(8,128)(2,1)S(1)}, u32[]{:S(2)}, u32[]{:S(2)}) async-start(bf16[8,64,512]{2,1,0:T(8,128)(2,1)} %bitcast.26), calls=%async_computation.2 | async-start | bytes 1048576 | tf_op jit(solution)/shard_map/all_to_all | solution.py:26
  121.2 1.8 %collective-permute-start.15 = (bf16[128,512]{1,0:T(8,128)(2,1)S(1)}, bf16[128,512]{1,0:T(8,128)(2,1)S(1)}, u32[]{:S(2)}, u32[]{:S(2)}) collective-permute-start(bf16[128,512]{1,0:T(8,128)(2,1)S(1)} %get-tuple-element.36.refs_0_), channel_id=1, source_target_pairs={{0,128},{128,0},{1,129},{129,1},{2,130},{130,2},{3,131},{131,3},{4... | collective-permute-start | bytes 393224 | tf_op jit(solution)/shard_map/ppermute | solution.py:22
  123.0 1.4 collective-permute-start.16
  124.4 2.3 %collective-permute-start.17 = (bf16[128,512]{1,0:T(8,128)(2,1)S(1)}, bf16[128,512]{1,0:T(8,128)(2,1)S(1)}, u32[]{:S(2)}, u32[]{:S(2)}) collective-permute-start(bf16[128,512]{1,0:T(8,128)(2,1)S(1)} %get-tuple-element.36.refs_0_), channel_id=1, source_target_pairs={{0,64},{32,96},{64,0},{96,32},{1,65},{33,97},{65,1},{97,33},{2,66}... | collective-permute-start | bytes 393224 | tf_op jit(solution)/shard_map/ppermute | solution.py:22
  126.7 1.0 collective-permute-start.18
  127.7 1.1 collective-permute-start.19
  128.8 1.2 collective-permute-start.20
  130.0 1.0 collective-permute-done.16.refs_2_
  131.0 0.8 collective-permute-start.21
  131.8 2.1 %collective-permute-done.17.refs_3_ = bf16[128,512]{1,0:T(8,128)(2,1)S(1)} collective-permute-done((bf16[128,512]{1,0:T(8,128)(2,1)S(1)}, bf16[128,512]{1,0:T(8,128)(2,1)S(1)}, u32[]{:S(2)}, u32[]{:S(2)}) %collective-permute-start.17) | collective-permute-done | bytes 131104 | tf_op jit(solution)/shard_map/ppermute | solution.py:22
  133.9 2.3 %collective-permute-done.19.refs_5_ = bf16[128,512]{1,0:T(8,128)(2,1)S(1)} collective-permute-done((bf16[128,512]{1,0:T(8,128)(2,1)S(1)}, bf16[128,512]{1,0:T(8,128)(2,1)S(1)}, u32[]{:S(2)}, u32[]{:S(2)}) %collective-permute-start.19) | collective-permute-done | bytes 131104 | tf_op jit(solution)/shard_map/ppermute | solution.py:22
  136.2 1.5 collective-permute-done.20.refs_6_
  137.7 1.7 %gram.3 = (f32[64,512]{1,0:T(8,128)S(1)}, bf16[64,512]{1,0:T(8,128)(2,1)S(1)}, bf16[64,512]{1,0:T(8,128)(2,1)S(1)}, bf16[64,512]{1,0:T(8,128)(2,1)S(1)}, bf16[64...) custom-call(s32[17]{0:T(128)S(1)} %stack.71.place_ref, ...), custom_call_target="tpu_custom_call" | custom-call | tf_op jit(solution)/shard_map/gram/pallas_call | solution.py:234
  139.4 5.6 %collective-permute-start.22 = (bf16[64,512]{1,0:T(8,128)(2,1)S(1)}, bf16[64,512]{1,0:T(8,128)(2,1)S(1)}, u32[]{:S(2)}, u32[]{:S(2)}) collective-permute-start(bf16[64,512]{1,0:T(8,128)(2,1)S(1)} %get-tuple-element.22), channel_id=1, source_target_pairs={{0,16},{4,20},{8,24},{12,28},{16,0},{20,4},{24,8},{28,12},{1,17},{... | collective-permute-start | bytes 196616 | tf_op jit(solution)/shard_map/ppermute | solution.py:22
  145.0 0.6 collective-permute-start.23
  145.6 4.5 %collective-permute-start.24 = (bf16[64,512]{1,0:T(8,128)(2,1)S(1)}, bf16[64,512]{1,0:T(8,128)(2,1)S(1)}, u32[]{:S(2)}, u32[]{:S(2)}) collective-permute-start(bf16[64,512]{1,0:T(8,128)(2,1)S(1)} %get-tuple-element.24), channel_id=1, source_target_pairs={{0,20},{4,24},{8,28},{12,0},{16,4},{20,8},{24,12},{28,16},{1,21},{... | collective-permute-start | bytes 196616 | tf_op jit(solution)/shard_map/ppermute | solution.py:22
  150.1 0.6 collective-permute-start.25
  150.7 3.6 %collective-permute-start.26 = (bf16[64,512]{1,0:T(8,128)(2,1)S(1)}, bf16[64,512]{1,0:T(8,128)(2,1)S(1)}, u32[]{:S(2)}, u32[]{:S(2)}) collective-permute-start(bf16[64,512]{1,0:T(8,128)(2,1)S(1)} %get-tuple-element.26), channel_id=1, source_target_pairs={{0,24},{4,28},{8,0},{12,4},{16,8},{20,12},{24,16},{28,20},{1,25},{... | collective-permute-start | bytes 196616 | tf_op jit(solution)/shard_map/ppermute | solution.py:22
  154.2 0.6 collective-permute-start.27
  154.8 0.1 collective-permute-done.23
  154.9 2.5 %collective-permute-start.28 = (bf16[64,512]{1,0:T(8,128)(2,1)S(1)}, bf16[64,512]{1,0:T(8,128)(2,1)S(1)}, u32[]{:S(2)}, u32[]{:S(2)}) collective-permute-start(bf16[64,512]{1,0:T(8,128)(2,1)S(1)} %get-tuple-element.28), channel_id=1, source_target_pairs={{0,28},{4,0},{8,4},{12,8},{16,12},{20,16},{24,20},{28,24},{1,29},{... | collective-permute-start | bytes 196616 | tf_op jit(solution)/shard_map/ppermute | solution.py:22
  157.5 2.2 %collective-permute-done.27 = bf16[64,512]{1,0:T(8,128)(2,1)S(1)} collective-permute-done((bf16[64,512]{1,0:T(8,128)(2,1)S(1)}, bf16[64,512]{1,0:T(8,128)(2,1)S(1)}, u32[]{:S(2)}, u32[]{:S(2)}) %collective-permute-start.27) | collective-permute-done | bytes 65568 | tf_op jit(solution)/shard_map/ppermute | solution.py:22
  159.7 0.1 convert_add_fusion
  159.8 0.1 convert_reduce_fusion
  159.9 0.7 pad_maximum_fusion.2
  (29 shorter events, 0.1 us)
Async XLA Ops:
  0.0 40.2 %copy-start = (f32[4,128]{1,0:T(4,128)S(1)}, f32[4,128]{1,0:T(4,128)}, u32[]{:S(2)}) copy-start(f32[4,128]{1,0:T(4,128)} %wind_x_ref.5) | copy-start | bytes 6148
  0.0 40.2 %copy-start.1 = (f32[4,128]{1,0:T(4,128)S(1)}, f32[4,128]{1,0:T(4,128)}, u32[]{:S(2)}) copy-start(f32[4,128]{1,0:T(4,128)} %wind_y_ref.5) | copy-start | bytes 6148
  4.8 46.8 %all-to-all-start = ((bf16[64,8,256]{2,1,0:T(8,128)(2,1)}), bf16[64,8,256]{2,1,0:T(8,128)(2,1)S(1)}, u32[]{:S(2)}, u32[]{:S(2)}) async-start(bf16[64,8,256]{2,1,0:T(8,128)(2,1)} %fusion), calls=%async_computation | async-start | bytes 524288 | tf_op jit(solution)/shard_map/all_to_all | solution.py:26
  20.4 19.8 %collective-permute-start.2 = (bf16[1936,128]{1,0:T(8,128)(2,1)}, bf16[1936,128]{1,0:T(8,128)(2,1)S(1)}, u32[]{:S(2)}, u32[]{:S(2)}) collective-permute-start(bf16[1936,128]{1,0:T(8,128)(2,1)} %get-tuple-element.19), channel_id=1, source_target_pairs={{0,4},{4,8},{8,12},{12,16},{16,20},{20,24},{24,28},{28,32},{32,36}... | collective-permute-start | bytes 1486856 | tf_op jit(solution)/shard_map/ppermute | solution.py:22
  22.0 18.2 %collective-permute-start.3 = (bf16[1936,128]{1,0:T(8,128)(2,1)}, bf16[1936,128]{1,0:T(8,128)(2,1)S(1)}, u32[]{:S(2)}, u32[]{:S(2)}) collective-permute-start(bf16[1936,128]{1,0:T(8,128)(2,1)} %get-tuple-element.20), channel_id=1, source_target_pairs={{0,252},{4,0},{8,4},{12,8},{16,12},{20,16},{24,20},{28,24},{32,28}... | collective-permute-start | bytes 1486856 | tf_op jit(solution)/shard_map/ppermute | solution.py:22
  26.7 20.4 %collective-permute-start = (bf16[1168,128]{1,0:T(8,128)(2,1)}, bf16[1168,128]{1,0:T(8,128)(2,1)S(1)}, u32[]{:S(2)}, u32[]{:S(2)}) collective-permute-start(bf16[1168,128]{1,0:T(8,128)(2,1)} %get-tuple-element.17), channel_id=1, source_target_pairs={{0,4},{4,8},{8,12},{12,16},{16,20},{20,24},{24,28},{28,32},{32,36}... | collective-permute-start | bytes 897032 | tf_op jit(solution)/shard_map/ppermute | solution.py:22
  26.7 20.4 %collective-permute-start.1 = (bf16[1168,128]{1,0:T(8,128)(2,1)}, bf16[1168,128]{1,0:T(8,128)(2,1)S(1)}, u32[]{:S(2)}, u32[]{:S(2)}) collective-permute-start(bf16[1168,128]{1,0:T(8,128)(2,1)} %get-tuple-element.18), channel_id=1, source_target_pairs={{0,252},{4,0},{8,4},{12,8},{16,12},{20,16},{24,20},{28,24},{32,28}... | collective-permute-start | bytes 897032 | tf_op jit(solution)/shard_map/ppermute | solution.py:22
  53.5 23.7 %all-to-all-start.1 = ((bf16[64,8,512]{2,1,0:T(8,128)(2,1)}), bf16[64,8,512]{2,1,0:T(8,128)(2,1)S(1)}, u32[]{:S(2)}, u32[]{:S(2)}) async-start(bf16[64,8,512]{2,1,0:T(8,128)(2,1)} %bitcast.24), calls=%async_computation.1 | async-start | bytes 1048576 | tf_op jit(solution)/shard_map/all_to_all | solution.py:26
  61.1 37.6 %copy-start.2 = (bf16[128]{0:T(256)(128)(2,1)S(1)}, bf16[128]{0:T(256)(128)(2,1)}, u32[]{:S(2)}) copy-start(bf16[128]{0:T(256)(128)(2,1)} %param.11) | copy-start | bytes 772
  77.7 7.8 %collective-permute-start.4 = (bf16[128,512]{1,0:T(8,128)(2,1)S(1)}, bf16[128,512]{1,0:T(8,128)(2,1)S(1)}, u32[]{:S(2)}, u32[]{:S(2)}) collective-permute-start(bf16[128,512]{1,0:T(8,128)(2,1)S(1)} %get-tuple-element.30), channel_id=1, source_target_pairs={{0,0},{1,64},{2,128},{3,192},{32,32},{33,96},{34,160},{35,224},{64... | collective-permute-start | bytes 393224 | tf_op jit(solution)/shard_map/ppermute | solution.py:302
  80.6 7.4 %collective-permute-start.5 = (bf16[128,512]{1,0:T(8,128)(2,1)S(1)}, bf16[128,512]{1,0:T(8,128)(2,1)S(1)}, u32[]{:S(2)}, u32[]{:S(2)}) collective-permute-start(bf16[128,512]{1,0:T(8,128)(2,1)S(1)} %get-tuple-element.29), channel_id=1, source_target_pairs={{0,32},{1,96},{2,160},{3,224},{32,0},{33,64},{34,128},{35,192},{64... | collective-permute-start | bytes 393224 | tf_op jit(solution)/shard_map/ppermute | solution.py:303
  88.0 10.3 %collective-permute-start.6 = (bf16[256,512]{1,0:T(8,128)(2,1)S(1)}, bf16[256,512]{1,0:T(8,128)(2,1)S(1)}, u32[]{:S(2)}, u32[]{:S(2)}) collective-permute-start(bf16[256,512]{1,0:T(8,128)(2,1)S(1)} %pad_maximum_fusion.1), channel_id=1, source_target_pairs={{0,2},{2,0},{1,3},{3,1},{4,6},{6,4},{5,7},{7,5},{8,10},{10,8},{9,1... | collective-permute-start | bytes 786440 | tf_op jit(solution)/shard_map/ppermute | solution.py:22
  98.4 16.9 %collective-permute-start.7 = (bf16[512,512]{1,0:T(8,128)(2,1)S(1)}, bf16[512,512]{1,0:T(8,128)(2,1)S(1)}, u32[]{:S(2)}, u32[]{:S(2)}) collective-permute-start(bf16[512,512]{1,0:T(8,128)(2,1)S(1)} %pad_maximum_fusion), channel_id=1, source_target_pairs={{0,1},{1,0},{2,3},{3,2},{4,5},{5,4},{6,7},{7,6},{8,9},{9,8},{10,11... | collective-permute-start | bytes 1572872 | tf_op jit(solution)/shard_map/ppermute | solution.py:22
  98.8 5.7 %collective-permute-start.8 = (bf16[128,512]{1,0:T(8,128)(2,1)S(1)}, bf16[128,512]{1,0:T(8,128)(2,1)S(1)}, u32[]{:S(2)}, u32[]{:S(2)}) collective-permute-start(bf16[128,512]{1,0:T(8,128)(2,1)S(1)} %get-tuple-element.35.refs_0_), channel_id=1, source_target_pairs={{0,128},{128,0},{1,129},{129,1},{2,130},{130,2},{3,131},{131,3},{4... | collective-permute-start | bytes 393224 | tf_op jit(solution)/shard_map/ppermute | solution.py:22
  99.2 7.9 %collective-permute-start.10 = (bf16[128,512]{1,0:T(8,128)(2,1)S(1)}, bf16[128,512]{1,0:T(8,128)(2,1)S(1)}, u32[]{:S(2)}, u32[]{:S(2)}) collective-permute-start(bf16[128,512]{1,0:T(8,128)(2,1)S(1)} %get-tuple-element.35.refs_0_), channel_id=1, source_target_pairs={{0,64},{32,96},{64,0},{96,32},{1,65},{33,97},{65,1},{97,33},{2,66}... | collective-permute-start | bytes 393224 | tf_op jit(solution)/shard_map/ppermute | solution.py:22
  99.3 8.3 %collective-permute-start.11 = (bf16[128,512]{1,0:T(8,128)(2,1)S(1)}, bf16[128,512]{1,0:T(8,128)(2,1)S(1)}, u32[]{:S(2)}, u32[]{:S(2)}) collective-permute-start(bf16[128,512]{1,0:T(8,128)(2,1)S(1)} %get-tuple-element.35.refs_0_), channel_id=1, source_target_pairs={{0,96},{32,0},{64,32},{96,64},{1,97},{33,1},{65,33},{97,65},{2,98}... | collective-permute-start | bytes 393224 | tf_op jit(solution)/shard_map/ppermute | solution.py:22
  102.9 8.0 %collective-permute-start.9 = (bf16[128,512]{1,0:T(8,128)(2,1)S(1)}, bf16[128,512]{1,0:T(8,128)(2,1)S(1)}, u32[]{:S(2)}, u32[]{:S(2)}) collective-permute-start(bf16[128,512]{1,0:T(8,128)(2,1)S(1)} %get-tuple-element.35.refs_0_), channel_id=1, source_target_pairs={{0,32},{32,64},{64,96},{96,0},{1,33},{33,65},{65,97},{97,1},{2,34}... | collective-permute-start | bytes 393224 | tf_op jit(solution)/shard_map/ppermute | solution.py:22
  104.6 10.7 %collective-permute-start.12 = (bf16[128,512]{1,0:T(8,128)(2,1)S(1)}, bf16[128,512]{1,0:T(8,128)(2,1)S(1)}, u32[]{:S(2)}, u32[]{:S(2)}) collective-permute-start(bf16[128,512]{1,0:T(8,128)(2,1)S(1)} %collective-permute-done.8.refs_1_), channel_id=1, source_target_pairs={{0,32},{32,64},{64,96},{96,0},{1,33},{33,65},{65,97},{97,1},{2,34}... | collective-permute-start | bytes 393224 | tf_op jit(solution)/shard_map/ppermute | solution.py:22
  107.1 8.2 %collective-permute-start.13 = (bf16[128,512]{1,0:T(8,128)(2,1)S(1)}, bf16[128,512]{1,0:T(8,128)(2,1)S(1)}, u32[]{:S(2)}, u32[]{:S(2)}) collective-permute-start(bf16[128,512]{1,0:T(8,128)(2,1)S(1)} %collective-permute-done.8.refs_1_), channel_id=1, source_target_pairs={{0,64},{32,96},{64,0},{96,32},{1,65},{33,97},{65,1},{97,33},{2,66}... | collective-permute-start | bytes 393224 | tf_op jit(solution)/shard_map/ppermute | solution.py:22
  107.6 7.6 %collective-permute-start.14 = (bf16[128,512]{1,0:T(8,128)(2,1)S(1)}, bf16[128,512]{1,0:T(8,128)(2,1)S(1)}, u32[]{:S(2)}, u32[]{:S(2)}) collective-permute-start(bf16[128,512]{1,0:T(8,128)(2,1)S(1)} %collective-permute-done.8.refs_1_), channel_id=1, source_target_pairs={{0,96},{32,0},{64,32},{96,64},{1,97},{33,1},{65,33},{97,65},{2,98}... | collective-permute-start | bytes 393224 | tf_op jit(solution)/shard_map/ppermute | solution.py:22
  117.7 42.0 %all-to-all-start.2 = ((bf16[8,64,512]{2,1,0:T(8,128)(2,1)}), bf16[8,64,512]{2,1,0:T(8,128)(2,1)S(1)}, u32[]{:S(2)}, u32[]{:S(2)}) async-start(bf16[8,64,512]{2,1,0:T(8,128)(2,1)} %bitcast.26), calls=%async_computation.2 | async-start | bytes 1048576 | tf_op jit(solution)/shard_map/all_to_all | solution.py:26
  121.2 6.5 %collective-permute-start.15 = (bf16[128,512]{1,0:T(8,128)(2,1)S(1)}, bf16[128,512]{1,0:T(8,128)(2,1)S(1)}, u32[]{:S(2)}, u32[]{:S(2)}) collective-permute-start(bf16[128,512]{1,0:T(8,128)(2,1)S(1)} %get-tuple-element.36.refs_0_), channel_id=1, source_target_pairs={{0,128},{128,0},{1,129},{129,1},{2,130},{130,2},{3,131},{131,3},{4... | collective-permute-start | bytes 393224 | tf_op jit(solution)/shard_map/ppermute | solution.py:22
  123.0 8.0 %collective-permute-start.16 = (bf16[128,512]{1,0:T(8,128)(2,1)S(1)}, bf16[128,512]{1,0:T(8,128)(2,1)S(1)}, u32[]{:S(2)}, u32[]{:S(2)}) collective-permute-start(bf16[128,512]{1,0:T(8,128)(2,1)S(1)} %get-tuple-element.36.refs_0_), channel_id=1, source_target_pairs={{0,32},{32,64},{64,96},{96,0},{1,33},{33,65},{65,97},{97,1},{2,34}... | collective-permute-start | bytes 393224 | tf_op jit(solution)/shard_map/ppermute | solution.py:22
  124.4 9.5 %collective-permute-start.17 = (bf16[128,512]{1,0:T(8,128)(2,1)S(1)}, bf16[128,512]{1,0:T(8,128)(2,1)S(1)}, u32[]{:S(2)}, u32[]{:S(2)}) collective-permute-start(bf16[128,512]{1,0:T(8,128)(2,1)S(1)} %get-tuple-element.36.refs_0_), channel_id=1, source_target_pairs={{0,64},{32,96},{64,0},{96,32},{1,65},{33,97},{65,1},{97,33},{2,66}... | collective-permute-start | bytes 393224 | tf_op jit(solution)/shard_map/ppermute | solution.py:22
  126.7 7.2 %collective-permute-start.18 = (bf16[128,512]{1,0:T(8,128)(2,1)S(1)}, bf16[128,512]{1,0:T(8,128)(2,1)S(1)}, u32[]{:S(2)}, u32[]{:S(2)}) collective-permute-start(bf16[128,512]{1,0:T(8,128)(2,1)S(1)} %get-tuple-element.36.refs_0_), channel_id=1, source_target_pairs={{0,96},{32,0},{64,32},{96,64},{1,97},{33,1},{65,33},{97,65},{2,98}... | collective-permute-start | bytes 393224 | tf_op jit(solution)/shard_map/ppermute | solution.py:22
  127.7 8.5 %collective-permute-start.19 = (bf16[128,512]{1,0:T(8,128)(2,1)S(1)}, bf16[128,512]{1,0:T(8,128)(2,1)S(1)}, u32[]{:S(2)}, u32[]{:S(2)}) collective-permute-start(bf16[128,512]{1,0:T(8,128)(2,1)S(1)} %collective-permute-done.15.refs_1_), channel_id=1, source_target_pairs={{0,32},{32,64},{64,96},{96,0},{1,33},{33,65},{65,97},{97,1},{2,34}... | collective-permute-start | bytes 393224 | tf_op jit(solution)/shard_map/ppermute | solution.py:22
  128.8 9.0 %collective-permute-start.20 = (bf16[128,512]{1,0:T(8,128)(2,1)S(1)}, bf16[128,512]{1,0:T(8,128)(2,1)S(1)}, u32[]{:S(2)}, u32[]{:S(2)}) collective-permute-start(bf16[128,512]{1,0:T(8,128)(2,1)S(1)} %collective-permute-done.15.refs_1_), channel_id=1, source_target_pairs={{0,64},{32,96},{64,0},{96,32},{1,65},{33,97},{65,1},{97,33},{2,66}... | collective-permute-start | bytes 393224 | tf_op jit(solution)/shard_map/ppermute | solution.py:22
  131.0 6.7 %collective-permute-start.21 = (bf16[128,512]{1,0:T(8,128)(2,1)S(1)}, bf16[128,512]{1,0:T(8,128)(2,1)S(1)}, u32[]{:S(2)}, u32[]{:S(2)}) collective-permute-start(bf16[128,512]{1,0:T(8,128)(2,1)S(1)} %collective-permute-done.15.refs_1_), channel_id=1, source_target_pairs={{0,96},{32,0},{64,32},{96,64},{1,97},{33,1},{65,33},{97,65},{2,98}... | collective-permute-start | bytes 393224 | tf_op jit(solution)/shard_map/ppermute | solution.py:22
  139.4 14.8 %collective-permute-start.22 = (bf16[64,512]{1,0:T(8,128)(2,1)S(1)}, bf16[64,512]{1,0:T(8,128)(2,1)S(1)}, u32[]{:S(2)}, u32[]{:S(2)}) collective-permute-start(bf16[64,512]{1,0:T(8,128)(2,1)S(1)} %get-tuple-element.22), channel_id=1, source_target_pairs={{0,16},{4,20},{8,24},{12,28},{16,0},{20,4},{24,8},{28,12},{1,17},{... | collective-permute-start | bytes 196616 | tf_op jit(solution)/shard_map/ppermute | solution.py:22
  145.0 9.9 %collective-permute-start.23 = (bf16[64,512]{1,0:T(8,128)(2,1)S(1)}, bf16[64,512]{1,0:T(8,128)(2,1)S(1)}, u32[]{:S(2)}, u32[]{:S(2)}) collective-permute-start(bf16[64,512]{1,0:T(8,128)(2,1)S(1)} %get-tuple-element.23), channel_id=1, source_target_pairs={{0,12},{4,16},{8,20},{12,24},{16,28},{20,0},{24,4},{28,8},{1,13},{... | collective-permute-start | bytes 196616 | tf_op jit(solution)/shard_map/ppermute | solution.py:22
  145.6 11.8 %collective-permute-start.24 = (bf16[64,512]{1,0:T(8,128)(2,1)S(1)}, bf16[64,512]{1,0:T(8,128)(2,1)S(1)}, u32[]{:S(2)}, u32[]{:S(2)}) collective-permute-start(bf16[64,512]{1,0:T(8,128)(2,1)S(1)} %get-tuple-element.24), channel_id=1, source_target_pairs={{0,20},{4,24},{8,28},{12,0},{16,4},{20,8},{24,12},{28,16},{1,21},{... | collective-permute-start | bytes 196616 | tf_op jit(solution)/shard_map/ppermute | solution.py:22
  150.1 7.4 %collective-permute-start.25 = (bf16[64,512]{1,0:T(8,128)(2,1)S(1)}, bf16[64,512]{1,0:T(8,128)(2,1)S(1)}, u32[]{:S(2)}, u32[]{:S(2)}) collective-permute-start(bf16[64,512]{1,0:T(8,128)(2,1)S(1)} %get-tuple-element.25), channel_id=1, source_target_pairs={{0,8},{4,12},{8,16},{12,20},{16,24},{20,28},{24,0},{28,4},{1,9},{5... | collective-permute-start | bytes 196616 | tf_op jit(solution)/shard_map/ppermute | solution.py:22
  150.7 6.8 %collective-permute-start.26 = (bf16[64,512]{1,0:T(8,128)(2,1)S(1)}, bf16[64,512]{1,0:T(8,128)(2,1)S(1)}, u32[]{:S(2)}, u32[]{:S(2)}) collective-permute-start(bf16[64,512]{1,0:T(8,128)(2,1)S(1)} %get-tuple-element.26), channel_id=1, source_target_pairs={{0,24},{4,28},{8,0},{12,4},{16,8},{20,12},{24,16},{28,20},{1,25},{... | collective-permute-start | bytes 196616 | tf_op jit(solution)/shard_map/ppermute | solution.py:22
  154.2 5.5 %collective-permute-start.27 = (bf16[64,512]{1,0:T(8,128)(2,1)S(1)}, bf16[64,512]{1,0:T(8,128)(2,1)S(1)}, u32[]{:S(2)}, u32[]{:S(2)}) collective-permute-start(bf16[64,512]{1,0:T(8,128)(2,1)S(1)} %get-tuple-element.27), channel_id=1, source_target_pairs={{0,4},{4,8},{8,12},{12,16},{16,20},{20,24},{24,28},{28,0},{1,5},{5... | collective-permute-start | bytes 196616 | tf_op jit(solution)/shard_map/ppermute | solution.py:22
  154.9 4.8 %collective-permute-start.28 = (bf16[64,512]{1,0:T(8,128)(2,1)S(1)}, bf16[64,512]{1,0:T(8,128)(2,1)S(1)}, u32[]{:S(2)}, u32[]{:S(2)}) collective-permute-start(bf16[64,512]{1,0:T(8,128)(2,1)S(1)} %get-tuple-element.28), channel_id=1, source_target_pairs={{0,28},{4,0},{8,4},{12,8},{16,12},{20,16},{24,20},{28,24},{1,29},{... | collective-permute-start | bytes 196616 | tf_op jit(solution)/shard_map/ppermute | solution.py:22

commit v3 on v2

--- a/solution.py
+++ b/solution.py
@@ -194,16 +194,13 @@
     )(rows, sampled, sampled)
 
 
-def gram_body(apart, place_ref, same_ref, cross_ref, across_ref, other_ref, *refs):
-    cols, outs, scratch = refs[:8], refs[8:-3], refs[-3:]
+def gram_body(apart, place_ref, *refs):
+    rows, cols, outs, scratch = refs[:8], refs[8:16], refs[16:-3], refs[-3:]
     rows_ref, cols_ref, sum_ref = scratch
-    block = same_ref.shape[0]
-    parts = [same_ref[...], cross_ref[...]]
-    for ref in (across_ref, other_ref):
-        parts += [ref[s : s + block] for s in range(0, ref.shape[0], block)]
-    for k, part in enumerate(parts):
+    block = rows[0].shape[0]
+    for k, ref in enumerate(rows):
         at = pl.multiple_of(place_ref[k] * block, block)
-        rows_ref[:, pl.ds(at, block)] = part.T
+        rows_ref[:, pl.ds(at, block)] = ref[...].T
     for k, ref in enumerate(cols):
         at = pl.multiple_of(place_ref[8 + k] * block, block)
         cols_ref[pl.ds(at, block), :] = ref[...]
@@ -221,9 +218,9 @@
         out_ref[...] = sum_ref[pl.ds(at, size), :].astype(out_ref.dtype)
 
 
-def gram_tile(place, same, cross, across, other, cols, apart):
+def gram_tile(place, pieces, cols, apart):
     obs, width = cols[0].shape
-    rows = same.shape[1]
+    rows = pieces[0].shape[1]
     if apart:
         size = (rows // apart, width)
         shapes = [jax.ShapeDtypeStruct(size, jnp.float32)]
@@ -233,7 +230,7 @@
     whole = pl.BlockSpec(memory_space=pltpu.VMEM)
     return pl.pallas_call(
         functools.partial(gram_body, apart),
-        in_specs=[pl.BlockSpec(memory_space=pltpu.SMEM)] + [whole] * (4 + len(cols)),
+        in_specs=[pl.BlockSpec(memory_space=pltpu.SMEM)] + [whole] * (len(pieces) + len(cols)),
         out_specs=[whole] * len(shapes),
         out_shape=shapes,
         scratch_shapes=[
@@ -243,7 +240,7 @@
         ],
         compiler_params=pltpu.CompilerParams(vmem_limit_bytes=GRANT),
         name="gram",
-    )(place, same, cross, across, other, *cols)
+    )(place, *pieces, *cols)
 
 
 def on_device(pulses, wind_x, wind_y, obs_tile, obs_weight, obs_precision):
@@ -297,21 +294,30 @@
     here = lax.axis_index(XY)
     odd = here % 2
     pairs = [(i // peers, i % peers) for i in range(group * peers)]
-    to_same = [(a * peers + q, (2 * q + a % 2) * peers + a // 2) for a, q in pairs]
-    to_cross = [(a * peers + q, (2 * q + 1 - a % 2) * peers + a // 2) for a, q in pairs]
-    same = lax.ppermute(jnp.where(odd == 0, low, high), PLANE, to_same)
-    cross = lax.ppermute(jnp.where(odd == 0, high, low), PLANE, to_cross)
-    across = shifted(jnp.concatenate([same, cross], axis=0), "xh", 1)
-    other = shifted(jnp.concatenate([same, cross, across], axis=0), "core", 1)
+    mine = jnp.where(odd == 0, low, high), jnp.where(odd == 0, high, low)
+    pieces = []
+    for flip in (0, 2):
+        for s, value in enumerate(mine):
+            path = [
+                (a * peers + q, (2 * q + (a % 2 ^ s)) * peers + (a // 2 ^ flip)) for a, q in pairs
+            ]
+            pieces.append(lax.ppermute(value, PLANE, path))
+    for k in range(4):
+        pieces.append(shifted(pieces[k], "core", 1))
 
     deep = lax.axis_size("y")
     cols = []
     for part, value in enumerate(weighted):
         beside = shifted(value, "xl", 1)
         cols.append([value, beside])
-        for source in (value, beside):
-            for d in range(1, deep):
-                cols[part].append(shifted(source, "y", d))
+        for d in range(1, deep):
+            cols[part].append(shifted(value, "y", d))
+        for d in range(1, deep):
+            if part == 0:
+                cols[part].append(shifted(beside, "y", d))
+            else:
+                path = [(k, (1 - k // deep) * deep + (k + d) % deep) for k in range(group)]
+                cols[part].append(lax.ppermute(value, XY, path))
     xl, y = lax.axis_index("xl"), lax.axis_index("y")
     owners = [here, (1 - xl) * deep + y]
     owners += [xl * deep + (y - d) % deep for d in range(1, deep)]
@@ -321,10 +327,10 @@
     place = jnp.stack(row_owners + owners + [lax.axis_index("z")]).astype(jnp.int32)
 
     depth = lax.axis_size("z")
-    tile = gram_tile(place, same, cross, across, other, cols[0], 0)[0]
+    tile = gram_tile(place, pieces, cols[0], 0)[0]
     parts = exchanged(tile.reshape(depth, half // depth, half), "z")
     total = jnp.sum(parts.astype(jnp.float32), axis=0)
-    blocks = gram_tile(place, same, cross, across, other, cols[1], depth)
+    blocks = gram_tile(place, pieces, cols[1], depth)
     last = blocks[0]
     for d in (4, 3, 5, 2, 6, 1, 7):
         last = last + shifted(blocks[d], "z", d).astype(jnp.float32)

time: 161 us -> 153 us (0.950); the launches traced: 161 us -> 151 us
  waiting for transfers between devices: 56 us -> 39.6 us
  starting transfers between devices: 77.7 us -> 84.3 us
    ppermute x27 -> x26, waiting for transfers between devices: 33.8 us -> 20.6 us  [shifted(): lax.ppermute(value, axis, [(i, (i + steps) % count) for i in range(count)])]
    ppermute x2 -> x7, starting transfers between devices: 4.08 us -> 11.2 us  [the longest x4 6.33 us: on_device(): pieces.append(lax.ppermute(value, PLANE, path))]
    ppermute x2 -> x7, waiting for transfers between devices: 6.19 us -> 3.06 us  [the longest x4 1.95 us: on_device(): pieces.append(lax.ppermute(value, PLANE, path))]
    ppermute x27 -> x26, starting transfers between devices: 49.8 us -> 49.2 us  [shifted(): lax.ppermute(value, axis, [(i, (i + steps) % count) for i in range(count)])]
  transfers between devices with their start and end apart: 32 -> 36, of which waited for: 14 -> 11; matrix products, arithmetic and copies ran while one was open for 0% -> 0% of each run, Pallas kernels for 10% -> 11%
where the time goes in v3:
time: 153 us; the launch traced here: 151 us
  starting transfers between devices  84.3 us (55%)
  waiting for transfers between devices  39.6 us (26%)
  Pallas kernels  20.2 us (13%)
  other arithmetic  4.67 us (3%)
  matrix products  1.61 us (1%)
    ppermute x26, starting transfers between devices, shifted(): lax.ppermute(value, axis, [(i, (i + steps) % count) for i in range(count)])  49.2 us
    all_to_all x3, starting transfers between devices, exchanged(): return lax.all_to_all(value, axis, split_axis=0, concat_axis=0, tiled=True)  23.9 us
    ppermute x26, waiting for transfers between devices, shifted(): lax.ppermute(value, axis, [(i, (i + steps) % count) for i in range(count)])  20.6 us
    all_to_all x3, waiting for transfers between devices, exchanged(): return lax.all_to_all(value, axis, split_axis=0, concat_axis=0, tiled=True)  16 us
    pallas_call x2, Pallas kernels, transport(): pl.pallas_call(functools.partial(transport_body, skip), grid=(steps,), in...  11.4 us
    ppermute x4, starting transfers between devices, on_device(): pieces.append(lax.ppermute(value, PLANE, path))  6.33 us
    ppermute x3, starting transfers between devices, on_device(): cols[part].append(lax.ppermute(value, XY, path))  4.88 us
    pallas_call x2, Pallas kernels, gram_tile(): pl.pallas_call(functools.partial(gram_body, apart), in_specs=[pl.BlockSpe...  4.12 us
  transfers between devices with their start and end apart: 36, of which 11 were waited for; matrix products, arithmetic and copies ran while one was open for 0% of the time, Pallas kernels for 11%

profile of v3, /device:TPU:4, one launch (start us, length us, event | category | flops | bytes accessed | tf_op | source)
XLA Modules:
  0.0 150.7 jit_solution(16031869413452349326)
XLA Ops:
  0.0 0.9 convert_reduce_fusion.2
  0.9 0.7 fusion.15
  1.6 1.0 convert_reduce_fusion.1
  2.6 1.0 fusion.8
  3.6 0.1 iota_compare_fusion
  3.8 1.1 fusion
  4.8 12.7 %all-to-all-start = ((bf16[64,8,256]{2,1,0:T(8,128)(2,1)}), bf16[64,8,256]{2,1,0:T(8,128)(2,1)S(1)}, u32[]{:S(2)}, u32[]{:S(2)}) async-start(bf16[64,8,256]{2,1,0:T(8,128)(2,1)} %fusion), calls=%async_computation | async-start | bytes 524288 | tf_op jit(solution)/shard_map/all_to_all | solution.py:26
  17.6 2.9 %edges.1 = (bf16[1936,128]{1,0:T(8,128)(2,1)}, bf16[1936,128]{1,0:T(8,128)(2,1)}, bf16[1168,128]{1,0:T(8,128)(2,1)}, bf16[1168,128]{1,0:T(8,128)(2,1)}) custom-call(f32[4096,128]{1,0:T(8,128)} %bitcast.42, f32[4,128]{1,0:T(4,128)} %wind_x_ref.5, f32[4,128]{1,0:T(4,128)} %wind_y_ref.5), custom_call_target="tpu_custom_call" | custom-call | tf_op jit(solution)/shard_map/edges/pallas_call | solution.py:53
  20.4 1.6 %collective-permute-start.2 = (bf16[1936,128]{1,0:T(8,128)(2,1)}, bf16[1936,128]{1,0:T(8,128)(2,1)S(1)}, u32[]{:S(2)}, u32[]{:S(2)}) collective-permute-start(bf16[1936,128]{1,0:T(8,128)(2,1)} %get-tuple-element.19), channel_id=1, source_target_pairs={{0,4},{4,8},{8,12},{12,16},{16,20},{20,24},{24,28},{28,32},{32,36}... | collective-permute-start | bytes 1486856 | tf_op jit(solution)/shard_map/ppermute | solution.py:22
  22.0 4.7 %collective-permute-start.3 = (bf16[1936,128]{1,0:T(8,128)(2,1)}, bf16[1936,128]{1,0:T(8,128)(2,1)S(1)}, u32[]{:S(2)}, u32[]{:S(2)}) collective-permute-start(bf16[1936,128]{1,0:T(8,128)(2,1)} %get-tuple-element.20), channel_id=1, source_target_pairs={{0,252},{4,0},{8,4},{12,8},{16,12},{20,16},{24,20},{28,24},{32,28}... | collective-permute-start | bytes 1486856 | tf_op jit(solution)/shard_map/ppermute | solution.py:22
  26.7 0.0 collective-permute-start
  26.7 6.2 %collective-permute-start.1 = (bf16[1168,128]{1,0:T(8,128)(2,1)}, bf16[1168,128]{1,0:T(8,128)(2,1)S(1)}, u32[]{:S(2)}, u32[]{:S(2)}) collective-permute-start(bf16[1168,128]{1,0:T(8,128)(2,1)} %get-tuple-element.18), channel_id=1, source_target_pairs={{0,252},{4,0},{8,4},{12,8},{16,12},{20,16},{24,20},{28,24},{32,28}... | collective-permute-start | bytes 897032 | tf_op jit(solution)/shard_map/ppermute | solution.py:22
  32.9 7.3 %collective-permute-done.2.a0.a1.a2.a_winds = bf16[1936,128]{1,0:T(8,128)(2,1)S(1)} collective-permute-done((bf16[1936,128]{1,0:T(8,128)(2,1)}, bf16[1936,128]{1,0:T(8,128)(2,1)S(1)}, u32[]{:S(2)}, u32[]{:S(2)}) %collective-permute-start.2) | collective-permute-done | bytes 495648 | tf_op jit(solution)/shard_map/ppermute | solution.py:22
  40.2 6.9 %transport.2.refs_0_ = bf16[1024,512]{1,0:T(8,128)(2,1)S(1)} custom-call(f32[4096,128]{1,0:T(8,128)} %bitcast.43, bf16[1936,128]{1,0:T(8,128)(2,1)S(1)} %collective-permute-done.2.a0.a1.a2.a_winds, bf16[1936,128]{1,0:T(8,128)(2,1)S(1)} %collective-permute-done.2.a0.a1.a2.a_winds, bf16[1936,128]{1,0:T(8,128)(2,1)S(1)} %collective-permute-done.2.a0.a1.a2.a_winds, ...), custom_call_target="tpu_custom_call" | custom-call | tf_op jit(solution)/shard_map/transport/pallas_call | solution.py:140
  47.1 4.5 %transport.3.low_ref.high_ref = bf16[1024,512]{1,0:T(8,128)(2,1)S(1)} custom-call(f32[4096,128]{1,0:T(8,128)} %bitcast.44, bf16[1168,128]{1,0:T(8,128)(2,1)S(1)} %collective-permute-done.a0.a1.a2.a_winds, bf16[1168,128]{1,0:T(8,128)(2,1)S(1)} %collective-permute-done.a0.a1.a2.a_winds, ...), custom_call_target="tpu_custom_call", output_to_operand_aliasing={{}: (11, {})} | custom-call | tf_op jit(solution)/shard_map/transport/pallas_call | solution.py:140
  51.6 0.0 copy-start.2
  51.7 1.8 %jacobian.1 = bf16[512,512]{1,0:T(8,128)(2,1)} custom-call(bf16[512,256]{1,0:T(8,128)(2,1)S(1)} %bitcast.41, bf16[1024,512]{1,0:T(8,128)(2,1)S(1)} %transport.3.low_ref.high_ref, bf16[1024,512]{1,0:T(8,128)(2,1)S(1)} %transport.3.low_ref.high_ref), custom_call_target="tpu_custom_call" | custom-call | tf_op jit(solution)/shard_map/jacobian/pallas_call | solution.py:181
  53.5 7.7 %all-to-all-start.1 = ((bf16[64,8,512]{2,1,0:T(8,128)(2,1)}), bf16[64,8,512]{2,1,0:T(8,128)(2,1)S(1)}, u32[]{:S(2)}, u32[]{:S(2)}) async-start(bf16[64,8,512]{2,1,0:T(8,128)(2,1)} %bitcast.24), calls=%async_computation.1 | async-start | bytes 1048576 | tf_op jit(solution)/shard_map/all_to_all | solution.py:26
  61.2 16.0 %all-to-all-done.1 = bf16[64,8,512]{2,1,0:T(8,128)(2,1)S(1)} async-done(((bf16[64,8,512]{2,1,0:T(8,128)(2,1)}), bf16[64,8,512]{2,1,0:T(8,128)(2,1)S(1)}, u32[]{:S(2)}, u32[]{:S(2)}) %all-to-all-start.1) | async-done | bytes 524320 | tf_op jit(solution)/shard_map/all_to_all | solution.py:26
  77.2 0.3 fusion.3
  77.4 0.3 broadcast_select_fusion
  77.7 0.1 multiply_convert_fusion.1
  77.8 1.9 %collective-permute-start.12 = (bf16[128,512]{1,0:T(8,128)(2,1)S(1)}, bf16[128,512]{1,0:T(8,128)(2,1)S(1)}, u32[]{:S(2)}, u32[]{:S(2)}) collective-permute-start(bf16[128,512]{1,0:T(8,128)(2,1)S(1)} %get-tuple-element.35.refs_8_), channel_id=1, source_target_pairs={{0,128},{128,0},{1,129},{129,1},{2,130},{130,2},{3,131},{131,3},{4... | collective-permute-start | bytes 393224 | tf_op jit(solution)/shard_map/ppermute | solution.py:22
  79.7 0.5 collective-permute-start.13
  80.2 1.6 %collective-permute-start.14 = (bf16[128,512]{1,0:T(8,128)(2,1)S(1)}, bf16[128,512]{1,0:T(8,128)(2,1)S(1)}, u32[]{:S(2)}, u32[]{:S(2)}) collective-permute-start(bf16[128,512]{1,0:T(8,128)(2,1)S(1)} %get-tuple-element.35.refs_8_), channel_id=1, source_target_pairs={{0,64},{32,96},{64,0},{96,32},{1,65},{33,97},{65,1},{97,33},{2,66}... | collective-permute-start | bytes 393224 | tf_op jit(solution)/shard_map/ppermute | solution.py:22
  81.8 1.1 collective-permute-start.15
  82.9 1.2 collective-permute-start.6
  84.1 2.4 %collective-permute-start.7 = (bf16[128,512]{1,0:T(8,128)(2,1)S(1)}, bf16[128,512]{1,0:T(8,128)(2,1)S(1)}, u32[]{:S(2)}, u32[]{:S(2)}) collective-permute-start(bf16[128,512]{1,0:T(8,128)(2,1)S(1)} %get-tuple-element.29), channel_id=1, source_target_pairs={{0,34},{1,98},{2,162},{3,226},{32,2},{33,66},{34,130},{35,194},{64... | collective-permute-start | bytes 393224 | tf_op jit(solution)/shard_map/ppermute | solution.py:304
  86.5 2.8 %collective-permute-start.4 = (bf16[128,512]{1,0:T(8,128)(2,1)S(1)}, bf16[128,512]{1,0:T(8,128)(2,1)S(1)}, u32[]{:S(2)}, u32[]{:S(2)}) collective-permute-start(bf16[128,512]{1,0:T(8,128)(2,1)S(1)} %get-tuple-element.30), channel_id=1, source_target_pairs={{0,0},{1,64},{2,128},{3,192},{32,32},{33,96},{34,160},{35,224},{64... | collective-permute-start | bytes 393224 | tf_op jit(solution)/shard_map/ppermute | solution.py:304
  89.3 1.6 %collective-permute-done.14.refs_11_ = bf16[128,512]{1,0:T(8,128)(2,1)S(1)} collective-permute-done((bf16[128,512]{1,0:T(8,128)(2,1)S(1)}, bf16[128,512]{1,0:T(8,128)(2,1)S(1)}, u32[]{:S(2)}, u32[]{:S(2)}) %collective-permute-start.14) | collective-permute-done | bytes 131104 | tf_op jit(solution)/shard_map/ppermute | solution.py:22
  90.9 2.4 %collective-permute-start.16 = (bf16[128,512]{1,0:T(8,128)(2,1)S(1)}, bf16[128,512]{1,0:T(8,128)(2,1)S(1)}, u32[]{:S(2)}, u32[]{:S(2)}) collective-permute-start(bf16[128,512]{1,0:T(8,128)(2,1)S(1)} %collective-permute-done.12.refs_9_), channel_id=1, source_target_pairs={{0,32},{32,64},{64,96},{96,0},{1,33},{33,65},{65,97},{97,1},{2,34}... | collective-permute-start | bytes 393224 | tf_op jit(solution)/shard_map/ppermute | solution.py:22
  93.3 1.9 %collective-permute-start.17 = (bf16[128,512]{1,0:T(8,128)(2,1)S(1)}, bf16[128,512]{1,0:T(8,128)(2,1)S(1)}, u32[]{:S(2)}, u32[]{:S(2)}) collective-permute-start(bf16[128,512]{1,0:T(8,128)(2,1)S(1)} %collective-permute-done.12.refs_9_), channel_id=1, source_target_pairs={{0,64},{32,96},{64,0},{96,32},{1,65},{33,97},{65,1},{97,33},{2,66}... | collective-permute-start | bytes 393224 | tf_op jit(solution)/shard_map/ppermute | solution.py:22
  95.2 2.3 %collective-permute-start.18 = (bf16[128,512]{1,0:T(8,128)(2,1)S(1)}, bf16[128,512]{1,0:T(8,128)(2,1)S(1)}, u32[]{:S(2)}, u32[]{:S(2)}) collective-permute-start(bf16[128,512]{1,0:T(8,128)(2,1)S(1)} %collective-permute-done.12.refs_9_), channel_id=1, source_target_pairs={{0,96},{32,0},{64,32},{96,64},{1,97},{33,1},{65,33},{97,65},{2,98}... | collective-permute-start | bytes 393224 | tf_op jit(solution)/shard_map/ppermute | solution.py:22
  97.5 1.9 %collective-permute-done.5.refs_1_ = bf16[128,512]{1,0:T(8,128)(2,1)S(1)} collective-permute-done((bf16[128,512]{1,0:T(8,128)(2,1)S(1)}, bf16[128,512]{1,0:T(8,128)(2,1)S(1)}, u32[]{:S(2)}, u32[]{:S(2)}) %collective-permute-start.5) | collective-permute-done | bytes 131104 | tf_op jit(solution)/shard_map/ppermute | solution.py:304
  99.5 2.0 %collective-permute-done.16.refs_13_ = bf16[128,512]{1,0:T(8,128)(2,1)S(1)} collective-permute-done((bf16[128,512]{1,0:T(8,128)(2,1)S(1)}, bf16[128,512]{1,0:T(8,128)(2,1)S(1)}, u32[]{:S(2)}, u32[]{:S(2)}) %collective-permute-start.16) | collective-permute-done | bytes 131104 | tf_op jit(solution)/shard_map/ppermute | solution.py:22
  101.4 1.0 collective-permute-start.8
  102.5 0.0 collective-permute-start.9
  102.5 0.1 stack.71.place_ref
  102.6 0.6 collective-permute-done.18.refs_15_
  103.2 0.3 collective-permute-done.8.refs_4_
  103.5 0.4 collective-permute-done.9.refs_5_
  103.8 2.4 %gram.2 = bf16[512,512]{1,0:T(8,128)(2,1)} custom-call(s32[17]{0:T(128)S(1)} %stack.71.place_ref, bf16[128,512]{1,0:T(8,128)(2,1)S(1)} %collective-permute-done.4.refs_0_, bf16[128,512]{1,0:T(8,128)(2,1)S(1)} %collective-permute-done.5.refs_1_, bf16[128,512]{1,0:T(8,128)(2,1)S(1)} %collective-permute-done.6.refs_2_, ...), custom_call_target="tpu_custom_call" | custom-call | tf_op jit(solution)/shard_map/gram/pallas_call | solution.py:231
  106.3 3.5 %all-to-all-start.2 = ((bf16[8,64,512]{2,1,0:T(8,128)(2,1)}), bf16[8,64,512]{2,1,0:T(8,128)(2,1)S(1)}, u32[]{:S(2)}, u32[]{:S(2)}) async-start(bf16[8,64,512]{2,1,0:T(8,128)(2,1)} %bitcast.26), calls=%async_computation.2 | async-start | bytes 1048576 | tf_op jit(solution)/shard_map/all_to_all | solution.py:26
  109.8 0.6 collective-permute-start.19
  110.4 1.0 collective-permute-start.20
  111.3 2.7 %collective-permute-start.21 = (bf16[128,512]{1,0:T(8,128)(2,1)S(1)}, bf16[128,512]{1,0:T(8,128)(2,1)S(1)}, u32[]{:S(2)}, u32[]{:S(2)}) collective-permute-start(bf16[128,512]{1,0:T(8,128)(2,1)S(1)} %get-tuple-element.36.refs_8_), channel_id=1, source_target_pairs={{0,64},{32,96},{64,0},{96,32},{1,65},{33,97},{65,1},{97,33},{2,66}... | collective-permute-start | bytes 393224 | tf_op jit(solution)/shard_map/ppermute | solution.py:22
  114.1 2.0 %collective-permute-start.22 = (bf16[128,512]{1,0:T(8,128)(2,1)S(1)}, bf16[128,512]{1,0:T(8,128)(2,1)S(1)}, u32[]{:S(2)}, u32[]{:S(2)}) collective-permute-start(bf16[128,512]{1,0:T(8,128)(2,1)S(1)} %get-tuple-element.36.refs_8_), channel_id=1, source_target_pairs={{0,96},{32,0},{64,32},{96,64},{1,97},{33,1},{65,33},{97,65},{2,98}... | collective-permute-start | bytes 393224 | tf_op jit(solution)/shard_map/ppermute | solution.py:22
  116.1 1.3 collective-permute-start.23
  117.5 1.2 collective-permute-start.24
  118.7 2.3 %collective-permute-start.25 = (bf16[128,512]{1,0:T(8,128)(2,1)S(1)}, bf16[128,512]{1,0:T(8,128)(2,1)S(1)}, u32[]{:S(2)}, u32[]{:S(2)}) collective-permute-start(bf16[128,512]{1,0:T(8,128)(2,1)S(1)} %get-tuple-element.36.refs_8_), channel_id=1, source_target_pairs={{0,224},{32,128},{64,160},{96,192},{128,96},{160,0},{192,32},{224,... | collective-permute-start | bytes 393224 | tf_op jit(solution)/shard_map/ppermute | solution.py:320
  121.0 6.2 %collective-permute-done.21.refs_11_ = bf16[128,512]{1,0:T(8,128)(2,1)S(1)} collective-permute-done((bf16[128,512]{1,0:T(8,128)(2,1)S(1)}, bf16[128,512]{1,0:T(8,128)(2,1)S(1)}, u32[]{:S(2)}, u32[]{:S(2)}) %collective-permute-start.21) | collective-permute-done | bytes 131104 | tf_op jit(solution)/shard_map/ppermute | solution.py:22
  127.3 1.1 collective-permute-done.25.refs_15_
  128.4 1.7 %gram.3 = (f32[64,512]{1,0:T(8,128)S(1)}, bf16[64,512]{1,0:T(8,128)(2,1)S(1)}, bf16[64,512]{1,0:T(8,128)(2,1)S(1)}, bf16[64,512]{1,0:T(8,128)(2,1)S(1)}, bf16[64...) custom-call(s32[17]{0:T(128)S(1)} %stack.71.place_ref, ...), custom_call_target="tpu_custom_call" | custom-call | tf_op jit(solution)/shard_map/gram/pallas_call | solution.py:231
  130.1 5.1 %collective-permute-start.26 = (bf16[64,512]{1,0:T(8,128)(2,1)S(1)}, bf16[64,512]{1,0:T(8,128)(2,1)S(1)}, u32[]{:S(2)}, u32[]{:S(2)}) collective-permute-start(bf16[64,512]{1,0:T(8,128)(2,1)S(1)} %get-tuple-element.22), channel_id=1, source_target_pairs={{0,16},{4,20},{8,24},{12,28},{16,0},{20,4},{24,8},{28,12},{1,17},{... | collective-permute-start | bytes 196616 | tf_op jit(solution)/shard_map/ppermute | solution.py:22
  135.2 0.6 collective-permute-start.27
  135.8 4.5 %collective-permute-start.28 = (bf16[64,512]{1,0:T(8,128)(2,1)S(1)}, bf16[64,512]{1,0:T(8,128)(2,1)S(1)}, u32[]{:S(2)}, u32[]{:S(2)}) collective-permute-start(bf16[64,512]{1,0:T(8,128)(2,1)S(1)} %get-tuple-element.24), channel_id=1, source_target_pairs={{0,20},{4,24},{8,28},{12,0},{16,4},{20,8},{24,12},{28,16},{1,21},{... | collective-permute-start | bytes 196616 | tf_op jit(solution)/shard_map/ppermute | solution.py:22
  140.2 0.6 collective-permute-start.29
  140.8 3.6 %collective-permute-start.30 = (bf16[64,512]{1,0:T(8,128)(2,1)S(1)}, bf16[64,512]{1,0:T(8,128)(2,1)S(1)}, u32[]{:S(2)}, u32[]{:S(2)}) collective-permute-start(bf16[64,512]{1,0:T(8,128)(2,1)S(1)} %get-tuple-element.26), channel_id=1, source_target_pairs={{0,24},{4,28},{8,0},{12,4},{16,8},{20,12},{24,16},{28,20},{1,25},{... | collective-permute-start | bytes 196616 | tf_op jit(solution)/shard_map/ppermute | solution.py:22
  144.4 0.6 collective-permute-start.31
  144.9 2.7 %collective-permute-start.32 = (bf16[64,512]{1,0:T(8,128)(2,1)S(1)}, bf16[64,512]{1,0:T(8,128)(2,1)S(1)}, u32[]{:S(2)}, u32[]{:S(2)}) collective-permute-start(bf16[64,512]{1,0:T(8,128)(2,1)S(1)} %get-tuple-element.28), channel_id=1, source_target_pairs={{0,28},{4,0},{8,4},{12,8},{16,12},{20,16},{24,20},{28,24},{1,29},{... | collective-permute-start | bytes 196616 | tf_op jit(solution)/shard_map/ppermute | solution.py:22
  147.6 2.2 %collective-permute-done.31 = bf16[64,512]{1,0:T(8,128)(2,1)S(1)} collective-permute-done((bf16[64,512]{1,0:T(8,128)(2,1)S(1)}, bf16[64,512]{1,0:T(8,128)(2,1)S(1)}, u32[]{:S(2)}, u32[]{:S(2)}) %collective-permute-start.31) | collective-permute-done | bytes 65568 | tf_op jit(solution)/shard_map/ppermute | solution.py:22
  149.8 0.1 convert_add_fusion
  149.9 0.1 convert_reduce_fusion
  150.0 0.7 pad_maximum_fusion
  (35 shorter events, 0.1 us)
Async XLA Ops:
  0.0 40.2 %copy-start = (f32[4,128]{1,0:T(4,128)S(1)}, f32[4,128]{1,0:T(4,128)}, u32[]{:S(2)}) copy-start(f32[4,128]{1,0:T(4,128)} %wind_x_ref.5) | copy-start | bytes 6148
  0.0 40.2 %copy-start.1 = (f32[4,128]{1,0:T(4,128)S(1)}, f32[4,128]{1,0:T(4,128)}, u32[]{:S(2)}) copy-start(f32[4,128]{1,0:T(4,128)} %wind_y_ref.5) | copy-start | bytes 6148
  4.8 46.8 %all-to-all-start = ((bf16[64,8,256]{2,1,0:T(8,128)(2,1)}), bf16[64,8,256]{2,1,0:T(8,128)(2,1)S(1)}, u32[]{:S(2)}, u32[]{:S(2)}) async-start(bf16[64,8,256]{2,1,0:T(8,128)(2,1)} %fusion), calls=%async_computation | async-start | bytes 524288 | tf_op jit(solution)/shard_map/all_to_all | solution.py:26
  20.4 19.8 %collective-permute-start.2 = (bf16[1936,128]{1,0:T(8,128)(2,1)}, bf16[1936,128]{1,0:T(8,128)(2,1)S(1)}, u32[]{:S(2)}, u32[]{:S(2)}) collective-permute-start(bf16[1936,128]{1,0:T(8,128)(2,1)} %get-tuple-element.19), channel_id=1, source_target_pairs={{0,4},{4,8},{8,12},{12,16},{16,20},{20,24},{24,28},{28,32},{32,36}... | collective-permute-start | bytes 1486856 | tf_op jit(solution)/shard_map/ppermute | solution.py:22
  22.0 18.2 %collective-permute-start.3 = (bf16[1936,128]{1,0:T(8,128)(2,1)}, bf16[1936,128]{1,0:T(8,128)(2,1)S(1)}, u32[]{:S(2)}, u32[]{:S(2)}) collective-permute-start(bf16[1936,128]{1,0:T(8,128)(2,1)} %get-tuple-element.20), channel_id=1, source_target_pairs={{0,252},{4,0},{8,4},{12,8},{16,12},{20,16},{24,20},{28,24},{32,28}... | collective-permute-start | bytes 1486856 | tf_op jit(solution)/shard_map/ppermute | solution.py:22
  26.7 20.4 %collective-permute-start = (bf16[1168,128]{1,0:T(8,128)(2,1)}, bf16[1168,128]{1,0:T(8,128)(2,1)S(1)}, u32[]{:S(2)}, u32[]{:S(2)}) collective-permute-start(bf16[1168,128]{1,0:T(8,128)(2,1)} %get-tuple-element.17), channel_id=1, source_target_pairs={{0,4},{4,8},{8,12},{12,16},{16,20},{20,24},{24,28},{28,32},{32,36}... | collective-permute-start | bytes 897032 | tf_op jit(solution)/shard_map/ppermute | solution.py:22
  26.7 20.4 %collective-permute-start.1 = (bf16[1168,128]{1,0:T(8,128)(2,1)}, bf16[1168,128]{1,0:T(8,128)(2,1)S(1)}, u32[]{:S(2)}, u32[]{:S(2)}) collective-permute-start(bf16[1168,128]{1,0:T(8,128)(2,1)} %get-tuple-element.18), channel_id=1, source_target_pairs={{0,252},{4,0},{8,4},{12,8},{16,12},{20,16},{24,20},{28,24},{32,28}... | collective-permute-start | bytes 897032 | tf_op jit(solution)/shard_map/ppermute | solution.py:22
  51.6 9.5 %copy-start.2 = (bf16[128]{0:T(256)(128)(2,1)S(1)}, bf16[128]{0:T(256)(128)(2,1)}, u32[]{:S(2)}) copy-start(bf16[128]{0:T(256)(128)(2,1)} %param.11) | copy-start | bytes 772
  53.5 23.7 %all-to-all-start.1 = ((bf16[64,8,512]{2,1,0:T(8,128)(2,1)}), bf16[64,8,512]{2,1,0:T(8,128)(2,1)S(1)}, u32[]{:S(2)}, u32[]{:S(2)}) async-start(bf16[64,8,512]{2,1,0:T(8,128)(2,1)} %bitcast.24), calls=%async_computation.1 | async-start | bytes 1048576 | tf_op jit(solution)/shard_map/all_to_all | solution.py:26
  77.8 6.3 %collective-permute-start.12 = (bf16[128,512]{1,0:T(8,128)(2,1)S(1)}, bf16[128,512]{1,0:T(8,128)(2,1)S(1)}, u32[]{:S(2)}, u32[]{:S(2)}) collective-permute-start(bf16[128,512]{1,0:T(8,128)(2,1)S(1)} %get-tuple-element.35.refs_8_), channel_id=1, source_target_pairs={{0,128},{128,0},{1,129},{129,1},{2,130},{130,2},{3,131},{131,3},{4... | collective-permute-start | bytes 393224 | tf_op jit(solution)/shard_map/ppermute | solution.py:22
  79.7 6.8 %collective-permute-start.13 = (bf16[128,512]{1,0:T(8,128)(2,1)S(1)}, bf16[128,512]{1,0:T(8,128)(2,1)S(1)}, u32[]{:S(2)}, u32[]{:S(2)}) collective-permute-start(bf16[128,512]{1,0:T(8,128)(2,1)S(1)} %get-tuple-element.35.refs_8_), channel_id=1, source_target_pairs={{0,32},{32,64},{64,96},{96,0},{1,33},{33,65},{65,97},{97,1},{2,34}... | collective-permute-start | bytes 393224 | tf_op jit(solution)/shard_map/ppermute | solution.py:22
  80.2 10.6 %collective-permute-start.14 = (bf16[128,512]{1,0:T(8,128)(2,1)S(1)}, bf16[128,512]{1,0:T(8,128)(2,1)S(1)}, u32[]{:S(2)}, u32[]{:S(2)}) collective-permute-start(bf16[128,512]{1,0:T(8,128)(2,1)S(1)} %get-tuple-element.35.refs_8_), channel_id=1, source_target_pairs={{0,64},{32,96},{64,0},{96,32},{1,65},{33,97},{65,1},{97,33},{2,66}... | collective-permute-start | bytes 393224 | tf_op jit(solution)/shard_map/ppermute | solution.py:22
  81.8 9.1 %collective-permute-start.15 = (bf16[128,512]{1,0:T(8,128)(2,1)S(1)}, bf16[128,512]{1,0:T(8,128)(2,1)S(1)}, u32[]{:S(2)}, u32[]{:S(2)}) collective-permute-start(bf16[128,512]{1,0:T(8,128)(2,1)S(1)} %get-tuple-element.35.refs_8_), channel_id=1, source_target_pairs={{0,96},{32,0},{64,32},{96,64},{1,97},{33,1},{65,33},{97,65},{2,98}... | collective-permute-start | bytes 393224 | tf_op jit(solution)/shard_map/ppermute | solution.py:22
  82.9 10.3 %collective-permute-start.6 = (bf16[128,512]{1,0:T(8,128)(2,1)S(1)}, bf16[128,512]{1,0:T(8,128)(2,1)S(1)}, u32[]{:S(2)}, u32[]{:S(2)}) collective-permute-start(bf16[128,512]{1,0:T(8,128)(2,1)S(1)} %get-tuple-element.30), channel_id=1, source_target_pairs={{0,2},{1,66},{2,130},{3,194},{32,34},{33,98},{34,162},{35,226},{64... | collective-permute-start | bytes 393224 | tf_op jit(solution)/shard_map/ppermute | solution.py:304
  84.1 11.1 %collective-permute-start.7 = (bf16[128,512]{1,0:T(8,128)(2,1)S(1)}, bf16[128,512]{1,0:T(8,128)(2,1)S(1)}, u32[]{:S(2)}, u32[]{:S(2)}) collective-permute-start(bf16[128,512]{1,0:T(8,128)(2,1)S(1)} %get-tuple-element.29), channel_id=1, source_target_pairs={{0,34},{1,98},{2,162},{3,226},{32,2},{33,66},{34,130},{35,194},{64... | collective-permute-start | bytes 393224 | tf_op jit(solution)/shard_map/ppermute | solution.py:304
  86.5 11.0 %collective-permute-start.4 = (bf16[128,512]{1,0:T(8,128)(2,1)S(1)}, bf16[128,512]{1,0:T(8,128)(2,1)S(1)}, u32[]{:S(2)}, u32[]{:S(2)}) collective-permute-start(bf16[128,512]{1,0:T(8,128)(2,1)S(1)} %get-tuple-element.30), channel_id=1, source_target_pairs={{0,0},{1,64},{2,128},{3,192},{32,32},{33,96},{34,160},{35,224},{64... | collective-permute-start | bytes 393224 | tf_op jit(solution)/shard_map/ppermute | solution.py:304
  90.9 8.6 %collective-permute-start.5 = (bf16[128,512]{1,0:T(8,128)(2,1)S(1)}, bf16[128,512]{1,0:T(8,128)(2,1)S(1)}, u32[]{:S(2)}, u32[]{:S(2)}) collective-permute-start(bf16[128,512]{1,0:T(8,128)(2,1)S(1)} %get-tuple-element.29), channel_id=1, source_target_pairs={{0,32},{1,96},{2,160},{3,224},{32,0},{33,64},{34,128},{35,192},{64... | collective-permute-start | bytes 393224 | tf_op jit(solution)/shard_map/ppermute | solution.py:304
  90.9 10.6 %collective-permute-start.16 = (bf16[128,512]{1,0:T(8,128)(2,1)S(1)}, bf16[128,512]{1,0:T(8,128)(2,1)S(1)}, u32[]{:S(2)}, u32[]{:S(2)}) collective-permute-start(bf16[128,512]{1,0:T(8,128)(2,1)S(1)} %collective-permute-done.12.refs_9_), channel_id=1, source_target_pairs={{0,32},{32,64},{64,96},{96,0},{1,33},{33,65},{65,97},{97,1},{2,34}... | collective-permute-start | bytes 393224 | tf_op jit(solution)/shard_map/ppermute | solution.py:22
  93.3 9.2 %collective-permute-start.17 = (bf16[128,512]{1,0:T(8,128)(2,1)S(1)}, bf16[128,512]{1,0:T(8,128)(2,1)S(1)}, u32[]{:S(2)}, u32[]{:S(2)}) collective-permute-start(bf16[128,512]{1,0:T(8,128)(2,1)S(1)} %collective-permute-done.12.refs_9_), channel_id=1, source_target_pairs={{0,64},{32,96},{64,0},{96,32},{1,65},{33,97},{65,1},{97,33},{2,66}... | collective-permute-start | bytes 393224 | tf_op jit(solution)/shard_map/ppermute | solution.py:22
  95.2 8.0 %collective-permute-start.18 = (bf16[128,512]{1,0:T(8,128)(2,1)S(1)}, bf16[128,512]{1,0:T(8,128)(2,1)S(1)}, u32[]{:S(2)}, u32[]{:S(2)}) collective-permute-start(bf16[128,512]{1,0:T(8,128)(2,1)S(1)} %collective-permute-done.12.refs_9_), channel_id=1, source_target_pairs={{0,96},{32,0},{64,32},{96,64},{1,97},{33,1},{65,33},{97,65},{2,98}... | collective-permute-start | bytes 393224 | tf_op jit(solution)/shard_map/ppermute | solution.py:22
  97.5 5.6 %collective-permute-start.10 = (bf16[128,512]{1,0:T(8,128)(2,1)S(1)}, bf16[128,512]{1,0:T(8,128)(2,1)S(1)}, u32[]{:S(2)}, u32[]{:S(2)}) collective-permute-start(bf16[128,512]{1,0:T(8,128)(2,1)S(1)} %collective-permute-done.6.refs_2_), channel_id=1, source_target_pairs={{0,1},{1,0},{2,3},{3,2},{4,5},{5,4},{6,7},{7,6},{8,9},{9,8},{10,11... | collective-permute-start | bytes 393224 | tf_op jit(solution)/shard_map/ppermute | solution.py:22
  99.5 3.7 %collective-permute-start.11 = (bf16[128,512]{1,0:T(8,128)(2,1)S(1)}, bf16[128,512]{1,0:T(8,128)(2,1)S(1)}, u32[]{:S(2)}, u32[]{:S(2)}) collective-permute-start(bf16[128,512]{1,0:T(8,128)(2,1)S(1)} %collective-permute-done.7.refs_3_), channel_id=1, source_target_pairs={{0,1},{1,0},{2,3},{3,2},{4,5},{5,4},{6,7},{7,6},{8,9},{9,8},{10,11... | collective-permute-start | bytes 393224 | tf_op jit(solution)/shard_map/ppermute | solution.py:22
  101.4 2.0 %collective-permute-start.8 = (bf16[128,512]{1,0:T(8,128)(2,1)S(1)}, bf16[128,512]{1,0:T(8,128)(2,1)S(1)}, u32[]{:S(2)}, u32[]{:S(2)}) collective-permute-start(bf16[128,512]{1,0:T(8,128)(2,1)S(1)} %collective-permute-done.4.refs_0_), channel_id=1, source_target_pairs={{0,1},{1,0},{2,3},{3,2},{4,5},{5,4},{6,7},{7,6},{8,9},{9,8},{10,11... | collective-permute-start | bytes 393224 | tf_op jit(solution)/shard_map/ppermute | solution.py:22
  102.5 1.3 collective-permute-start.9
  106.3 43.6 %all-to-all-start.2 = ((bf16[8,64,512]{2,1,0:T(8,128)(2,1)}), bf16[8,64,512]{2,1,0:T(8,128)(2,1)S(1)}, u32[]{:S(2)}, u32[]{:S(2)}) async-start(bf16[8,64,512]{2,1,0:T(8,128)(2,1)} %bitcast.26), calls=%async_computation.2 | async-start | bytes 1048576 | tf_op jit(solution)/shard_map/all_to_all | solution.py:26
  109.8 7.7 %collective-permute-start.19 = (bf16[128,512]{1,0:T(8,128)(2,1)S(1)}, bf16[128,512]{1,0:T(8,128)(2,1)S(1)}, u32[]{:S(2)}, u32[]{:S(2)}) collective-permute-start(bf16[128,512]{1,0:T(8,128)(2,1)S(1)} %get-tuple-element.36.refs_8_), channel_id=1, source_target_pairs={{0,128},{128,0},{1,129},{129,1},{2,130},{130,2},{3,131},{131,3},{4... | collective-permute-start | bytes 393224 | tf_op jit(solution)/shard_map/ppermute | solution.py:22
  110.4 8.3 %collective-permute-start.20 = (bf16[128,512]{1,0:T(8,128)(2,1)S(1)}, bf16[128,512]{1,0:T(8,128)(2,1)S(1)}, u32[]{:S(2)}, u32[]{:S(2)}) collective-permute-start(bf16[128,512]{1,0:T(8,128)(2,1)S(1)} %get-tuple-element.36.refs_8_), channel_id=1, source_target_pairs={{0,32},{32,64},{64,96},{96,0},{1,33},{33,65},{65,97},{97,1},{2,34}... | collective-permute-start | bytes 393224 | tf_op jit(solution)/shard_map/ppermute | solution.py:22
  111.3 15.9 %collective-permute-start.21 = (bf16[128,512]{1,0:T(8,128)(2,1)S(1)}, bf16[128,512]{1,0:T(8,128)(2,1)S(1)}, u32[]{:S(2)}, u32[]{:S(2)}) collective-permute-start(bf16[128,512]{1,0:T(8,128)(2,1)S(1)} %get-tuple-element.36.refs_8_), channel_id=1, source_target_pairs={{0,64},{32,96},{64,0},{96,32},{1,65},{33,97},{65,1},{97,33},{2,66}... | collective-permute-start | bytes 393224 | tf_op jit(solution)/shard_map/ppermute | solution.py:22
  114.1 13.2 %collective-permute-start.22 = (bf16[128,512]{1,0:T(8,128)(2,1)S(1)}, bf16[128,512]{1,0:T(8,128)(2,1)S(1)}, u32[]{:S(2)}, u32[]{:S(2)}) collective-permute-start(bf16[128,512]{1,0:T(8,128)(2,1)S(1)} %get-tuple-element.36.refs_8_), channel_id=1, source_target_pairs={{0,96},{32,0},{64,32},{96,64},{1,97},{33,1},{65,33},{97,65},{2,98}... | collective-permute-start | bytes 393224 | tf_op jit(solution)/shard_map/ppermute | solution.py:22
  116.1 11.1 %collective-permute-start.23 = (bf16[128,512]{1,0:T(8,128)(2,1)S(1)}, bf16[128,512]{1,0:T(8,128)(2,1)S(1)}, u32[]{:S(2)}, u32[]{:S(2)}) collective-permute-start(bf16[128,512]{1,0:T(8,128)(2,1)S(1)} %get-tuple-element.36.refs_8_), channel_id=1, source_target_pairs={{0,160},{32,192},{64,224},{96,128},{128,32},{160,64},{192,96},{224... | collective-permute-start | bytes 393224 | tf_op jit(solution)/shard_map/ppermute | solution.py:320
  117.5 9.8 %collective-permute-start.24 = (bf16[128,512]{1,0:T(8,128)(2,1)S(1)}, bf16[128,512]{1,0:T(8,128)(2,1)S(1)}, u32[]{:S(2)}, u32[]{:S(2)}) collective-permute-start(bf16[128,512]{1,0:T(8,128)(2,1)S(1)} %get-tuple-element.36.refs_8_), channel_id=1, source_target_pairs={{0,192},{32,224},{64,128},{96,160},{128,64},{160,96},{192,0},{224,... | collective-permute-start | bytes 393224 | tf_op jit(solution)/shard_map/ppermute | solution.py:320
  118.7 9.7 %collective-permute-start.25 = (bf16[128,512]{1,0:T(8,128)(2,1)S(1)}, bf16[128,512]{1,0:T(8,128)(2,1)S(1)}, u32[]{:S(2)}, u32[]{:S(2)}) collective-permute-start(bf16[128,512]{1,0:T(8,128)(2,1)S(1)} %get-tuple-element.36.refs_8_), channel_id=1, source_target_pairs={{0,224},{32,128},{64,160},{96,192},{128,96},{160,0},{192,32},{224,... | collective-permute-start | bytes 393224 | tf_op jit(solution)/shard_map/ppermute | solution.py:320
  130.1 14.3 %collective-permute-start.26 = (bf16[64,512]{1,0:T(8,128)(2,1)S(1)}, bf16[64,512]{1,0:T(8,128)(2,1)S(1)}, u32[]{:S(2)}, u32[]{:S(2)}) collective-permute-start(bf16[64,512]{1,0:T(8,128)(2,1)S(1)} %get-tuple-element.22), channel_id=1, source_target_pairs={{0,16},{4,20},{8,24},{12,28},{16,0},{20,4},{24,8},{28,12},{1,17},{... | collective-permute-start | bytes 196616 | tf_op jit(solution)/shard_map/ppermute | solution.py:22
  135.2 9.7 %collective-permute-start.27 = (bf16[64,512]{1,0:T(8,128)(2,1)S(1)}, bf16[64,512]{1,0:T(8,128)(2,1)S(1)}, u32[]{:S(2)}, u32[]{:S(2)}) collective-permute-start(bf16[64,512]{1,0:T(8,128)(2,1)S(1)} %get-tuple-element.23), channel_id=1, source_target_pairs={{0,12},{4,16},{8,20},{12,24},{16,28},{20,0},{24,4},{28,8},{1,13},{... | collective-permute-start | bytes 196616 | tf_op jit(solution)/shard_map/ppermute | solution.py:22
  135.8 11.8 %collective-permute-start.28 = (bf16[64,512]{1,0:T(8,128)(2,1)S(1)}, bf16[64,512]{1,0:T(8,128)(2,1)S(1)}, u32[]{:S(2)}, u32[]{:S(2)}) collective-permute-start(bf16[64,512]{1,0:T(8,128)(2,1)S(1)} %get-tuple-element.24), channel_id=1, source_target_pairs={{0,20},{4,24},{8,28},{12,0},{16,4},{20,8},{24,12},{28,16},{1,21},{... | collective-permute-start | bytes 196616 | tf_op jit(solution)/shard_map/ppermute | solution.py:22
  140.2 7.4 %collective-permute-start.29 = (bf16[64,512]{1,0:T(8,128)(2,1)S(1)}, bf16[64,512]{1,0:T(8,128)(2,1)S(1)}, u32[]{:S(2)}, u32[]{:S(2)}) collective-permute-start(bf16[64,512]{1,0:T(8,128)(2,1)S(1)} %get-tuple-element.25), channel_id=1, source_target_pairs={{0,8},{4,12},{8,16},{12,20},{16,24},{20,28},{24,0},{28,4},{1,9},{5... | collective-permute-start | bytes 196616 | tf_op jit(solution)/shard_map/ppermute | solution.py:22
  140.8 6.8 %collective-permute-start.30 = (bf16[64,512]{1,0:T(8,128)(2,1)S(1)}, bf16[64,512]{1,0:T(8,128)(2,1)S(1)}, u32[]{:S(2)}, u32[]{:S(2)}) collective-permute-start(bf16[64,512]{1,0:T(8,128)(2,1)S(1)} %get-tuple-element.26), channel_id=1, source_target_pairs={{0,24},{4,28},{8,0},{12,4},{16,8},{20,12},{24,16},{28,20},{1,25},{... | collective-permute-start | bytes 196616 | tf_op jit(solution)/shard_map/ppermute | solution.py:22
  144.4 5.5 %collective-permute-start.31 = (bf16[64,512]{1,0:T(8,128)(2,1)S(1)}, bf16[64,512]{1,0:T(8,128)(2,1)S(1)}, u32[]{:S(2)}, u32[]{:S(2)}) collective-permute-start(bf16[64,512]{1,0:T(8,128)(2,1)S(1)} %get-tuple-element.27), channel_id=1, source_target_pairs={{0,4},{4,8},{8,12},{12,16},{16,20},{20,24},{24,28},{28,0},{1,5},{5... | collective-permute-start | bytes 196616 | tf_op jit(solution)/shard_map/ppermute | solution.py:22
  144.9 4.9 %collective-permute-start.32 = (bf16[64,512]{1,0:T(8,128)(2,1)S(1)}, bf16[64,512]{1,0:T(8,128)(2,1)S(1)}, u32[]{:S(2)}, u32[]{:S(2)}) collective-permute-start(bf16[64,512]{1,0:T(8,128)(2,1)S(1)} %get-tuple-element.28), channel_id=1, source_target_pairs={{0,28},{4,0},{8,4},{12,8},{16,12},{20,16},{24,20},{28,24},{1,29},{... | collective-permute-start | bytes 196616 | tf_op jit(solution)/shard_map/ppermute | solution.py:22

commit v4 on v3

--- a/solution.py
+++ b/solution.py
@@ -195,17 +195,22 @@
 
 
 def gram_body(apart, place_ref, *refs):
-    rows, cols, outs, scratch = refs[:8], refs[8:16], refs[16:-3], refs[-3:]
+    outs = apart if apart else 1
+    rows, cols, outs, scratch = refs[:8], refs[8 : -3 - outs], refs[-3 - outs : -3], refs[-3:]
     rows_ref, cols_ref, sum_ref = scratch
     block = rows[0].shape[0]
     for k, ref in enumerate(rows):
         at = pl.multiple_of(place_ref[k] * block, block)
         rows_ref[:, pl.ds(at, block)] = ref[...].T
-    for k, ref in enumerate(cols):
-        at = pl.multiple_of(place_ref[8 + k] * block, block)
-        cols_ref[pl.ds(at, block), :] = ref[...]
+    if len(cols) > 1:
+        for k, ref in enumerate(cols):
+            at = pl.multiple_of(place_ref[8 + k] * block, block)
+            cols_ref[pl.ds(at, block), :] = ref[...]
+        right = cols_ref[...]
+    else:
+        right = cols[0][...]
     tile = lax.dot_general(
-        rows_ref[...], cols_ref[...], (((1,), (0,)), ((), ())), preferred_element_type=jnp.float32
+        rows_ref[...], right, (((1,), (0,)), ((), ())), preferred_element_type=jnp.float32
     )
     if not apart:
         outs[0][...] = tile.astype(jnp.bfloat16)
@@ -219,7 +224,7 @@
 
 
 def gram_tile(place, pieces, cols, apart):
-    obs, width = cols[0].shape
+    count, width = sum(v.shape[0] for v in cols), cols[0].shape[1]
     rows = pieces[0].shape[1]
     if apart:
         size = (rows // apart, width)
@@ -234,8 +239,8 @@
         out_specs=[whole] * len(shapes),
         out_shape=shapes,
         scratch_shapes=[
-            pltpu.VMEM((rows, len(cols) * obs), jnp.bfloat16),
-            pltpu.VMEM((len(cols) * obs, width), jnp.bfloat16),
+            pltpu.VMEM((rows, count), jnp.bfloat16),
+            pltpu.VMEM((count, width), jnp.bfloat16),
             pltpu.VMEM((rows, width), jnp.float32),
         ],
         compiler_params=pltpu.CompilerParams(vmem_limit_bytes=GRANT),
@@ -306,18 +311,14 @@
         pieces.append(shifted(pieces[k], "core", 1))
 
     deep = lax.axis_size("y")
-    cols = []
-    for part, value in enumerate(weighted):
-        beside = shifted(value, "xl", 1)
-        cols.append([value, beside])
-        for d in range(1, deep):
-            cols[part].append(shifted(value, "y", d))
-        for d in range(1, deep):
-            if part == 0:
-                cols[part].append(shifted(beside, "y", d))
-            else:
-                path = [(k, (1 - k // deep) * deep + (k + d) % deep) for k in range(group)]
-                cols[part].append(lax.ppermute(value, XY, path))
+    first_cols = exchanged(jnp.broadcast_to(weighted[0], (group, obs, half)), XY)
+    value = weighted[1]
+    cols = [value, shifted(value, "xl", 1)]
+    for d in range(1, deep):
+        cols.append(shifted(value, "y", d))
+    for d in range(1, deep):
+        path = [(k, (1 - k // deep) * deep + (k + d) % deep) for k in range(group)]
+        cols.append(lax.ppermute(value, XY, path))
     xl, y = lax.axis_index("xl"), lax.axis_index("y")
     owners = [here, (1 - xl) * deep + y]
     owners += [xl * deep + (y - d) % deep for d in range(1, deep)]
@@ -327,10 +328,10 @@
     place = jnp.stack(row_owners + owners + [lax.axis_index("z")]).astype(jnp.int32)
 
     depth = lax.axis_size("z")
-    tile = gram_tile(place, pieces, cols[0], 0)[0]
+    tile = gram_tile(place, pieces, [first_cols.reshape(group * obs, half)], 0)[0]
     parts = exchanged(tile.reshape(depth, half // depth, half), "z")
     total = jnp.sum(parts.astype(jnp.float32), axis=0)
-    blocks = gram_tile(place, pieces, cols[1], depth)
+    blocks = gram_tile(place, pieces, cols, depth)
     last = blocks[0]
     for d in (4, 3, 5, 2, 6, 1, 7):
         last = last + shifted(blocks[d], "z", d).astype(jnp.float32)

time: 153 us -> 154 us (level)
  waiting for transfers between devices: 39.6 us -> 34.2 us
  starting transfers between devices: 84.3 us -> 89.4 us
    ppermute x26 -> x19, waiting for transfers between devices: 20.6 us -> 11 us  [shifted(): lax.ppermute(value, axis, [(i, (i + steps) % count) for i in range(count)])]
    ppermute x26 -> x19, starting transfers between devices: 49.2 us -> 41.5 us  [shifted(): lax.ppermute(value, axis, [(i, (i + steps) % count) for i in range(count)])]
    ppermute x3, starting transfers between devices: 4.88 us -> 11.8 us  [on_device(): cols.append(lax.ppermute(value, XY, path))]
    all_to_all x3 -> x4, starting transfers between devices: 23.9 us -> 27.8 us  [exchanged(): return lax.all_to_all(value, axis, split_axis=0, concat_axis=0, tiled=True)]
    ppermute x4, waiting for transfers between devices: 1.95 us -> 5.24 us  [on_device(): pieces.append(lax.ppermute(value, PLANE, path))]
    ppermute x4, starting transfers between devices: 6.33 us -> 8.28 us  [on_device(): pieces.append(lax.ppermute(value, PLANE, path))]
    all_to_all x3 -> x4, waiting for transfers between devices: 16 us -> 16 us  [exchanged(): return lax.all_to_all(value, axis, split_axis=0, concat_axis=0, tiled=True)]
  transfers between devices with their start and end apart: 36 -> 30, of which waited for: 11 -> 10; matrix products, arithmetic and copies ran while one was open for 0% -> 0% of each run, Pallas kernels for 11% -> 11%
where the time goes in v4:
time: 154 us; the launch traced here: 151 us
  starting transfers between devices  89.4 us (58%)
  waiting for transfers between devices  34.2 us (22%)
  Pallas kernels  20.1 us (13%)
  other arithmetic  4.67 us (3%)
  matrix products  1.61 us (1%)
    ppermute x19, starting transfers between devices, shifted(): lax.ppermute(value, axis, [(i, (i + steps) % count) for i in range(count)])  41.5 us
    all_to_all x4, starting transfers between devices, exchanged(): return lax.all_to_all(value, axis, split_axis=0, concat_axis=0, tiled=True)  27.8 us
    all_to_all x4, waiting for transfers between devices, exchanged(): return lax.all_to_all(value, axis, split_axis=0, concat_axis=0, tiled=True)  16 us
    ppermute x3, starting transfers between devices, on_device(): cols.append(lax.ppermute(value, XY, path))  11.8 us
    pallas_call x2, Pallas kernels, transport(): pl.pallas_call(functools.partial(transport_body, skip), grid=(steps,), in...  11.4 us
    ppermute x19, waiting for transfers between devices, shifted(): lax.ppermute(value, axis, [(i, (i + steps) % count) for i in range(count)])  11 us
    ppermute x4, starting transfers between devices, on_device(): pieces.append(lax.ppermute(value, PLANE, path))  8.28 us
    ppermute x4, waiting for transfers between devices, on_device(): pieces.append(lax.ppermute(value, PLANE, path))  5.24 us
  transfers between devices with their start and end apart: 30, of which 10 were waited for; matrix products, arithmetic and copies ran while one was open for 0% of the time, Pallas kernels for 11%

profile of v4, /device:TPU:4, one launch (start us, length us, event | category | flops | bytes accessed | tf_op | source)
XLA Modules:
  0.0 151.4 jit_solution(11881505931642132341)
XLA Ops:
  0.0 0.9 convert_reduce_fusion.2
  0.9 0.7 fusion.15
  1.6 1.0 convert_reduce_fusion.1
  2.6 1.0 fusion.8
  3.6 0.1 iota_compare_fusion
  3.8 1.1 fusion
  4.8 12.7 %all-to-all-start = ((bf16[64,8,256]{2,1,0:T(8,128)(2,1)}), bf16[64,8,256]{2,1,0:T(8,128)(2,1)S(1)}, u32[]{:S(2)}, u32[]{:S(2)}) async-start(bf16[64,8,256]{2,1,0:T(8,128)(2,1)} %fusion), calls=%async_computation | async-start | bytes 524288 | tf_op jit(solution)/shard_map/all_to_all | solution.py:26
  17.6 2.9 %edges.1 = (bf16[1936,128]{1,0:T(8,128)(2,1)}, bf16[1936,128]{1,0:T(8,128)(2,1)}, bf16[1168,128]{1,0:T(8,128)(2,1)}, bf16[1168,128]{1,0:T(8,128)(2,1)}) custom-call(f32[4096,128]{1,0:T(8,128)} %bitcast.44, f32[4,128]{1,0:T(4,128)} %wind_x_ref.5, f32[4,128]{1,0:T(4,128)} %wind_y_ref.5), custom_call_target="tpu_custom_call" | custom-call | tf_op jit(solution)/shard_map/edges/pallas_call | solution.py:53
  20.4 1.6 %collective-permute-start.2 = (bf16[1936,128]{1,0:T(8,128)(2,1)}, bf16[1936,128]{1,0:T(8,128)(2,1)S(1)}, u32[]{:S(2)}, u32[]{:S(2)}) collective-permute-start(bf16[1936,128]{1,0:T(8,128)(2,1)} %get-tuple-element.19), channel_id=1, source_target_pairs={{0,4},{4,8},{8,12},{12,16},{16,20},{20,24},{24,28},{28,32},{32,36}... | collective-permute-start | bytes 1486856 | tf_op jit(solution)/shard_map/ppermute | solution.py:22
  22.0 4.7 %collective-permute-start.3 = (bf16[1936,128]{1,0:T(8,128)(2,1)}, bf16[1936,128]{1,0:T(8,128)(2,1)S(1)}, u32[]{:S(2)}, u32[]{:S(2)}) collective-permute-start(bf16[1936,128]{1,0:T(8,128)(2,1)} %get-tuple-element.20), channel_id=1, source_target_pairs={{0,252},{4,0},{8,4},{12,8},{16,12},{20,16},{24,20},{28,24},{32,28}... | collective-permute-start | bytes 1486856 | tf_op jit(solution)/shard_map/ppermute | solution.py:22
  26.7 0.0 collective-permute-start
  26.7 6.2 %collective-permute-start.1 = (bf16[1168,128]{1,0:T(8,128)(2,1)}, bf16[1168,128]{1,0:T(8,128)(2,1)S(1)}, u32[]{:S(2)}, u32[]{:S(2)}) collective-permute-start(bf16[1168,128]{1,0:T(8,128)(2,1)} %get-tuple-element.18), channel_id=1, source_target_pairs={{0,252},{4,0},{8,4},{12,8},{16,12},{20,16},{24,20},{28,24},{32,28}... | collective-permute-start | bytes 897032 | tf_op jit(solution)/shard_map/ppermute | solution.py:22
  32.9 7.3 %collective-permute-done.2.a0.a1.a2.a_winds = bf16[1936,128]{1,0:T(8,128)(2,1)S(1)} collective-permute-done((bf16[1936,128]{1,0:T(8,128)(2,1)}, bf16[1936,128]{1,0:T(8,128)(2,1)S(1)}, u32[]{:S(2)}, u32[]{:S(2)}) %collective-permute-start.2) | collective-permute-done | bytes 495648 | tf_op jit(solution)/shard_map/ppermute | solution.py:22
  40.2 0.0 collective-permute-done.3.b0.b1.b2.b_winds
  40.2 6.9 %transport.2.refs_0_ = bf16[1024,512]{1,0:T(8,128)(2,1)S(1)} custom-call(f32[4096,128]{1,0:T(8,128)} %bitcast.45, bf16[1936,128]{1,0:T(8,128)(2,1)S(1)} %collective-permute-done.2.a0.a1.a2.a_winds, bf16[1936,128]{1,0:T(8,128)(2,1)S(1)} %collective-permute-done.2.a0.a1.a2.a_winds, bf16[1936,128]{1,0:T(8,128)(2,1)S(1)} %collective-permute-done.2.a0.a1.a2.a_winds, ...), custom_call_target="tpu_custom_call" | custom-call | tf_op jit(solution)/shard_map/transport/pallas_call | solution.py:140
  47.1 0.0 collective-permute-done.a0.a1.a2.a_winds
  47.1 0.0 collective-permute-done.1.b0.b1.b2.b_winds
  47.1 4.5 %transport.3.low_ref.high_ref = bf16[1024,512]{1,0:T(8,128)(2,1)S(1)} custom-call(f32[4096,128]{1,0:T(8,128)} %bitcast.46, bf16[1168,128]{1,0:T(8,128)(2,1)S(1)} %collective-permute-done.a0.a1.a2.a_winds, bf16[1168,128]{1,0:T(8,128)(2,1)S(1)} %collective-permute-done.a0.a1.a2.a_winds, ...), custom_call_target="tpu_custom_call", output_to_operand_aliasing={{}: (11, {})} | custom-call | tf_op jit(solution)/shard_map/transport/pallas_call | solution.py:140
  51.6 0.0 copy-start.2
  51.7 0.0 all-to-all-done
  51.7 1.8 %jacobian.1 = bf16[512,512]{1,0:T(8,128)(2,1)} custom-call(bf16[512,256]{1,0:T(8,128)(2,1)S(1)} %bitcast.43, bf16[1024,512]{1,0:T(8,128)(2,1)S(1)} %transport.3.low_ref.high_ref, bf16[1024,512]{1,0:T(8,128)(2,1)S(1)} %transport.3.low_ref.high_ref), custom_call_target="tpu_custom_call" | custom-call | tf_op jit(solution)/shard_map/jacobian/pallas_call | solution.py:181
  53.5 7.6 %all-to-all-start.1 = ((bf16[64,8,512]{2,1,0:T(8,128)(2,1)}), bf16[64,8,512]{2,1,0:T(8,128)(2,1)S(1)}, u32[]{:S(2)}, u32[]{:S(2)}) async-start(bf16[64,8,512]{2,1,0:T(8,128)(2,1)} %bitcast.24), calls=%async_computation.1 | async-start | bytes 1048576 | tf_op jit(solution)/shard_map/all_to_all | solution.py:26
  61.2 16.0 %all-to-all-done.1 = bf16[64,8,512]{2,1,0:T(8,128)(2,1)S(1)} async-done(((bf16[64,8,512]{2,1,0:T(8,128)(2,1)}), bf16[64,8,512]{2,1,0:T(8,128)(2,1)S(1)}, u32[]{:S(2)}, u32[]{:S(2)}) %all-to-all-start.1) | async-done | bytes 524320 | tf_op jit(solution)/shard_map/all_to_all | solution.py:26
  77.2 0.3 fusion.3
  77.4 0.3 broadcast_select_fusion
  77.7 0.1 multiply_convert_fusion.1
  77.8 1.1 broadcast_in_dim.2
  78.9 3.6 %all-to-all-start.2 = ((bf16[8,128,512]{2,1,0:T(8,128)(2,1)}), bf16[8,128,512]{2,1,0:T(8,128)(2,1)S(1)}, u32[]{:S(2)}, u32[]{:S(2)}) async-start(bf16[8,128,512]{2,1,0:T(8,128)(2,1)} %broadcast_in_dim.2), calls=%async_computation.2 | async-start | bytes 2097152 | tf_op jit(solution)/shard_map/all_to_all | solution.py:26
  82.5 2.0 %collective-permute-start.6 = (bf16[128,512]{1,0:T(8,128)(2,1)S(1)}, bf16[128,512]{1,0:T(8,128)(2,1)S(1)}, u32[]{:S(2)}, u32[]{:S(2)}) collective-permute-start(bf16[128,512]{1,0:T(8,128)(2,1)S(1)} %get-tuple-element.30), channel_id=1, source_target_pairs={{0,2},{1,66},{2,130},{3,194},{32,34},{33,98},{34,162},{35,226},{64... | collective-permute-start | bytes 393224 | tf_op jit(solution)/shard_map/ppermute | solution.py:309
  84.4 2.3 %collective-permute-start.7 = (bf16[128,512]{1,0:T(8,128)(2,1)S(1)}, bf16[128,512]{1,0:T(8,128)(2,1)S(1)}, u32[]{:S(2)}, u32[]{:S(2)}) collective-permute-start(bf16[128,512]{1,0:T(8,128)(2,1)S(1)} %get-tuple-element.29), channel_id=1, source_target_pairs={{0,34},{1,98},{2,162},{3,226},{32,2},{33,66},{34,130},{35,194},{64... | collective-permute-start | bytes 393224 | tf_op jit(solution)/shard_map/ppermute | solution.py:309
  86.7 3.1 %collective-permute-start.4 = (bf16[128,512]{1,0:T(8,128)(2,1)S(1)}, bf16[128,512]{1,0:T(8,128)(2,1)S(1)}, u32[]{:S(2)}, u32[]{:S(2)}) collective-permute-start(bf16[128,512]{1,0:T(8,128)(2,1)S(1)} %get-tuple-element.30), channel_id=1, source_target_pairs={{0,0},{1,64},{2,128},{3,192},{32,32},{33,96},{34,160},{35,224},{64... | collective-permute-start | bytes 393224 | tf_op jit(solution)/shard_map/ppermute | solution.py:309
  89.9 0.9 collective-permute-start.5
  90.7 5.0 %collective-permute-done.6.refs_2_ = bf16[128,512]{1,0:T(8,128)(2,1)S(1)} collective-permute-done((bf16[128,512]{1,0:T(8,128)(2,1)S(1)}, bf16[128,512]{1,0:T(8,128)(2,1)S(1)}, u32[]{:S(2)}, u32[]{:S(2)}) %collective-permute-start.6) | collective-permute-done | bytes 131104 | tf_op jit(solution)/shard_map/ppermute | solution.py:309
  95.7 4.1 %collective-permute-start.10 = (bf16[128,512]{1,0:T(8,128)(2,1)S(1)}, bf16[128,512]{1,0:T(8,128)(2,1)S(1)}, u32[]{:S(2)}, u32[]{:S(2)}) collective-permute-start(bf16[128,512]{1,0:T(8,128)(2,1)S(1)} %collective-permute-done.6.refs_2_), channel_id=1, source_target_pairs={{0,1},{1,0},{2,3},{3,2},{4,5},{5,4},{6,7},{7,6},{8,9},{9,8},{10,11... | collective-permute-start | bytes 393224 | tf_op jit(solution)/shard_map/ppermute | solution.py:22
  99.8 1.0 collective-permute-start.11
  100.8 0.0 collective-permute-start.8
  100.8 0.2 collective-permute-done.5.refs_1_
  101.1 0.6 collective-permute-start.9
  101.7 0.1 stack.71.place_ref
  101.8 0.1 collective-permute-done.11.refs_7_
  101.8 0.4 collective-permute-done.8.refs_4_
  102.2 0.5 collective-permute-done.9.refs_5_
  102.6 2.4 %gram.2 = bf16[512,512]{1,0:T(8,128)(2,1)} custom-call(s32[17]{0:T(128)S(1)} %stack.71.place_ref, bf16[128,512]{1,0:T(8,128)(2,1)S(1)} %collective-permute-done.4.refs_0_, bf16[128,512]{1,0:T(8,128)(2,1)S(1)} %collective-permute-done.5.refs_1_, bf16[128,512]{1,0:T(8,128)(2,1)S(1)} %collective-permute-done.6.refs_2_, ...), custom_call_target="tpu_custom_call" | custom-call | tf_op jit(solution)/shard_map/gram/pallas_call | solution.py:236
  105.0 3.9 %all-to-all-start.3 = ((bf16[8,64,512]{2,1,0:T(8,128)(2,1)}), bf16[8,64,512]{2,1,0:T(8,128)(2,1)S(1)}, u32[]{:S(2)}, u32[]{:S(2)}) async-start(bf16[8,64,512]{2,1,0:T(8,128)(2,1)} %bitcast.27), calls=%async_computation.3 | async-start | bytes 1048576 | tf_op jit(solution)/shard_map/all_to_all | solution.py:26
  108.9 1.3 collective-permute-start.12
  110.2 0.5 collective-permute-start.13
  110.7 3.1 %collective-permute-start.14 = (bf16[128,512]{1,0:T(8,128)(2,1)S(1)}, bf16[128,512]{1,0:T(8,128)(2,1)S(1)}, u32[]{:S(2)}, u32[]{:S(2)}) collective-permute-start(bf16[128,512]{1,0:T(8,128)(2,1)S(1)} %get-tuple-element.36.refs_8_), channel_id=1, source_target_pairs={{0,64},{32,96},{64,0},{96,32},{1,65},{33,97},{65,1},{97,33},{2,66}... | collective-permute-start | bytes 393224 | tf_op jit(solution)/shard_map/ppermute | solution.py:22
  113.8 0.6 collective-permute-start.15
  114.4 2.8 %collective-permute-start.16 = (bf16[128,512]{1,0:T(8,128)(2,1)S(1)}, bf16[128,512]{1,0:T(8,128)(2,1)S(1)}, u32[]{:S(2)}, u32[]{:S(2)}) collective-permute-start(bf16[128,512]{1,0:T(8,128)(2,1)S(1)} %get-tuple-element.36.refs_8_), channel_id=1, source_target_pairs={{0,160},{32,192},{64,224},{96,128},{128,32},{160,64},{192,96},{224... | collective-permute-start | bytes 393224 | tf_op jit(solution)/shard_map/ppermute | solution.py:321
  117.2 9.0 %collective-permute-start.18 = (bf16[128,512]{1,0:T(8,128)(2,1)S(1)}, bf16[128,512]{1,0:T(8,128)(2,1)S(1)}, u32[]{:S(2)}, u32[]{:S(2)}) collective-permute-start(bf16[128,512]{1,0:T(8,128)(2,1)S(1)} %get-tuple-element.36.refs_8_), channel_id=1, source_target_pairs={{0,224},{32,128},{64,160},{96,192},{128,96},{160,0},{192,32},{224,... | collective-permute-start | bytes 393224 | tf_op jit(solution)/shard_map/ppermute | solution.py:321
  126.2 0.5 collective-permute-done.14.refs_11_
  126.7 2.0 %collective-permute-done.18.refs_15_ = bf16[128,512]{1,0:T(8,128)(2,1)S(1)} collective-permute-done((bf16[128,512]{1,0:T(8,128)(2,1)S(1)}, bf16[128,512]{1,0:T(8,128)(2,1)S(1)}, u32[]{:S(2)}, u32[]{:S(2)}) %collective-permute-start.18) | collective-permute-done | bytes 131104 | tf_op jit(solution)/shard_map/ppermute | solution.py:321
  128.7 1.7 %gram.3 = (f32[64,512]{1,0:T(8,128)S(1)}, bf16[64,512]{1,0:T(8,128)(2,1)S(1)}, bf16[64,512]{1,0:T(8,128)(2,1)S(1)}, bf16[64,512]{1,0:T(8,128)(2,1)S(1)}, bf16[64...) custom-call(s32[17]{0:T(128)S(1)} %stack.71.place_ref, ...), custom_call_target="tpu_custom_call" | custom-call | tf_op jit(solution)/shard_map/gram/pallas_call | solution.py:236
  130.4 5.5 %collective-permute-start.19 = (bf16[64,512]{1,0:T(8,128)(2,1)S(1)}, bf16[64,512]{1,0:T(8,128)(2,1)S(1)}, u32[]{:S(2)}, u32[]{:S(2)}) collective-permute-start(bf16[64,512]{1,0:T(8,128)(2,1)S(1)} %get-tuple-element.22), channel_id=1, source_target_pairs={{0,16},{4,20},{8,24},{12,28},{16,0},{20,4},{24,8},{28,12},{1,17},{... | collective-permute-start | bytes 196616 | tf_op jit(solution)/shard_map/ppermute | solution.py:22
  135.8 0.6 collective-permute-start.20
  136.4 4.5 %collective-permute-start.21 = (bf16[64,512]{1,0:T(8,128)(2,1)S(1)}, bf16[64,512]{1,0:T(8,128)(2,1)S(1)}, u32[]{:S(2)}, u32[]{:S(2)}) collective-permute-start(bf16[64,512]{1,0:T(8,128)(2,1)S(1)} %get-tuple-element.24), channel_id=1, source_target_pairs={{0,20},{4,24},{8,28},{12,0},{16,4},{20,8},{24,12},{28,16},{1,21},{... | collective-permute-start | bytes 196616 | tf_op jit(solution)/shard_map/ppermute | solution.py:22
  140.9 0.6 collective-permute-start.22
  141.5 3.6 %collective-permute-start.23 = (bf16[64,512]{1,0:T(8,128)(2,1)S(1)}, bf16[64,512]{1,0:T(8,128)(2,1)S(1)}, u32[]{:S(2)}, u32[]{:S(2)}) collective-permute-start(bf16[64,512]{1,0:T(8,128)(2,1)S(1)} %get-tuple-element.26), channel_id=1, source_target_pairs={{0,24},{4,28},{8,0},{12,4},{16,8},{20,12},{24,16},{28,20},{1,25},{... | collective-permute-start | bytes 196616 | tf_op jit(solution)/shard_map/ppermute | solution.py:22
  145.0 0.6 collective-permute-start.24
  145.6 2.7 %collective-permute-start.25 = (bf16[64,512]{1,0:T(8,128)(2,1)S(1)}, bf16[64,512]{1,0:T(8,128)(2,1)S(1)}, u32[]{:S(2)}, u32[]{:S(2)}) collective-permute-start(bf16[64,512]{1,0:T(8,128)(2,1)S(1)} %get-tuple-element.28), channel_id=1, source_target_pairs={{0,28},{4,0},{8,4},{12,8},{16,12},{20,16},{24,20},{28,24},{1,29},{... | collective-permute-start | bytes 196616 | tf_op jit(solution)/shard_map/ppermute | solution.py:22
  148.3 2.2 %collective-permute-done.24 = bf16[64,512]{1,0:T(8,128)(2,1)S(1)} collective-permute-done((bf16[64,512]{1,0:T(8,128)(2,1)S(1)}, bf16[64,512]{1,0:T(8,128)(2,1)S(1)}, u32[]{:S(2)}, u32[]{:S(2)}) %collective-permute-start.24) | collective-permute-done | bytes 65568 | tf_op jit(solution)/shard_map/ppermute | solution.py:22
  150.5 0.1 convert_add_fusion
  150.6 0.1 convert_reduce_fusion
  150.7 0.7 pad_maximum_fusion
  (24 shorter events, 0.1 us)
Async XLA Ops:
  0.0 40.2 %copy-start = (f32[4,128]{1,0:T(4,128)S(1)}, f32[4,128]{1,0:T(4,128)}, u32[]{:S(2)}) copy-start(f32[4,128]{1,0:T(4,128)} %wind_x_ref.5) | copy-start | bytes 6148
  0.0 40.2 %copy-start.1 = (f32[4,128]{1,0:T(4,128)S(1)}, f32[4,128]{1,0:T(4,128)}, u32[]{:S(2)}) copy-start(f32[4,128]{1,0:T(4,128)} %wind_y_ref.5) | copy-start | bytes 6148
  4.8 46.8 %all-to-all-start = ((bf16[64,8,256]{2,1,0:T(8,128)(2,1)}), bf16[64,8,256]{2,1,0:T(8,128)(2,1)S(1)}, u32[]{:S(2)}, u32[]{:S(2)}) async-start(bf16[64,8,256]{2,1,0:T(8,128)(2,1)} %fusion), calls=%async_computation | async-start | bytes 524288 | tf_op jit(solution)/shard_map/all_to_all | solution.py:26
  20.4 19.8 %collective-permute-start.2 = (bf16[1936,128]{1,0:T(8,128)(2,1)}, bf16[1936,128]{1,0:T(8,128)(2,1)S(1)}, u32[]{:S(2)}, u32[]{:S(2)}) collective-permute-start(bf16[1936,128]{1,0:T(8,128)(2,1)} %get-tuple-element.19), channel_id=1, source_target_pairs={{0,4},{4,8},{8,12},{12,16},{16,20},{20,24},{24,28},{28,32},{32,36}... | collective-permute-start | bytes 1486856 | tf_op jit(solution)/shard_map/ppermute | solution.py:22
  22.0 18.2 %collective-permute-start.3 = (bf16[1936,128]{1,0:T(8,128)(2,1)}, bf16[1936,128]{1,0:T(8,128)(2,1)S(1)}, u32[]{:S(2)}, u32[]{:S(2)}) collective-permute-start(bf16[1936,128]{1,0:T(8,128)(2,1)} %get-tuple-element.20), channel_id=1, source_target_pairs={{0,252},{4,0},{8,4},{12,8},{16,12},{20,16},{24,20},{28,24},{32,28}... | collective-permute-start | bytes 1486856 | tf_op jit(solution)/shard_map/ppermute | solution.py:22
  26.7 20.4 %collective-permute-start = (bf16[1168,128]{1,0:T(8,128)(2,1)}, bf16[1168,128]{1,0:T(8,128)(2,1)S(1)}, u32[]{:S(2)}, u32[]{:S(2)}) collective-permute-start(bf16[1168,128]{1,0:T(8,128)(2,1)} %get-tuple-element.17), channel_id=1, source_target_pairs={{0,4},{4,8},{8,12},{12,16},{16,20},{20,24},{24,28},{28,32},{32,36}... | collective-permute-start | bytes 897032 | tf_op jit(solution)/shard_map/ppermute | solution.py:22
  26.7 20.4 %collective-permute-start.1 = (bf16[1168,128]{1,0:T(8,128)(2,1)}, bf16[1168,128]{1,0:T(8,128)(2,1)S(1)}, u32[]{:S(2)}, u32[]{:S(2)}) collective-permute-start(bf16[1168,128]{1,0:T(8,128)(2,1)} %get-tuple-element.18), channel_id=1, source_target_pairs={{0,252},{4,0},{8,4},{12,8},{16,12},{20,16},{24,20},{28,24},{32,28}... | collective-permute-start | bytes 897032 | tf_op jit(solution)/shard_map/ppermute | solution.py:22
  51.6 9.5 %copy-start.2 = (bf16[128]{0:T(256)(128)(2,1)S(1)}, bf16[128]{0:T(256)(128)(2,1)}, u32[]{:S(2)}) copy-start(bf16[128]{0:T(256)(128)(2,1)} %param.11) | copy-start | bytes 772
  53.5 23.7 %all-to-all-start.1 = ((bf16[64,8,512]{2,1,0:T(8,128)(2,1)}), bf16[64,8,512]{2,1,0:T(8,128)(2,1)S(1)}, u32[]{:S(2)}, u32[]{:S(2)}) async-start(bf16[64,8,512]{2,1,0:T(8,128)(2,1)} %bitcast.24), calls=%async_computation.1 | async-start | bytes 1048576 | tf_op jit(solution)/shard_map/all_to_all | solution.py:26
  78.9 23.8 %all-to-all-start.2 = ((bf16[8,128,512]{2,1,0:T(8,128)(2,1)}), bf16[8,128,512]{2,1,0:T(8,128)(2,1)S(1)}, u32[]{:S(2)}, u32[]{:S(2)}) async-start(bf16[8,128,512]{2,1,0:T(8,128)(2,1)} %broadcast_in_dim.2), calls=%async_computation.2 | async-start | bytes 2097152 | tf_op jit(solution)/shard_map/all_to_all | solution.py:26
  82.5 13.3 %collective-permute-start.6 = (bf16[128,512]{1,0:T(8,128)(2,1)S(1)}, bf16[128,512]{1,0:T(8,128)(2,1)S(1)}, u32[]{:S(2)}, u32[]{:S(2)}) collective-permute-start(bf16[128,512]{1,0:T(8,128)(2,1)S(1)} %get-tuple-element.30), channel_id=1, source_target_pairs={{0,2},{1,66},{2,130},{3,194},{32,34},{33,98},{34,162},{35,226},{64... | collective-permute-start | bytes 393224 | tf_op jit(solution)/shard_map/ppermute | solution.py:309
  84.4 15.4 %collective-permute-start.7 = (bf16[128,512]{1,0:T(8,128)(2,1)S(1)}, bf16[128,512]{1,0:T(8,128)(2,1)S(1)}, u32[]{:S(2)}, u32[]{:S(2)}) collective-permute-start(bf16[128,512]{1,0:T(8,128)(2,1)S(1)} %get-tuple-element.29), channel_id=1, source_target_pairs={{0,34},{1,98},{2,162},{3,226},{32,2},{33,66},{34,130},{35,194},{64... | collective-permute-start | bytes 393224 | tf_op jit(solution)/shard_map/ppermute | solution.py:309
  86.7 14.1 %collective-permute-start.4 = (bf16[128,512]{1,0:T(8,128)(2,1)S(1)}, bf16[128,512]{1,0:T(8,128)(2,1)S(1)}, u32[]{:S(2)}, u32[]{:S(2)}) collective-permute-start(bf16[128,512]{1,0:T(8,128)(2,1)S(1)} %get-tuple-element.30), channel_id=1, source_target_pairs={{0,0},{1,64},{2,128},{3,192},{32,32},{33,96},{34,160},{35,224},{64... | collective-permute-start | bytes 393224 | tf_op jit(solution)/shard_map/ppermute | solution.py:309
  89.9 11.2 %collective-permute-start.5 = (bf16[128,512]{1,0:T(8,128)(2,1)S(1)}, bf16[128,512]{1,0:T(8,128)(2,1)S(1)}, u32[]{:S(2)}, u32[]{:S(2)}) collective-permute-start(bf16[128,512]{1,0:T(8,128)(2,1)S(1)} %get-tuple-element.29), channel_id=1, source_target_pairs={{0,32},{1,96},{2,160},{3,224},{32,0},{33,64},{34,128},{35,192},{64... | collective-permute-start | bytes 393224 | tf_op jit(solution)/shard_map/ppermute | solution.py:309
  95.7 6.0 %collective-permute-start.10 = (bf16[128,512]{1,0:T(8,128)(2,1)S(1)}, bf16[128,512]{1,0:T(8,128)(2,1)S(1)}, u32[]{:S(2)}, u32[]{:S(2)}) collective-permute-start(bf16[128,512]{1,0:T(8,128)(2,1)S(1)} %collective-permute-done.6.refs_2_), channel_id=1, source_target_pairs={{0,1},{1,0},{2,3},{3,2},{4,5},{5,4},{6,7},{7,6},{8,9},{9,8},{10,11... | collective-permute-start | bytes 393224 | tf_op jit(solution)/shard_map/ppermute | solution.py:22
  99.8 2.0 %collective-permute-start.11 = (bf16[128,512]{1,0:T(8,128)(2,1)S(1)}, bf16[128,512]{1,0:T(8,128)(2,1)S(1)}, u32[]{:S(2)}, u32[]{:S(2)}) collective-permute-start(bf16[128,512]{1,0:T(8,128)(2,1)S(1)} %collective-permute-done.7.refs_3_), channel_id=1, source_target_pairs={{0,1},{1,0},{2,3},{3,2},{4,5},{5,4},{6,7},{7,6},{8,9},{9,8},{10,11... | collective-permute-start | bytes 393224 | tf_op jit(solution)/shard_map/ppermute | solution.py:22
  100.8 1.3 collective-permute-start.8
  101.1 1.6 %collective-permute-start.9 = (bf16[128,512]{1,0:T(8,128)(2,1)S(1)}, bf16[128,512]{1,0:T(8,128)(2,1)S(1)}, u32[]{:S(2)}, u32[]{:S(2)}) collective-permute-start(bf16[128,512]{1,0:T(8,128)(2,1)S(1)} %collective-permute-done.5.refs_1_), channel_id=1, source_target_pairs={{0,1},{1,0},{2,3},{3,2},{4,5},{5,4},{6,7},{7,6},{8,9},{9,8},{10,11... | collective-permute-start | bytes 393224 | tf_op jit(solution)/shard_map/ppermute | solution.py:22
  105.0 45.6 %all-to-all-start.3 = ((bf16[8,64,512]{2,1,0:T(8,128)(2,1)}), bf16[8,64,512]{2,1,0:T(8,128)(2,1)S(1)}, u32[]{:S(2)}, u32[]{:S(2)}) async-start(bf16[8,64,512]{2,1,0:T(8,128)(2,1)} %bitcast.27), calls=%async_computation.3 | async-start | bytes 1048576 | tf_op jit(solution)/shard_map/all_to_all | solution.py:26
  108.9 8.3 %collective-permute-start.12 = (bf16[128,512]{1,0:T(8,128)(2,1)S(1)}, bf16[128,512]{1,0:T(8,128)(2,1)S(1)}, u32[]{:S(2)}, u32[]{:S(2)}) collective-permute-start(bf16[128,512]{1,0:T(8,128)(2,1)S(1)} %get-tuple-element.36.refs_8_), channel_id=1, source_target_pairs={{0,128},{128,0},{1,129},{129,1},{2,130},{130,2},{3,131},{131,3},{4... | collective-permute-start | bytes 393224 | tf_op jit(solution)/shard_map/ppermute | solution.py:22
  110.2 7.0 %collective-permute-start.13 = (bf16[128,512]{1,0:T(8,128)(2,1)S(1)}, bf16[128,512]{1,0:T(8,128)(2,1)S(1)}, u32[]{:S(2)}, u32[]{:S(2)}) collective-permute-start(bf16[128,512]{1,0:T(8,128)(2,1)S(1)} %get-tuple-element.36.refs_8_), channel_id=1, source_target_pairs={{0,32},{32,64},{64,96},{96,0},{1,33},{33,65},{65,97},{97,1},{2,34}... | collective-permute-start | bytes 393224 | tf_op jit(solution)/shard_map/ppermute | solution.py:22
  110.7 16.0 %collective-permute-start.14 = (bf16[128,512]{1,0:T(8,128)(2,1)S(1)}, bf16[128,512]{1,0:T(8,128)(2,1)S(1)}, u32[]{:S(2)}, u32[]{:S(2)}) collective-permute-start(bf16[128,512]{1,0:T(8,128)(2,1)S(1)} %get-tuple-element.36.refs_8_), channel_id=1, source_target_pairs={{0,64},{32,96},{64,0},{96,32},{1,65},{33,97},{65,1},{97,33},{2,66}... | collective-permute-start | bytes 393224 | tf_op jit(solution)/shard_map/ppermute | solution.py:22
  113.8 12.9 %collective-permute-start.15 = (bf16[128,512]{1,0:T(8,128)(2,1)S(1)}, bf16[128,512]{1,0:T(8,128)(2,1)S(1)}, u32[]{:S(2)}, u32[]{:S(2)}) collective-permute-start(bf16[128,512]{1,0:T(8,128)(2,1)S(1)} %get-tuple-element.36.refs_8_), channel_id=1, source_target_pairs={{0,96},{32,0},{64,32},{96,64},{1,97},{33,1},{65,33},{97,65},{2,98}... | collective-permute-start | bytes 393224 | tf_op jit(solution)/shard_map/ppermute | solution.py:22
  114.4 12.3 %collective-permute-start.16 = (bf16[128,512]{1,0:T(8,128)(2,1)S(1)}, bf16[128,512]{1,0:T(8,128)(2,1)S(1)}, u32[]{:S(2)}, u32[]{:S(2)}) collective-permute-start(bf16[128,512]{1,0:T(8,128)(2,1)S(1)} %get-tuple-element.36.refs_8_), channel_id=1, source_target_pairs={{0,160},{32,192},{64,224},{96,128},{128,32},{160,64},{192,96},{224... | collective-permute-start | bytes 393224 | tf_op jit(solution)/shard_map/ppermute | solution.py:321
  117.2 9.5 %collective-permute-start.17 = (bf16[128,512]{1,0:T(8,128)(2,1)S(1)}, bf16[128,512]{1,0:T(8,128)(2,1)S(1)}, u32[]{:S(2)}, u32[]{:S(2)}) collective-permute-start(bf16[128,512]{1,0:T(8,128)(2,1)S(1)} %get-tuple-element.36.refs_8_), channel_id=1, source_target_pairs={{0,192},{32,224},{64,128},{96,160},{128,64},{160,96},{192,0},{224,... | collective-permute-start | bytes 393224 | tf_op jit(solution)/shard_map/ppermute | solution.py:321
  117.2 11.5 %collective-permute-start.18 = (bf16[128,512]{1,0:T(8,128)(2,1)S(1)}, bf16[128,512]{1,0:T(8,128)(2,1)S(1)}, u32[]{:S(2)}, u32[]{:S(2)}) collective-permute-start(bf16[128,512]{1,0:T(8,128)(2,1)S(1)} %get-tuple-element.36.refs_8_), channel_id=1, source_target_pairs={{0,224},{32,128},{64,160},{96,192},{128,96},{160,0},{192,32},{224,... | collective-permute-start | bytes 393224 | tf_op jit(solution)/shard_map/ppermute | solution.py:321
  130.4 14.6 %collective-permute-start.19 = (bf16[64,512]{1,0:T(8,128)(2,1)S(1)}, bf16[64,512]{1,0:T(8,128)(2,1)S(1)}, u32[]{:S(2)}, u32[]{:S(2)}) collective-permute-start(bf16[64,512]{1,0:T(8,128)(2,1)S(1)} %get-tuple-element.22), channel_id=1, source_target_pairs={{0,16},{4,20},{8,24},{12,28},{16,0},{20,4},{24,8},{28,12},{1,17},{... | collective-permute-start | bytes 196616 | tf_op jit(solution)/shard_map/ppermute | solution.py:22
  135.8 9.7 %collective-permute-start.20 = (bf16[64,512]{1,0:T(8,128)(2,1)S(1)}, bf16[64,512]{1,0:T(8,128)(2,1)S(1)}, u32[]{:S(2)}, u32[]{:S(2)}) collective-permute-start(bf16[64,512]{1,0:T(8,128)(2,1)S(1)} %get-tuple-element.23), channel_id=1, source_target_pairs={{0,12},{4,16},{8,20},{12,24},{16,28},{20,0},{24,4},{28,8},{1,13},{... | collective-permute-start | bytes 196616 | tf_op jit(solution)/shard_map/ppermute | solution.py:22
  136.4 11.8 %collective-permute-start.21 = (bf16[64,512]{1,0:T(8,128)(2,1)S(1)}, bf16[64,512]{1,0:T(8,128)(2,1)S(1)}, u32[]{:S(2)}, u32[]{:S(2)}) collective-permute-start(bf16[64,512]{1,0:T(8,128)(2,1)S(1)} %get-tuple-element.24), channel_id=1, source_target_pairs={{0,20},{4,24},{8,28},{12,0},{16,4},{20,8},{24,12},{28,16},{1,21},{... | collective-permute-start | bytes 196616 | tf_op jit(solution)/shard_map/ppermute | solution.py:22
  140.9 7.4 %collective-permute-start.22 = (bf16[64,512]{1,0:T(8,128)(2,1)S(1)}, bf16[64,512]{1,0:T(8,128)(2,1)S(1)}, u32[]{:S(2)}, u32[]{:S(2)}) collective-permute-start(bf16[64,512]{1,0:T(8,128)(2,1)S(1)} %get-tuple-element.25), channel_id=1, source_target_pairs={{0,8},{4,12},{8,16},{12,20},{16,24},{20,28},{24,0},{28,4},{1,9},{5... | collective-permute-start | bytes 196616 | tf_op jit(solution)/shard_map/ppermute | solution.py:22
  141.5 6.8 %collective-permute-start.23 = (bf16[64,512]{1,0:T(8,128)(2,1)S(1)}, bf16[64,512]{1,0:T(8,128)(2,1)S(1)}, u32[]{:S(2)}, u32[]{:S(2)}) collective-permute-start(bf16[64,512]{1,0:T(8,128)(2,1)S(1)} %get-tuple-element.26), channel_id=1, source_target_pairs={{0,24},{4,28},{8,0},{12,4},{16,8},{20,12},{24,16},{28,20},{1,25},{... | collective-permute-start | bytes 196616 | tf_op jit(solution)/shard_map/ppermute | solution.py:22
  145.0 5.5 %collective-permute-start.24 = (bf16[64,512]{1,0:T(8,128)(2,1)S(1)}, bf16[64,512]{1,0:T(8,128)(2,1)S(1)}, u32[]{:S(2)}, u32[]{:S(2)}) collective-permute-start(bf16[64,512]{1,0:T(8,128)(2,1)S(1)} %get-tuple-element.27), channel_id=1, source_target_pairs={{0,4},{4,8},{8,12},{12,16},{16,20},{20,24},{24,28},{28,0},{1,5},{5... | collective-permute-start | bytes 196616 | tf_op jit(solution)/shard_map/ppermute | solution.py:22
  145.6 4.9 %collective-permute-start.25 = (bf16[64,512]{1,0:T(8,128)(2,1)S(1)}, bf16[64,512]{1,0:T(8,128)(2,1)S(1)}, u32[]{:S(2)}, u32[]{:S(2)}) collective-permute-start(bf16[64,512]{1,0:T(8,128)(2,1)S(1)} %get-tuple-element.28), channel_id=1, source_target_pairs={{0,28},{4,0},{8,4},{12,8},{16,12},{20,16},{24,20},{28,24},{1,29},{... | collective-permute-start | bytes 196616 | tf_op jit(solution)/shard_map/ppermute | solution.py:22

commit v5 on v2

--- a/solution.py
+++ b/solution.py
@@ -41,7 +41,7 @@
 
 
 def spans(tracers):
-    cut = tracers * 5 // 8
+    cut = tracers * 3 // 4
     return [(0, cut), (cut, tracers - cut)]
 
 
@@ -53,27 +53,14 @@
     return pl.pallas_call(edge_rows, out_shape=shapes, name="edges")(pulses, wind_x, wind_y)
 
 
-PIECE = 16
+PIECE = 64
 
 
 def transport_body(
-    skip, pulse_ref, a0, a1, a2, b0, b1, b2, a_winds, b_winds, wind_x_ref, wind_y_ref, *refs
+    pulse_ref, a0, a1, a2, b0, b1, b2, a_winds, b_winds, wind_x_ref, wind_y_ref, *refs
 ):
-    out_ref, coef_ref, fetched_ref, sems = refs[-4:]
+    out_ref, coef_ref = refs[-2:]
     count = out_ref.shape[0]
-    block = pl.program_id(0)
-
-    def fetch(i):
-        source = pulse_ref.at[pl.ds((skip + i) * 4 * count, 4 * count)]
-        return pltpu.make_async_copy(source, fetched_ref.at[i % 2], sems.at[i % 2])
-
-    @pl.when(block == 0)
-    def _():
-        fetch(block).start()
-
-    @pl.when(block + 1 < pl.num_programs(0))
-    def _():
-        fetch(block + 1).start()
 
     @pl.when(pl.program_id(0) == 0)
     def _():
@@ -94,13 +81,11 @@
             for w in range(8):
                 coef_ref[k * 8 + w] = jnp.broadcast_to(part[w : w + 1], (PIECE, 128))
 
-    fetch(block).wait()
-    slot = block % 2
     for piece in range(count // PIECE):
         at = piece * PIECE
         field = (
             [ref[at : at + PIECE].astype(jnp.float32) for ref in (a0, a1, a2)]
-            + [fetched_ref[slot, pl.ds(4 * at + r, PIECE, 4), :] for r in range(4)]
+            + [pulse_ref[pl.ds(4 * at + r, PIECE, 4), :] for r in range(4)]
             + [ref[at : at + PIECE].astype(jnp.float32) for ref in (b0, b1, b2)]
         )
         for step in range(STEPS):
@@ -120,7 +105,7 @@
             out_ref[at : at + PIECE, r * 128 : (r + 1) * 128] = field[r].astype(jnp.bfloat16)
 
 
-def transport(pulses, above, below, wind_x, wind_y, span, into=None, block=128):
+def transport(pulses, above, below, wind_x, wind_y, span, into=None, block=256):
     tracers = pulses.shape[0] // 4
     start, size = span
     skip, steps = start // block, size // block
@@ -130,7 +115,7 @@
     last = [pl.BlockSpec((16, 128), lambda i: (STEPS * size // 16, 0))] * 2
     wind = pl.BlockSpec((4, 128), lambda i: (0, 0))
     operands = [pulses, *[above] * 3, *[below] * 3, above, below, wind_x, wind_y]
-    specs = [pl.BlockSpec(memory_space=pltpu.HBM)] + halo + halo + last
+    specs = [pl.BlockSpec((4 * block, 128), lambda i: (skip + i, 0))] + halo + halo + last
     specs += [wind, wind]
     aliases = {}
     if into is not None:
@@ -138,15 +123,13 @@
         operands.append(into)
         specs.append(pl.BlockSpec(memory_space=pl.ANY))
     return pl.pallas_call(
-        functools.partial(transport_body, skip),
+        transport_body,
         grid=(steps,),
         in_specs=specs,
         out_specs=pl.BlockSpec((block, 512), lambda i: (skip + i, 0)),
         out_shape=jax.ShapeDtypeStruct((tracers, 512), jnp.bfloat16),
         scratch_shapes=[
             pltpu.VMEM((40, PIECE, 128), jnp.float32),
-            pltpu.VMEM((2, 4 * block, 128), jnp.float32),
-            pltpu.SemaphoreType.DMA((2,)),
         ],
         input_output_aliases=aliases,
         compiler_params=pltpu.CompilerParams(vmem_limit_bytes=GRANT),
@@ -280,6 +263,8 @@
     rows_in = exchanged(rows_out.reshape(cells, 2 * CAP, split), CELLS)
 
     jac_tile = jacobian(rows_in.reshape(cells * 2 * CAP, split), sampled)
+    precision = obs_precision.astype(jnp.float32)[:, None]
+    jac_tile, precision = lax.optimization_barrier((jac_tile, precision))
     jac_back = exchanged(jac_tile.reshape(cells, 2 * CAP, half), CELLS)
     jac_back = jac_back.reshape(cells * 2 * CAP, half)
     jac = [
@@ -288,7 +273,6 @@
         )
         for c in chosen
     ]
-    precision = obs_precision.astype(jnp.float32)[:, None]
     weighted = [(precision * j).astype(jnp.bfloat16) for j in jac]
     low, high = [j.astype(jnp.bfloat16) for j in jac]
 

time: 161 us -> 150 us (0.932)
  Pallas kernels: 20.2 us -> 16.1 us
  other arithmetic: 4.73 us -> 1.54 us
  starting transfers between devices: 77.7 us -> 75.6 us
    all_to_all x3, starting transfers between devices: 23.9 us -> 18.2 us  [exchanged(): return lax.all_to_all(value, axis, split_axis=0, concat_axis=0, tiled=True)]
    pallas_call x2, Pallas kernels: 11.4 us -> 7.24 us  [transport(): pl.pallas_call(transport_body, grid=(steps,), in_specs=specs, out_specs=p...]
    ppermute x27, starting transfers between devices: 49.8 us -> 53.3 us  [shifted(): lax.ppermute(value, axis, [(i, (i + steps) % count) for i in range(count)])]
    ppermute x27, waiting for transfers between devices: 33.8 us -> 30.4 us  [shifted(): lax.ppermute(value, axis, [(i, (i + steps) % count) for i in range(count)])]
    all_to_all x3, waiting for transfers between devices: 16 us -> 17.9 us  [exchanged(): return lax.all_to_all(value, axis, split_axis=0, concat_axis=0, tiled=True)]
  transfers between devices with their start and end apart: 32 -> 32, of which waited for: 14 -> 16; matrix products, arithmetic and copies ran while one was open for 0% -> 1% of each run, Pallas kernels for 10% -> 6%
where the time goes in v5:
time: 150 us
  starting transfers between devices  75.6 us (50%)
  waiting for transfers between devices  54.5 us (36%)
  Pallas kernels  16.1 us (11%)
  matrix products  1.61 us (1%)
  other arithmetic  1.54 us (1%)
    ppermute x27, starting transfers between devices, shifted(): lax.ppermute(value, axis, [(i, (i + steps) % count) for i in range(count)])  53.3 us
    ppermute x27, waiting for transfers between devices, shifted(): lax.ppermute(value, axis, [(i, (i + steps) % count) for i in range(count)])  30.4 us
    all_to_all x3, starting transfers between devices, exchanged(): return lax.all_to_all(value, axis, split_axis=0, concat_axis=0, tiled=True)  18.2 us
    all_to_all x3, waiting for transfers between devices, exchanged(): return lax.all_to_all(value, axis, split_axis=0, concat_axis=0, tiled=True)  17.9 us
    pallas_call x2, Pallas kernels, transport(): pl.pallas_call(transport_body, grid=(steps,), in_specs=specs, out_specs=p...  7.24 us
    pallas_call x2, Pallas kernels, gram_tile(): pl.pallas_call(functools.partial(gram_body, apart), in_specs=[pl.BlockSpe...  4.11 us
    ppermute x1, waiting for transfers between devices, on_device(): same = lax.ppermute(jnp.where(odd == 0, low, high), PLANE, to_same)  3.76 us
  transfers between devices with their start and end apart: 32, of which 16 were waited for; matrix products, arithmetic and copies ran while one was open for 1% of the time, Pallas kernels for 6%

profile of v5, /device:TPU:4, one launch (start us, length us, event | category | flops | bytes accessed | tf_op | source)
XLA Modules:
  0.0 149.8 jit_solution(7449159285523710033)
XLA Ops:
  0.0 3.0 %edges.1 = (bf16[2320,128]{1,0:T(8,128)(2,1)}, bf16[2320,128]{1,0:T(8,128)(2,1)}, bf16[784,128]{1,0:T(8,128)(2,1)}, bf16[784,128]{1,0:T(8,128)(2,1)}) custom-call(f32[4096,128]{1,0:T(8,128)} %bitcast.46, f32[4,128]{1,0:T(4,128)} %wind_x_ref.5, f32[4,128]{1,0:T(4,128)} %wind_y_ref.5), custom_call_target="tpu_custom_call" | custom-call | tf_op jit(solution)/shard_map/edges/pallas_call | solution.py:53
  3.0 1.9 %collective-permute-start.2 = (bf16[2320,128]{1,0:T(8,128)(2,1)}, bf16[2320,128]{1,0:T(8,128)(2,1)S(1)}, u32[]{:S(2)}, u32[]{:S(2)}) collective-permute-start(bf16[2320,128]{1,0:T(8,128)(2,1)} %get-tuple-element.21), channel_id=1, source_target_pairs={{0,4},{4,8},{8,12},{12,16},{16,20},{20,24},{24,28},{28,32},{32,36}... | collective-permute-start | bytes 1781768 | tf_op jit(solution)/shard_map/ppermute | solution.py:22
  4.9 7.0 %collective-permute-start.3 = (bf16[2320,128]{1,0:T(8,128)(2,1)}, bf16[2320,128]{1,0:T(8,128)(2,1)S(1)}, u32[]{:S(2)}, u32[]{:S(2)}) collective-permute-start(bf16[2320,128]{1,0:T(8,128)(2,1)} %get-tuple-element.22), channel_id=1, source_target_pairs={{0,252},{4,0},{8,4},{12,8},{16,12},{20,16},{24,20},{28,24},{32,28}... | collective-permute-start | bytes 1781768 | tf_op jit(solution)/shard_map/ppermute | solution.py:22
  11.9 0.2 convert_reduce_fusion.2
  12.1 0.1 convert_reduce_fusion.1
  12.2 0.1 fusion.8
  12.4 0.1 iota_compare_fusion
  12.5 1.1 fusion
  13.6 7.0 %all-to-all-start = ((bf16[64,8,256]{2,1,0:T(8,128)(2,1)}), bf16[64,8,256]{2,1,0:T(8,128)(2,1)S(1)}, u32[]{:S(2)}, u32[]{:S(2)}) async-start(bf16[64,8,256]{2,1,0:T(8,128)(2,1)} %fusion), calls=%async_computation | async-start | bytes 524288 | tf_op jit(solution)/shard_map/all_to_all | solution.py:26
  20.6 1.6 %collective-permute-start = (bf16[784,128]{1,0:T(8,128)(2,1)}, bf16[784,128]{1,0:T(8,128)(2,1)S(1)}, u32[]{:S(2)}, u32[]{:S(2)}) collective-permute-start(bf16[784,128]{1,0:T(8,128)(2,1)} %get-tuple-element.19), channel_id=1, source_target_pairs={{0,4},{4,8},{8,12},{12,16},{16,20},{20,24},{24,28},{28,32},{32,36}... | collective-permute-start | bytes 602120 | tf_op jit(solution)/shard_map/ppermute | solution.py:22
  22.3 4.7 %collective-permute-start.1 = (bf16[784,128]{1,0:T(8,128)(2,1)}, bf16[784,128]{1,0:T(8,128)(2,1)S(1)}, u32[]{:S(2)}, u32[]{:S(2)}) collective-permute-start(bf16[784,128]{1,0:T(8,128)(2,1)} %get-tuple-element.20), channel_id=1, source_target_pairs={{0,252},{4,0},{8,4},{12,8},{16,12},{20,16},{24,20},{28,24},{32,28}... | collective-permute-start | bytes 602120 | tf_op jit(solution)/shard_map/ppermute | solution.py:22
  26.9 2.5 %collective-permute-done.3.b0.b1.b2.b_winds = bf16[2320,128]{1,0:T(8,128)(2,1)S(1)} collective-permute-done((bf16[2320,128]{1,0:T(8,128)(2,1)}, bf16[2320,128]{1,0:T(8,128)(2,1)S(1)}, u32[]{:S(2)}, u32[]{:S(2)}) %collective-permute-start.3) | collective-permute-done | bytes 593952 | tf_op jit(solution)/shard_map/ppermute | solution.py:22
  29.4 5.0 %transport.2.refs_0_ = bf16[1024,512]{1,0:T(8,128)(2,1)S(1)} custom-call(f32[4096,128]{1,0:T(8,128)} %bitcast.47, bf16[2320,128]{1,0:T(8,128)(2,1)S(1)} %collective-permute-done.2.a0.a1.a2.a_winds, bf16[2320,128]{1,0:T(8,128)(2,1)S(1)} %collective-permute-done.2.a0.a1.a2.a_winds, bf16[2320,128]{1,0:T(8,128)(2,1)S(1)} %collective-permute-done.2.a0.a1.a2.a_winds, ...), custom_call_target="tpu_custom_call" | custom-call | tf_op jit(solution)/shard_map/transport/pallas_call | solution.py:125
  34.4 1.6 %collective-permute-done.a0.a1.a2.a_winds = bf16[784,128]{1,0:T(8,128)(2,1)S(1)} collective-permute-done((bf16[784,128]{1,0:T(8,128)(2,1)}, bf16[784,128]{1,0:T(8,128)(2,1)S(1)}, u32[]{:S(2)}, u32[]{:S(2)}) %collective-permute-start) | collective-permute-done | bytes 200736 | tf_op jit(solution)/shard_map/ppermute | solution.py:22
  36.0 2.2 %transport.3.low_ref.high_ref = bf16[1024,512]{1,0:T(8,128)(2,1)S(1)} custom-call(f32[4096,128]{1,0:T(8,128)} %bitcast.48, bf16[784,128]{1,0:T(8,128)(2,1)S(1)} %collective-permute-done.a0.a1.a2.a_winds, bf16[784,128]{1,0:T(8,128)(2,1)S(1)} %collective-permute-done.a0.a1.a2.a_winds, ...), custom_call_target="tpu_custom_call", output_to_operand_aliasing={{}: (11, {})} | custom-call | tf_op jit(solution)/shard_map/transport/pallas_call | solution.py:125
  38.3 1.8 %jacobian.1 = bf16[512,512]{1,0:T(8,128)(2,1)} custom-call(bf16[512,256]{1,0:T(8,128)(2,1)S(1)} %bitcast.45, bf16[1024,512]{1,0:T(8,128)(2,1)S(1)} %transport.3.low_ref.high_ref, bf16[1024,512]{1,0:T(8,128)(2,1)S(1)} %transport.3.low_ref.high_ref), custom_call_target="tpu_custom_call" | custom-call | tf_op jit(solution)/shard_map/jacobian/pallas_call | solution.py:164
  40.1 7.7 %all-to-all-start.1 = ((bf16[64,8,512]{2,1,0:T(8,128)(2,1)}), bf16[64,8,512]{2,1,0:T(8,128)(2,1)S(1)}, u32[]{:S(2)}, u32[]{:S(2)}) async-start(bf16[64,8,512]{2,1,0:T(8,128)(2,1)} %bitcast.25), calls=%async_computation.1 | async-start | bytes 1048576 | tf_op jit(solution)/shard_map/all_to_all | solution.py:26
  47.8 17.9 %all-to-all-done.1 = bf16[64,8,512]{2,1,0:T(8,128)(2,1)S(1)} async-done(((bf16[64,8,512]{2,1,0:T(8,128)(2,1)}), bf16[64,8,512]{2,1,0:T(8,128)(2,1)S(1)}, u32[]{:S(2)}, u32[]{:S(2)}) %all-to-all-start.1) | async-done | bytes 524320 | tf_op jit(solution)/shard_map/all_to_all | solution.py:26
  65.7 0.3 fusion.3
  66.0 0.3 broadcast_select_fusion
  66.2 2.9 %collective-permute-start.4 = (bf16[128,512]{1,0:T(8,128)(2,1)S(1)}, bf16[128,512]{1,0:T(8,128)(2,1)S(1)}, u32[]{:S(2)}, u32[]{:S(2)}) collective-permute-start(bf16[128,512]{1,0:T(8,128)(2,1)S(1)} %get-tuple-element.34), channel_id=1, source_target_pairs={{0,0},{1,64},{2,128},{3,192},{32,32},{33,96},{34,160},{35,224},{64... | collective-permute-start | bytes 393224 | tf_op jit(solution)/shard_map/ppermute | solution.py:286
  69.2 1.1 collective-permute-start.5
  70.3 3.8 %collective-permute-done.4.same_ref = bf16[128,512]{1,0:T(8,128)(2,1)S(1)} collective-permute-done((bf16[128,512]{1,0:T(8,128)(2,1)S(1)}, bf16[128,512]{1,0:T(8,128)(2,1)S(1)}, u32[]{:S(2)}, u32[]{:S(2)}) %collective-permute-start.4) | collective-permute-done | bytes 131104 | tf_op jit(solution)/shard_map/ppermute | solution.py:286
  74.1 2.4 %collective-permute-done.5.cross_ref = bf16[128,512]{1,0:T(8,128)(2,1)S(1)} collective-permute-done((bf16[128,512]{1,0:T(8,128)(2,1)S(1)}, bf16[128,512]{1,0:T(8,128)(2,1)S(1)}, u32[]{:S(2)}, u32[]{:S(2)}) %collective-permute-start.5) | collective-permute-done | bytes 131104 | tf_op jit(solution)/shard_map/ppermute | solution.py:287
  76.6 0.1 collective-permute-start.6
  76.7 8.6 %collective-permute-done.6.across_ref = bf16[256,512]{1,0:T(8,128)(2,1)S(1)} collective-permute-done((bf16[256,512]{1,0:T(8,128)(2,1)S(1)}, bf16[256,512]{1,0:T(8,128)(2,1)S(1)}, u32[]{:S(2)}, u32[]{:S(2)}) %collective-permute-start.6) | collective-permute-done | bytes 262176 | tf_op jit(solution)/shard_map/ppermute | solution.py:22
  85.3 0.1 collective-permute-start.7
  85.4 0.1 multiply_convert_fusion.1
  85.5 2.2 %collective-permute-start.8 = (bf16[128,512]{1,0:T(8,128)(2,1)S(1)}, bf16[128,512]{1,0:T(8,128)(2,1)S(1)}, u32[]{:S(2)}, u32[]{:S(2)}) collective-permute-start(bf16[128,512]{1,0:T(8,128)(2,1)S(1)} %get-tuple-element.39.refs_0_), channel_id=1, source_target_pairs={{0,128},{128,0},{1,129},{129,1},{2,130},{130,2},{3,131},{131,3},{4... | collective-permute-start | bytes 393224 | tf_op jit(solution)/shard_map/ppermute | solution.py:22
  87.7 0.1 collective-permute-start.10
  87.9 3.1 %collective-permute-start.11 = (bf16[128,512]{1,0:T(8,128)(2,1)S(1)}, bf16[128,512]{1,0:T(8,128)(2,1)S(1)}, u32[]{:S(2)}, u32[]{:S(2)}) collective-permute-start(bf16[128,512]{1,0:T(8,128)(2,1)S(1)} %get-tuple-element.39.refs_0_), channel_id=1, source_target_pairs={{0,96},{32,0},{64,32},{96,64},{1,97},{33,1},{65,33},{97,65},{2,98}... | collective-permute-start | bytes 393224 | tf_op jit(solution)/shard_map/ppermute | solution.py:22
  91.0 0.6 collective-permute-done.8.refs_1_
  91.5 1.1 collective-permute-start.12
  92.6 3.0 %collective-permute-done.10.refs_3_ = bf16[128,512]{1,0:T(8,128)(2,1)S(1)} collective-permute-done((bf16[128,512]{1,0:T(8,128)(2,1)S(1)}, bf16[128,512]{1,0:T(8,128)(2,1)S(1)}, u32[]{:S(2)}, u32[]{:S(2)}) %collective-permute-start.10) | collective-permute-done | bytes 131104 | tf_op jit(solution)/shard_map/ppermute | solution.py:22
  95.6 0.1 collective-permute-start.13
  95.7 0.2 collective-permute-done.11.refs_4_
  95.9 2.9 %collective-permute-start.14 = (bf16[128,512]{1,0:T(8,128)(2,1)S(1)}, bf16[128,512]{1,0:T(8,128)(2,1)S(1)}, u32[]{:S(2)}, u32[]{:S(2)}) collective-permute-start(bf16[128,512]{1,0:T(8,128)(2,1)S(1)} %collective-permute-done.8.refs_1_), channel_id=1, source_target_pairs={{0,96},{32,0},{64,32},{96,64},{1,97},{33,1},{65,33},{97,65},{2,98}... | collective-permute-start | bytes 393224 | tf_op jit(solution)/shard_map/ppermute | solution.py:22
  98.8 0.1 stack.71.place_ref
  98.9 4.3 %collective-permute-done.12.refs_5_ = bf16[128,512]{1,0:T(8,128)(2,1)S(1)} collective-permute-done((bf16[128,512]{1,0:T(8,128)(2,1)S(1)}, bf16[128,512]{1,0:T(8,128)(2,1)S(1)}, u32[]{:S(2)}, u32[]{:S(2)}) %collective-permute-start.12) | collective-permute-done | bytes 131104 | tf_op jit(solution)/shard_map/ppermute | solution.py:22
  103.2 2.4 %gram.2 = bf16[512,512]{1,0:T(8,128)(2,1)} custom-call(s32[17]{0:T(128)S(1)} %stack.71.place_ref, bf16[128,512]{1,0:T(8,128)(2,1)S(1)} %collective-permute-done.4.same_ref, bf16[128,512]{1,0:T(8,128)(2,1)S(1)} %collective-permute-done.5.cross_ref, bf16[256,512]{1,0:T(8,128)(2,1)S(1)} %collective-permute-done.6.across_ref, ...), custom_call_target="tpu_custom_call" | custom-call | tf_op jit(solution)/shard_map/gram/pallas_call | solution.py:217
  105.6 3.5 %all-to-all-start.2 = ((bf16[8,64,512]{2,1,0:T(8,128)(2,1)}), bf16[8,64,512]{2,1,0:T(8,128)(2,1)S(1)}, u32[]{:S(2)}, u32[]{:S(2)}) async-start(bf16[8,64,512]{2,1,0:T(8,128)(2,1)} %bitcast.28), calls=%async_computation.2 | async-start | bytes 1048576 | tf_op jit(solution)/shard_map/all_to_all | solution.py:26
  109.1 1.7 %collective-permute-start.15 = (bf16[128,512]{1,0:T(8,128)(2,1)S(1)}, bf16[128,512]{1,0:T(8,128)(2,1)S(1)}, u32[]{:S(2)}, u32[]{:S(2)}) collective-permute-start(bf16[128,512]{1,0:T(8,128)(2,1)S(1)} %get-tuple-element.40.refs_0_), channel_id=1, source_target_pairs={{0,128},{128,0},{1,129},{129,1},{2,130},{130,2},{3,131},{131,3},{4... | collective-permute-start | bytes 393224 | tf_op jit(solution)/shard_map/ppermute | solution.py:22
  110.9 1.0 collective-permute-start.16
  111.9 3.5 %collective-permute-start.17 = (bf16[128,512]{1,0:T(8,128)(2,1)S(1)}, bf16[128,512]{1,0:T(8,128)(2,1)S(1)}, u32[]{:S(2)}, u32[]{:S(2)}) collective-permute-start(bf16[128,512]{1,0:T(8,128)(2,1)S(1)} %get-tuple-element.40.refs_0_), channel_id=1, source_target_pairs={{0,64},{32,96},{64,0},{96,32},{1,65},{33,97},{65,1},{97,33},{2,66}... | collective-permute-start | bytes 393224 | tf_op jit(solution)/shard_map/ppermute | solution.py:22
  115.4 2.0 %collective-permute-start.19 = (bf16[128,512]{1,0:T(8,128)(2,1)S(1)}, bf16[128,512]{1,0:T(8,128)(2,1)S(1)}, u32[]{:S(2)}, u32[]{:S(2)}) collective-permute-start(bf16[128,512]{1,0:T(8,128)(2,1)S(1)} %collective-permute-done.15.refs_1_), channel_id=1, source_target_pairs={{0,32},{32,64},{64,96},{96,0},{1,33},{33,65},{65,97},{97,1},{2,34}... | collective-permute-start | bytes 393224 | tf_op jit(solution)/shard_map/ppermute | solution.py:22
  117.4 1.6 %collective-permute-start.20 = (bf16[128,512]{1,0:T(8,128)(2,1)S(1)}, bf16[128,512]{1,0:T(8,128)(2,1)S(1)}, u32[]{:S(2)}, u32[]{:S(2)}) collective-permute-start(bf16[128,512]{1,0:T(8,128)(2,1)S(1)} %collective-permute-done.15.refs_1_), channel_id=1, source_target_pairs={{0,64},{32,96},{64,0},{96,32},{1,65},{33,97},{65,1},{97,33},{2,66}... | collective-permute-start | bytes 393224 | tf_op jit(solution)/shard_map/ppermute | solution.py:22
  119.0 1.3 collective-permute-start.21
  120.3 2.2 %collective-permute-done.17.refs_3_ = bf16[128,512]{1,0:T(8,128)(2,1)S(1)} collective-permute-done((bf16[128,512]{1,0:T(8,128)(2,1)S(1)}, bf16[128,512]{1,0:T(8,128)(2,1)S(1)}, u32[]{:S(2)}, u32[]{:S(2)}) %collective-permute-start.17) | collective-permute-done | bytes 131104 | tf_op jit(solution)/shard_map/ppermute | solution.py:22
  122.5 1.4 collective-permute-done.19.refs_5_
  123.9 2.9 %collective-permute-done.20.refs_6_ = bf16[128,512]{1,0:T(8,128)(2,1)S(1)} collective-permute-done((bf16[128,512]{1,0:T(8,128)(2,1)S(1)}, bf16[128,512]{1,0:T(8,128)(2,1)S(1)}, u32[]{:S(2)}, u32[]{:S(2)}) %collective-permute-start.20) | collective-permute-done | bytes 131104 | tf_op jit(solution)/shard_map/ppermute | solution.py:22
  126.9 1.7 %gram.3 = (f32[64,512]{1,0:T(8,128)S(1)}, bf16[64,512]{1,0:T(8,128)(2,1)S(1)}, bf16[64,512]{1,0:T(8,128)(2,1)S(1)}, bf16[64,512]{1,0:T(8,128)(2,1)S(1)}, bf16[64...) custom-call(s32[17]{0:T(128)S(1)} %stack.71.place_ref, ...), custom_call_target="tpu_custom_call" | custom-call | tf_op jit(solution)/shard_map/gram/pallas_call | solution.py:217
  128.6 5.6 %collective-permute-start.22 = (bf16[64,512]{1,0:T(8,128)(2,1)S(1)}, bf16[64,512]{1,0:T(8,128)(2,1)S(1)}, u32[]{:S(2)}, u32[]{:S(2)}) collective-permute-start(bf16[64,512]{1,0:T(8,128)(2,1)S(1)} %get-tuple-element.26), channel_id=1, source_target_pairs={{0,16},{4,20},{8,24},{12,28},{16,0},{20,4},{24,8},{28,12},{1,17},{... | collective-permute-start | bytes 196616 | tf_op jit(solution)/shard_map/ppermute | solution.py:22
  134.1 0.6 collective-permute-start.23
  134.7 4.5 %collective-permute-start.24 = (bf16[64,512]{1,0:T(8,128)(2,1)S(1)}, bf16[64,512]{1,0:T(8,128)(2,1)S(1)}, u32[]{:S(2)}, u32[]{:S(2)}) collective-permute-start(bf16[64,512]{1,0:T(8,128)(2,1)S(1)} %get-tuple-element.28), channel_id=1, source_target_pairs={{0,20},{4,24},{8,28},{12,0},{16,4},{20,8},{24,12},{28,16},{1,21},{... | collective-permute-start | bytes 196616 | tf_op jit(solution)/shard_map/ppermute | solution.py:22
  139.2 0.6 collective-permute-start.25
  139.7 3.6 %collective-permute-start.26 = (bf16[64,512]{1,0:T(8,128)(2,1)S(1)}, bf16[64,512]{1,0:T(8,128)(2,1)S(1)}, u32[]{:S(2)}, u32[]{:S(2)}) collective-permute-start(bf16[64,512]{1,0:T(8,128)(2,1)S(1)} %get-tuple-element.30), channel_id=1, source_target_pairs={{0,24},{4,28},{8,0},{12,4},{16,8},{20,12},{24,16},{28,20},{1,25},{... | collective-permute-start | bytes 196616 | tf_op jit(solution)/shard_map/ppermute | solution.py:22
  143.3 0.6 collective-permute-start.27
  143.9 0.7 collective-permute-done.23
  144.6 1.9 %collective-permute-start.28 = (bf16[64,512]{1,0:T(8,128)(2,1)S(1)}, bf16[64,512]{1,0:T(8,128)(2,1)S(1)}, u32[]{:S(2)}, u32[]{:S(2)}) collective-permute-start(bf16[64,512]{1,0:T(8,128)(2,1)S(1)} %get-tuple-element.32), channel_id=1, source_target_pairs={{0,28},{4,0},{8,4},{12,8},{16,12},{20,16},{24,20},{28,24},{1,29},{... | collective-permute-start | bytes 196616 | tf_op jit(solution)/shard_map/ppermute | solution.py:22
  146.6 2.2 %collective-permute-done.27 = bf16[64,512]{1,0:T(8,128)(2,1)S(1)} collective-permute-done((bf16[64,512]{1,0:T(8,128)(2,1)S(1)}, bf16[64,512]{1,0:T(8,128)(2,1)S(1)}, u32[]{:S(2)}, u32[]{:S(2)}) %collective-permute-start.27) | collective-permute-done | bytes 65568 | tf_op jit(solution)/shard_map/ppermute | solution.py:22
  148.8 0.1 collective-permute-done.28
  148.9 0.1 convert_add_fusion
  149.0 0.1 convert_reduce_fusion
  149.0 0.7 pad_maximum_fusion.2
  (33 shorter events, 0.1 us)
Async XLA Ops:
  0.0 29.4 %copy-start = (f32[4,128]{1,0:T(4,128)S(1)}, f32[4,128]{1,0:T(4,128)}, u32[]{:S(2)}) copy-start(f32[4,128]{1,0:T(4,128)} %wind_x_ref.5) | copy-start | bytes 6148
  0.0 29.4 %copy-start.1 = (f32[4,128]{1,0:T(4,128)S(1)}, f32[4,128]{1,0:T(4,128)}, u32[]{:S(2)}) copy-start(f32[4,128]{1,0:T(4,128)} %wind_y_ref.5) | copy-start | bytes 6148
  0.0 11.9 %copy-start.3 = (s32[128,1]{0,1:T(1,128)S(1)}, s32[128,1]{0,1:T(1,128)}, u32[]{:S(2)}) copy-start(s32[128,1]{0,1:T(1,128)} %param.9) | copy-start | bytes 1540
  0.0 12.1 %copy-start.2 = (bf16[128,512]{1,0:T(8,128)(2,1)S(1)}, bf16[128,512]{1,0:T(8,128)(2,1)}, u32[]{:S(2)}) copy-start(bf16[128,512]{1,0:T(8,128)(2,1)} %param.10) | copy-start | bytes 393220
  0.0 26.9 %copy-start.4 = (bf16[128]{0:T(256)(128)(2,1)S(1)}, bf16[128]{0:T(256)(128)(2,1)}, u32[]{:S(2)}) copy-start(bf16[128]{0:T(256)(128)(2,1)} %param.11) | copy-start | bytes 772
  3.0 24.0 %collective-permute-start.2 = (bf16[2320,128]{1,0:T(8,128)(2,1)}, bf16[2320,128]{1,0:T(8,128)(2,1)S(1)}, u32[]{:S(2)}, u32[]{:S(2)}) collective-permute-start(bf16[2320,128]{1,0:T(8,128)(2,1)} %get-tuple-element.21), channel_id=1, source_target_pairs={{0,4},{4,8},{8,12},{12,16},{16,20},{20,24},{24,28},{28,32},{32,36}... | collective-permute-start | bytes 1781768 | tf_op jit(solution)/shard_map/ppermute | solution.py:22
  4.9 24.5 %collective-permute-start.3 = (bf16[2320,128]{1,0:T(8,128)(2,1)}, bf16[2320,128]{1,0:T(8,128)(2,1)S(1)}, u32[]{:S(2)}, u32[]{:S(2)}) collective-permute-start(bf16[2320,128]{1,0:T(8,128)(2,1)} %get-tuple-element.22), channel_id=1, source_target_pairs={{0,252},{4,0},{8,4},{12,8},{16,12},{20,16},{24,20},{28,24},{32,28}... | collective-permute-start | bytes 1781768 | tf_op jit(solution)/shard_map/ppermute | solution.py:22
  13.6 24.7 %all-to-all-start = ((bf16[64,8,256]{2,1,0:T(8,128)(2,1)}), bf16[64,8,256]{2,1,0:T(8,128)(2,1)S(1)}, u32[]{:S(2)}, u32[]{:S(2)}) async-start(bf16[64,8,256]{2,1,0:T(8,128)(2,1)} %fusion), calls=%async_computation | async-start | bytes 524288 | tf_op jit(solution)/shard_map/all_to_all | solution.py:26
  20.6 15.4 %collective-permute-start = (bf16[784,128]{1,0:T(8,128)(2,1)}, bf16[784,128]{1,0:T(8,128)(2,1)S(1)}, u32[]{:S(2)}, u32[]{:S(2)}) collective-permute-start(bf16[784,128]{1,0:T(8,128)(2,1)} %get-tuple-element.19), channel_id=1, source_target_pairs={{0,4},{4,8},{8,12},{12,16},{16,20},{20,24},{24,28},{28,32},{32,36}... | collective-permute-start | bytes 602120 | tf_op jit(solution)/shard_map/ppermute | solution.py:22
  22.3 13.8 %collective-permute-start.1 = (bf16[784,128]{1,0:T(8,128)(2,1)}, bf16[784,128]{1,0:T(8,128)(2,1)S(1)}, u32[]{:S(2)}, u32[]{:S(2)}) collective-permute-start(bf16[784,128]{1,0:T(8,128)(2,1)} %get-tuple-element.20), channel_id=1, source_target_pairs={{0,252},{4,0},{8,4},{12,8},{16,12},{20,16},{24,20},{28,24},{32,28}... | collective-permute-start | bytes 602120 | tf_op jit(solution)/shard_map/ppermute | solution.py:22
  40.1 25.6 %all-to-all-start.1 = ((bf16[64,8,512]{2,1,0:T(8,128)(2,1)}), bf16[64,8,512]{2,1,0:T(8,128)(2,1)S(1)}, u32[]{:S(2)}, u32[]{:S(2)}) async-start(bf16[64,8,512]{2,1,0:T(8,128)(2,1)} %bitcast.25), calls=%async_computation.1 | async-start | bytes 1048576 | tf_op jit(solution)/shard_map/all_to_all | solution.py:26
  66.2 7.8 %collective-permute-start.4 = (bf16[128,512]{1,0:T(8,128)(2,1)S(1)}, bf16[128,512]{1,0:T(8,128)(2,1)S(1)}, u32[]{:S(2)}, u32[]{:S(2)}) collective-permute-start(bf16[128,512]{1,0:T(8,128)(2,1)S(1)} %get-tuple-element.34), channel_id=1, source_target_pairs={{0,0},{1,64},{2,128},{3,192},{32,32},{33,96},{34,160},{35,224},{64... | collective-permute-start | bytes 393224 | tf_op jit(solution)/shard_map/ppermute | solution.py:286
  69.2 7.4 %collective-permute-start.5 = (bf16[128,512]{1,0:T(8,128)(2,1)S(1)}, bf16[128,512]{1,0:T(8,128)(2,1)S(1)}, u32[]{:S(2)}, u32[]{:S(2)}) collective-permute-start(bf16[128,512]{1,0:T(8,128)(2,1)S(1)} %get-tuple-element.33), channel_id=1, source_target_pairs={{0,32},{1,96},{2,160},{3,224},{32,0},{33,64},{34,128},{35,192},{64... | collective-permute-start | bytes 393224 | tf_op jit(solution)/shard_map/ppermute | solution.py:287
  76.6 8.7 %collective-permute-start.6 = (bf16[256,512]{1,0:T(8,128)(2,1)S(1)}, bf16[256,512]{1,0:T(8,128)(2,1)S(1)}, u32[]{:S(2)}, u32[]{:S(2)}) collective-permute-start(bf16[256,512]{1,0:T(8,128)(2,1)S(1)} %pad_maximum_fusion.1), channel_id=1, source_target_pairs={{0,2},{2,0},{1,3},{3,1},{4,6},{6,4},{5,7},{7,5},{8,10},{10,8},{9,1... | collective-permute-start | bytes 786440 | tf_op jit(solution)/shard_map/ppermute | solution.py:22
  85.3 17.9 %collective-permute-start.7 = (bf16[512,512]{1,0:T(8,128)(2,1)S(1)}, bf16[512,512]{1,0:T(8,128)(2,1)S(1)}, u32[]{:S(2)}, u32[]{:S(2)}) collective-permute-start(bf16[512,512]{1,0:T(8,128)(2,1)S(1)} %pad_maximum_fusion), channel_id=1, source_target_pairs={{0,1},{1,0},{2,3},{3,2},{4,5},{5,4},{6,7},{7,6},{8,9},{9,8},{10,11... | collective-permute-start | bytes 1572872 | tf_op jit(solution)/shard_map/ppermute | solution.py:22
  85.5 6.0 %collective-permute-start.8 = (bf16[128,512]{1,0:T(8,128)(2,1)S(1)}, bf16[128,512]{1,0:T(8,128)(2,1)S(1)}, u32[]{:S(2)}, u32[]{:S(2)}) collective-permute-start(bf16[128,512]{1,0:T(8,128)(2,1)S(1)} %get-tuple-element.39.refs_0_), channel_id=1, source_target_pairs={{0,128},{128,0},{1,129},{129,1},{2,130},{130,2},{3,131},{131,3},{4... | collective-permute-start | bytes 393224 | tf_op jit(solution)/shard_map/ppermute | solution.py:22
  87.7 7.9 %collective-permute-start.10 = (bf16[128,512]{1,0:T(8,128)(2,1)S(1)}, bf16[128,512]{1,0:T(8,128)(2,1)S(1)}, u32[]{:S(2)}, u32[]{:S(2)}) collective-permute-start(bf16[128,512]{1,0:T(8,128)(2,1)S(1)} %get-tuple-element.39.refs_0_), channel_id=1, source_target_pairs={{0,64},{32,96},{64,0},{96,32},{1,65},{33,97},{65,1},{97,33},{2,66}... | collective-permute-start | bytes 393224 | tf_op jit(solution)/shard_map/ppermute | solution.py:22
  87.9 8.1 %collective-permute-start.11 = (bf16[128,512]{1,0:T(8,128)(2,1)S(1)}, bf16[128,512]{1,0:T(8,128)(2,1)S(1)}, u32[]{:S(2)}, u32[]{:S(2)}) collective-permute-start(bf16[128,512]{1,0:T(8,128)(2,1)S(1)} %get-tuple-element.39.refs_0_), channel_id=1, source_target_pairs={{0,96},{32,0},{64,32},{96,64},{1,97},{33,1},{65,33},{97,65},{2,98}... | collective-permute-start | bytes 393224 | tf_op jit(solution)/shard_map/ppermute | solution.py:22
  91.0 8.0 %collective-permute-start.9 = (bf16[128,512]{1,0:T(8,128)(2,1)S(1)}, bf16[128,512]{1,0:T(8,128)(2,1)S(1)}, u32[]{:S(2)}, u32[]{:S(2)}) collective-permute-start(bf16[128,512]{1,0:T(8,128)(2,1)S(1)} %get-tuple-element.39.refs_0_), channel_id=1, source_target_pairs={{0,32},{32,64},{64,96},{96,0},{1,33},{33,65},{65,97},{97,1},{2,34}... | collective-permute-start | bytes 393224 | tf_op jit(solution)/shard_map/ppermute | solution.py:22
  91.5 11.7 %collective-permute-start.12 = (bf16[128,512]{1,0:T(8,128)(2,1)S(1)}, bf16[128,512]{1,0:T(8,128)(2,1)S(1)}, u32[]{:S(2)}, u32[]{:S(2)}) collective-permute-start(bf16[128,512]{1,0:T(8,128)(2,1)S(1)} %collective-permute-done.8.refs_1_), channel_id=1, source_target_pairs={{0,32},{32,64},{64,96},{96,0},{1,33},{33,65},{65,97},{97,1},{2,34}... | collective-permute-start | bytes 393224 | tf_op jit(solution)/shard_map/ppermute | solution.py:22
  95.6 7.6 %collective-permute-start.13 = (bf16[128,512]{1,0:T(8,128)(2,1)S(1)}, bf16[128,512]{1,0:T(8,128)(2,1)S(1)}, u32[]{:S(2)}, u32[]{:S(2)}) collective-permute-start(bf16[128,512]{1,0:T(8,128)(2,1)S(1)} %collective-permute-done.8.refs_1_), channel_id=1, source_target_pairs={{0,64},{32,96},{64,0},{96,32},{1,65},{33,97},{65,1},{97,33},{2,66}... | collective-permute-start | bytes 393224 | tf_op jit(solution)/shard_map/ppermute | solution.py:22
  95.9 7.3 %collective-permute-start.14 = (bf16[128,512]{1,0:T(8,128)(2,1)S(1)}, bf16[128,512]{1,0:T(8,128)(2,1)S(1)}, u32[]{:S(2)}, u32[]{:S(2)}) collective-permute-start(bf16[128,512]{1,0:T(8,128)(2,1)S(1)} %collective-permute-done.8.refs_1_), channel_id=1, source_target_pairs={{0,96},{32,0},{64,32},{96,64},{1,97},{33,1},{65,33},{97,65},{2,98}... | collective-permute-start | bytes 393224 | tf_op jit(solution)/shard_map/ppermute | solution.py:22
  105.6 43.3 %all-to-all-start.2 = ((bf16[8,64,512]{2,1,0:T(8,128)(2,1)}), bf16[8,64,512]{2,1,0:T(8,128)(2,1)S(1)}, u32[]{:S(2)}, u32[]{:S(2)}) async-start(bf16[8,64,512]{2,1,0:T(8,128)(2,1)} %bitcast.28), calls=%async_computation.2 | async-start | bytes 1048576 | tf_op jit(solution)/shard_map/all_to_all | solution.py:26
  109.1 6.2 %collective-permute-start.15 = (bf16[128,512]{1,0:T(8,128)(2,1)S(1)}, bf16[128,512]{1,0:T(8,128)(2,1)S(1)}, u32[]{:S(2)}, u32[]{:S(2)}) collective-permute-start(bf16[128,512]{1,0:T(8,128)(2,1)S(1)} %get-tuple-element.40.refs_0_), channel_id=1, source_target_pairs={{0,128},{128,0},{1,129},{129,1},{2,130},{130,2},{3,131},{131,3},{4... | collective-permute-start | bytes 393224 | tf_op jit(solution)/shard_map/ppermute | solution.py:22
  110.9 8.1 %collective-permute-start.16 = (bf16[128,512]{1,0:T(8,128)(2,1)S(1)}, bf16[128,512]{1,0:T(8,128)(2,1)S(1)}, u32[]{:S(2)}, u32[]{:S(2)}) collective-permute-start(bf16[128,512]{1,0:T(8,128)(2,1)S(1)} %get-tuple-element.40.refs_0_), channel_id=1, source_target_pairs={{0,32},{32,64},{64,96},{96,0},{1,33},{33,65},{65,97},{97,1},{2,34}... | collective-permute-start | bytes 393224 | tf_op jit(solution)/shard_map/ppermute | solution.py:22
  111.9 10.7 %collective-permute-start.17 = (bf16[128,512]{1,0:T(8,128)(2,1)S(1)}, bf16[128,512]{1,0:T(8,128)(2,1)S(1)}, u32[]{:S(2)}, u32[]{:S(2)}) collective-permute-start(bf16[128,512]{1,0:T(8,128)(2,1)S(1)} %get-tuple-element.40.refs_0_), channel_id=1, source_target_pairs={{0,64},{32,96},{64,0},{96,32},{1,65},{33,97},{65,1},{97,33},{2,66}... | collective-permute-start | bytes 393224 | tf_op jit(solution)/shard_map/ppermute | solution.py:22
  115.4 7.2 %collective-permute-start.18 = (bf16[128,512]{1,0:T(8,128)(2,1)S(1)}, bf16[128,512]{1,0:T(8,128)(2,1)S(1)}, u32[]{:S(2)}, u32[]{:S(2)}) collective-permute-start(bf16[128,512]{1,0:T(8,128)(2,1)S(1)} %get-tuple-element.40.refs_0_), channel_id=1, source_target_pairs={{0,96},{32,0},{64,32},{96,64},{1,97},{33,1},{65,33},{97,65},{2,98}... | collective-permute-start | bytes 393224 | tf_op jit(solution)/shard_map/ppermute | solution.py:22
  115.4 8.5 %collective-permute-start.19 = (bf16[128,512]{1,0:T(8,128)(2,1)S(1)}, bf16[128,512]{1,0:T(8,128)(2,1)S(1)}, u32[]{:S(2)}, u32[]{:S(2)}) collective-permute-start(bf16[128,512]{1,0:T(8,128)(2,1)S(1)} %collective-permute-done.15.refs_1_), channel_id=1, source_target_pairs={{0,32},{32,64},{64,96},{96,0},{1,33},{33,65},{65,97},{97,1},{2,34}... | collective-permute-start | bytes 393224 | tf_op jit(solution)/shard_map/ppermute | solution.py:22
  117.4 9.5 %collective-permute-start.20 = (bf16[128,512]{1,0:T(8,128)(2,1)S(1)}, bf16[128,512]{1,0:T(8,128)(2,1)S(1)}, u32[]{:S(2)}, u32[]{:S(2)}) collective-permute-start(bf16[128,512]{1,0:T(8,128)(2,1)S(1)} %collective-permute-done.15.refs_1_), channel_id=1, source_target_pairs={{0,64},{32,96},{64,0},{96,32},{1,65},{33,97},{65,1},{97,33},{2,66}... | collective-permute-start | bytes 393224 | tf_op jit(solution)/shard_map/ppermute | solution.py:22
  119.0 7.9 %collective-permute-start.21 = (bf16[128,512]{1,0:T(8,128)(2,1)S(1)}, bf16[128,512]{1,0:T(8,128)(2,1)S(1)}, u32[]{:S(2)}, u32[]{:S(2)}) collective-permute-start(bf16[128,512]{1,0:T(8,128)(2,1)S(1)} %collective-permute-done.15.refs_1_), channel_id=1, source_target_pairs={{0,96},{32,0},{64,32},{96,64},{1,97},{33,1},{65,33},{97,65},{2,98}... | collective-permute-start | bytes 393224 | tf_op jit(solution)/shard_map/ppermute | solution.py:22
  128.6 14.7 %collective-permute-start.22 = (bf16[64,512]{1,0:T(8,128)(2,1)S(1)}, bf16[64,512]{1,0:T(8,128)(2,1)S(1)}, u32[]{:S(2)}, u32[]{:S(2)}) collective-permute-start(bf16[64,512]{1,0:T(8,128)(2,1)S(1)} %get-tuple-element.26), channel_id=1, source_target_pairs={{0,16},{4,20},{8,24},{12,28},{16,0},{20,4},{24,8},{28,12},{1,17},{... | collective-permute-start | bytes 196616 | tf_op jit(solution)/shard_map/ppermute | solution.py:22
  134.1 10.5 %collective-permute-start.23 = (bf16[64,512]{1,0:T(8,128)(2,1)S(1)}, bf16[64,512]{1,0:T(8,128)(2,1)S(1)}, u32[]{:S(2)}, u32[]{:S(2)}) collective-permute-start(bf16[64,512]{1,0:T(8,128)(2,1)S(1)} %get-tuple-element.27), channel_id=1, source_target_pairs={{0,12},{4,16},{8,20},{12,24},{16,28},{20,0},{24,4},{28,8},{1,13},{... | collective-permute-start | bytes 196616 | tf_op jit(solution)/shard_map/ppermute | solution.py:22
  134.7 11.8 %collective-permute-start.24 = (bf16[64,512]{1,0:T(8,128)(2,1)S(1)}, bf16[64,512]{1,0:T(8,128)(2,1)S(1)}, u32[]{:S(2)}, u32[]{:S(2)}) collective-permute-start(bf16[64,512]{1,0:T(8,128)(2,1)S(1)} %get-tuple-element.28), channel_id=1, source_target_pairs={{0,20},{4,24},{8,28},{12,0},{16,4},{20,8},{24,12},{28,16},{1,21},{... | collective-permute-start | bytes 196616 | tf_op jit(solution)/shard_map/ppermute | solution.py:22
  139.2 7.4 %collective-permute-start.25 = (bf16[64,512]{1,0:T(8,128)(2,1)S(1)}, bf16[64,512]{1,0:T(8,128)(2,1)S(1)}, u32[]{:S(2)}, u32[]{:S(2)}) collective-permute-start(bf16[64,512]{1,0:T(8,128)(2,1)S(1)} %get-tuple-element.29), channel_id=1, source_target_pairs={{0,8},{4,12},{8,16},{12,20},{16,24},{20,28},{24,0},{28,4},{1,9},{5... | collective-permute-start | bytes 196616 | tf_op jit(solution)/shard_map/ppermute | solution.py:22
  139.7 6.8 %collective-permute-start.26 = (bf16[64,512]{1,0:T(8,128)(2,1)S(1)}, bf16[64,512]{1,0:T(8,128)(2,1)S(1)}, u32[]{:S(2)}, u32[]{:S(2)}) collective-permute-start(bf16[64,512]{1,0:T(8,128)(2,1)S(1)} %get-tuple-element.30), channel_id=1, source_target_pairs={{0,24},{4,28},{8,0},{12,4},{16,8},{20,12},{24,16},{28,20},{1,25},{... | collective-permute-start | bytes 196616 | tf_op jit(solution)/shard_map/ppermute | solution.py:22
  143.3 5.5 %collective-permute-start.27 = (bf16[64,512]{1,0:T(8,128)(2,1)S(1)}, bf16[64,512]{1,0:T(8,128)(2,1)S(1)}, u32[]{:S(2)}, u32[]{:S(2)}) collective-permute-start(bf16[64,512]{1,0:T(8,128)(2,1)S(1)} %get-tuple-element.31), channel_id=1, source_target_pairs={{0,4},{4,8},{8,12},{12,16},{16,20},{20,24},{24,28},{28,0},{1,5},{5... | collective-permute-start | bytes 196616 | tf_op jit(solution)/shard_map/ppermute | solution.py:22
  144.6 4.3 %collective-permute-start.28 = (bf16[64,512]{1,0:T(8,128)(2,1)S(1)}, bf16[64,512]{1,0:T(8,128)(2,1)S(1)}, u32[]{:S(2)}, u32[]{:S(2)}) collective-permute-start(bf16[64,512]{1,0:T(8,128)(2,1)S(1)} %get-tuple-element.32), channel_id=1, source_target_pairs={{0,28},{4,0},{8,4},{12,8},{16,12},{20,16},{24,20},{28,24},{1,29},{... | collective-permute-start | bytes 196616 | tf_op jit(solution)/shard_map/ppermute | solution.py:22

commit v6 on v5

--- a/solution.py
+++ b/solution.py
@@ -263,8 +263,21 @@
     rows_in = exchanged(rows_out.reshape(cells, 2 * CAP, split), CELLS)
 
     jac_tile = jacobian(rows_in.reshape(cells * 2 * CAP, split), sampled)
+    group = lax.axis_size(XY)
+    peers = lax.axis_size(TRACERS)
+    deep = lax.axis_size("y")
+    here = lax.axis_index(XY)
+    odd = here % 2
+    xl, y = lax.axis_index("xl"), lax.axis_index("y")
+    owners = [here, (1 - xl) * deep + y]
+    owners += [xl * deep + (y - d) % deep for d in range(1, deep)]
+    owners += [(1 - xl) * deep + (y - d) % deep for d in range(1, deep)]
+    tracer = lax.axis_index(TRACERS)
+    row_owners = [2 * (tracer ^ flip) + (odd ^ s) for flip in (0, 2, 1, 3) for s in (0, 1)]
+    place = jnp.stack(row_owners + owners + [lax.axis_index("z")]).astype(jnp.int32)
     precision = obs_precision.astype(jnp.float32)[:, None]
-    jac_tile, precision = lax.optimization_barrier((jac_tile, precision))
+    even = odd == 0
+    jac_tile, precision, place, even = lax.optimization_barrier((jac_tile, precision, place, even))
     jac_back = exchanged(jac_tile.reshape(cells, 2 * CAP, half), CELLS)
     jac_back = jac_back.reshape(cells * 2 * CAP, half)
     jac = [
@@ -276,19 +289,14 @@
     weighted = [(precision * j).astype(jnp.bfloat16) for j in jac]
     low, high = [j.astype(jnp.bfloat16) for j in jac]
 
-    group = lax.axis_size(XY)
-    peers = lax.axis_size(TRACERS)
-    here = lax.axis_index(XY)
-    odd = here % 2
     pairs = [(i // peers, i % peers) for i in range(group * peers)]
     to_same = [(a * peers + q, (2 * q + a % 2) * peers + a // 2) for a, q in pairs]
     to_cross = [(a * peers + q, (2 * q + 1 - a % 2) * peers + a // 2) for a, q in pairs]
-    same = lax.ppermute(jnp.where(odd == 0, low, high), PLANE, to_same)
-    cross = lax.ppermute(jnp.where(odd == 0, high, low), PLANE, to_cross)
+    same = lax.ppermute(jnp.where(even, low, high), PLANE, to_same)
+    cross = lax.ppermute(jnp.where(even, high, low), PLANE, to_cross)
     across = shifted(jnp.concatenate([same, cross], axis=0), "xh", 1)
     other = shifted(jnp.concatenate([same, cross, across], axis=0), "core", 1)
 
-    deep = lax.axis_size("y")
     cols = []
     for part, value in enumerate(weighted):
         beside = shifted(value, "xl", 1)
@@ -296,13 +304,6 @@
         for source in (value, beside):
             for d in range(1, deep):
                 cols[part].append(shifted(source, "y", d))
-    xl, y = lax.axis_index("xl"), lax.axis_index("y")
-    owners = [here, (1 - xl) * deep + y]
-    owners += [xl * deep + (y - d) % deep for d in range(1, deep)]
-    owners += [(1 - xl) * deep + (y - d) % deep for d in range(1, deep)]
-    tracer = lax.axis_index(TRACERS)
-    row_owners = [2 * (tracer ^ flip) + (odd ^ s) for flip in (0, 2, 1, 3) for s in (0, 1)]
-    place = jnp.stack(row_owners + owners + [lax.axis_index("z")]).astype(jnp.int32)
 
     depth = lax.axis_size("z")
     tile = gram_tile(place, same, cross, across, other, cols[0], 0)[0]

time: 150 us -> 149 us (level)
  blocking collectives: 0 us -> 25.4 us
  waiting for transfers between devices: 54.5 us -> 35.4 us
  starting transfers between devices: 75.6 us -> 69.2 us
    all_to_all x0 -> x1, blocking collectives: none -> 25.4 us  [exchanged(): return lax.all_to_all(value, axis, split_axis=0, concat_axis=0, tiled=True)]
    all_to_all x3 -> x2, waiting for transfers between devices: 17.9 us -> 0.01 us  [exchanged(): return lax.all_to_all(value, axis, split_axis=0, concat_axis=0, tiled=True)]
    all_to_all x3 -> x2, starting transfers between devices: 18.2 us -> 10.9 us  [exchanged(): return lax.all_to_all(value, axis, split_axis=0, concat_axis=0, tiled=True)]
  transfers between devices with their start and end apart: 32 -> 31, of which waited for: 16 -> 15; matrix products, arithmetic and copies ran while one was open for 1% -> 1% of each run, Pallas kernels for 6% -> 6%
where the time goes in v6:
time: 149 us
  starting transfers between devices  69.2 us (46%)
  waiting for transfers between devices  35.4 us (24%)
  blocking collectives  25.4 us (17%)
  Pallas kernels  15.4 us (10%)
  matrix products  1.6 us (1%)
  other arithmetic  1.54 us (1%)
    ppermute x27, starting transfers between devices, shifted(): lax.ppermute(value, axis, [(i, (i + steps) % count) for i in range(count)])  54.2 us
    ppermute x27, waiting for transfers between devices, shifted(): lax.ppermute(value, axis, [(i, (i + steps) % count) for i in range(count)])  29.2 us
    all_to_all x1, blocking collectives, exchanged(): return lax.all_to_all(value, axis, split_axis=0, concat_axis=0, tiled=True)  25.4 us
    all_to_all x2, starting transfers between devices, exchanged(): return lax.all_to_all(value, axis, split_axis=0, concat_axis=0, tiled=True)  10.9 us
    pallas_call x2, Pallas kernels, transport(): pl.pallas_call(transport_body, grid=(steps,), in_specs=specs, out_specs=p...  7.24 us
    pallas_call x2, Pallas kernels, gram_tile(): pl.pallas_call(functools.partial(gram_body, apart), in_specs=[pl.BlockSpe...  4.12 us
    ppermute x1, waiting for transfers between devices, on_device(): same = lax.ppermute(jnp.where(even, low, high), PLANE, to_same)  3.74 us
  transfers between devices with their start and end apart: 31, of which 15 were waited for; matrix products, arithmetic and copies ran while one was open for 1% of the time, Pallas kernels for 6%

profile of v6, /device:TPU:4, one launch (start us, length us, event | category | flops | bytes accessed | tf_op | source)
XLA Modules:
  0.0 148.9 jit_solution(2349424805907764085)
XLA Ops:
  0.0 3.0 %edges.1 = (bf16[2320,128]{1,0:T(8,128)(2,1)}, bf16[2320,128]{1,0:T(8,128)(2,1)}, bf16[784,128]{1,0:T(8,128)(2,1)}, bf16[784,128]{1,0:T(8,128)(2,1)}) custom-call(f32[4096,128]{1,0:T(8,128)} %bitcast.47, f32[4,128]{1,0:T(4,128)} %wind_x_ref.5, f32[4,128]{1,0:T(4,128)} %wind_y_ref.5), custom_call_target="tpu_custom_call" | custom-call | tf_op jit(solution)/shard_map/edges/pallas_call | solution.py:53
  3.0 1.9 %collective-permute-start.2 = (bf16[2320,128]{1,0:T(8,128)(2,1)}, bf16[2320,128]{1,0:T(8,128)(2,1)S(1)}, u32[]{:S(2)}, u32[]{:S(2)}) collective-permute-start(bf16[2320,128]{1,0:T(8,128)(2,1)} %get-tuple-element.23), channel_id=1, source_target_pairs={{0,4},{4,8},{8,12},{12,16},{16,20},{20,24},{24,28},{28,32},{32,36}... | collective-permute-start | bytes 1781768 | tf_op jit(solution)/shard_map/ppermute | solution.py:22
  4.9 7.0 %collective-permute-start.3 = (bf16[2320,128]{1,0:T(8,128)(2,1)}, bf16[2320,128]{1,0:T(8,128)(2,1)S(1)}, u32[]{:S(2)}, u32[]{:S(2)}) collective-permute-start(bf16[2320,128]{1,0:T(8,128)(2,1)} %get-tuple-element.24), channel_id=1, source_target_pairs={{0,252},{4,0},{8,4},{12,8},{16,12},{20,16},{24,20},{28,24},{32,28}... | collective-permute-start | bytes 1781768 | tf_op jit(solution)/shard_map/ppermute | solution.py:22
  12.0 0.2 convert_reduce_fusion.2
  12.2 0.1 convert_reduce_fusion.1
  12.3 0.1 fusion.8
  12.4 0.1 iota_compare_fusion
  12.5 1.1 fusion
  13.6 7.0 %all-to-all-start = ((bf16[64,8,256]{2,1,0:T(8,128)(2,1)}), bf16[64,8,256]{2,1,0:T(8,128)(2,1)S(1)}, u32[]{:S(2)}, u32[]{:S(2)}) async-start(bf16[64,8,256]{2,1,0:T(8,128)(2,1)} %fusion), calls=%async_computation | async-start | bytes 524288 | tf_op jit(solution)/shard_map/all_to_all | solution.py:26
  20.6 1.6 %collective-permute-start = (bf16[784,128]{1,0:T(8,128)(2,1)}, bf16[784,128]{1,0:T(8,128)(2,1)S(1)}, u32[]{:S(2)}, u32[]{:S(2)}) collective-permute-start(bf16[784,128]{1,0:T(8,128)(2,1)} %get-tuple-element.21), channel_id=1, source_target_pairs={{0,4},{4,8},{8,12},{12,16},{16,20},{20,24},{24,28},{28,32},{32,36}... | collective-permute-start | bytes 602120 | tf_op jit(solution)/shard_map/ppermute | solution.py:22
  22.3 4.7 %collective-permute-start.1 = (bf16[784,128]{1,0:T(8,128)(2,1)}, bf16[784,128]{1,0:T(8,128)(2,1)S(1)}, u32[]{:S(2)}, u32[]{:S(2)}) collective-permute-start(bf16[784,128]{1,0:T(8,128)(2,1)} %get-tuple-element.22), channel_id=1, source_target_pairs={{0,252},{4,0},{8,4},{12,8},{16,12},{20,16},{24,20},{28,24},{32,28}... | collective-permute-start | bytes 602120 | tf_op jit(solution)/shard_map/ppermute | solution.py:22
  27.0 0.1 stack.71.place_ref
  27.1 2.4 %collective-permute-done.3.b0.b1.b2.b_winds = bf16[2320,128]{1,0:T(8,128)(2,1)S(1)} collective-permute-done((bf16[2320,128]{1,0:T(8,128)(2,1)}, bf16[2320,128]{1,0:T(8,128)(2,1)S(1)}, u32[]{:S(2)}, u32[]{:S(2)}) %collective-permute-start.3) | collective-permute-done | bytes 593952 | tf_op jit(solution)/shard_map/ppermute | solution.py:22
  29.4 5.0 %transport.2.refs_0_ = bf16[1024,512]{1,0:T(8,128)(2,1)S(1)} custom-call(f32[4096,128]{1,0:T(8,128)} %bitcast.48, bf16[2320,128]{1,0:T(8,128)(2,1)S(1)} %collective-permute-done.2.a0.a1.a2.a_winds, bf16[2320,128]{1,0:T(8,128)(2,1)S(1)} %collective-permute-done.2.a0.a1.a2.a_winds, bf16[2320,128]{1,0:T(8,128)(2,1)S(1)} %collective-permute-done.2.a0.a1.a2.a_winds, ...), custom_call_target="tpu_custom_call" | custom-call | tf_op jit(solution)/shard_map/transport/pallas_call | solution.py:125
  34.5 1.6 %collective-permute-done.a0.a1.a2.a_winds = bf16[784,128]{1,0:T(8,128)(2,1)S(1)} collective-permute-done((bf16[784,128]{1,0:T(8,128)(2,1)}, bf16[784,128]{1,0:T(8,128)(2,1)S(1)}, u32[]{:S(2)}, u32[]{:S(2)}) %collective-permute-start) | collective-permute-done | bytes 200736 | tf_op jit(solution)/shard_map/ppermute | solution.py:22
  36.1 2.2 %transport.3.low_ref.high_ref = bf16[1024,512]{1,0:T(8,128)(2,1)S(1)} custom-call(f32[4096,128]{1,0:T(8,128)} %bitcast.49, bf16[784,128]{1,0:T(8,128)(2,1)S(1)} %collective-permute-done.a0.a1.a2.a_winds, bf16[784,128]{1,0:T(8,128)(2,1)S(1)} %collective-permute-done.a0.a1.a2.a_winds, ...), custom_call_target="tpu_custom_call", output_to_operand_aliasing={{}: (11, {})} | custom-call | tf_op jit(solution)/shard_map/transport/pallas_call | solution.py:125
  38.3 0.0 all-to-all-done
  38.3 1.1 jacobian.1
  39.4 25.4 %all_to_all.15 = bf16[64,8,512]{2,1,0:T(8,128)(2,1)S(1)} all-to-all(bf16[64,8,512]{2,1,0:T(8,128)(2,1)S(1)} %bitcast.45), channel_id=1, replica_groups=mesh['xl'=2,'y'=4,'z'=8,'xh'=2,'core'=2] {'xl','y','z'}, dimensions={0} | all-to-all | bytes 1048576 | tf_op jit(solution)/shard_map/all_to_all | solution.py:26
  64.8 0.3 fusion.3
  65.1 0.3 broadcast_select_fusion
  65.4 2.9 %collective-permute-start.4 = (bf16[128,512]{1,0:T(8,128)(2,1)S(1)}, bf16[128,512]{1,0:T(8,128)(2,1)S(1)}, u32[]{:S(2)}, u32[]{:S(2)}) collective-permute-start(bf16[128,512]{1,0:T(8,128)(2,1)S(1)} %get-tuple-element.38), channel_id=1, source_target_pairs={{0,0},{1,64},{2,128},{3,192},{32,32},{33,96},{34,160},{35,224},{64... | collective-permute-start | bytes 393224 | tf_op jit(solution)/shard_map/ppermute | solution.py:295
  68.3 1.2 collective-permute-start.5
  69.4 3.7 %collective-permute-done.4.same_ref = bf16[128,512]{1,0:T(8,128)(2,1)S(1)} collective-permute-done((bf16[128,512]{1,0:T(8,128)(2,1)S(1)}, bf16[128,512]{1,0:T(8,128)(2,1)S(1)}, u32[]{:S(2)}, u32[]{:S(2)}) %collective-permute-start.4) | collective-permute-done | bytes 131104 | tf_op jit(solution)/shard_map/ppermute | solution.py:295
  73.2 2.5 %collective-permute-done.5.cross_ref = bf16[128,512]{1,0:T(8,128)(2,1)S(1)} collective-permute-done((bf16[128,512]{1,0:T(8,128)(2,1)S(1)}, bf16[128,512]{1,0:T(8,128)(2,1)S(1)}, u32[]{:S(2)}, u32[]{:S(2)}) %collective-permute-start.5) | collective-permute-done | bytes 131104 | tf_op jit(solution)/shard_map/ppermute | solution.py:296
  75.7 0.1 collective-permute-start.6
  75.8 8.6 %collective-permute-done.6.across_ref = bf16[256,512]{1,0:T(8,128)(2,1)S(1)} collective-permute-done((bf16[256,512]{1,0:T(8,128)(2,1)S(1)}, bf16[256,512]{1,0:T(8,128)(2,1)S(1)}, u32[]{:S(2)}, u32[]{:S(2)}) %collective-permute-start.6) | collective-permute-done | bytes 262176 | tf_op jit(solution)/shard_map/ppermute | solution.py:22
  84.5 0.1 collective-permute-start.7
  84.6 0.1 multiply_convert_fusion.1
  84.7 1.3 collective-permute-start.8
  86.0 1.0 collective-permute-start.10
  87.0 3.1 %collective-permute-start.11 = (bf16[128,512]{1,0:T(8,128)(2,1)S(1)}, bf16[128,512]{1,0:T(8,128)(2,1)S(1)}, u32[]{:S(2)}, u32[]{:S(2)}) collective-permute-start(bf16[128,512]{1,0:T(8,128)(2,1)S(1)} %get-tuple-element.43.refs_0_), channel_id=1, source_target_pairs={{0,96},{32,0},{64,32},{96,64},{1,97},{33,1},{65,33},{97,65},{2,98}... | collective-permute-start | bytes 393224 | tf_op jit(solution)/shard_map/ppermute | solution.py:22
  90.1 0.6 collective-permute-done.8.refs_1_
  90.6 1.0 collective-permute-start.12
  91.7 2.2 %collective-permute-done.10.refs_3_ = bf16[128,512]{1,0:T(8,128)(2,1)S(1)} collective-permute-done((bf16[128,512]{1,0:T(8,128)(2,1)S(1)}, bf16[128,512]{1,0:T(8,128)(2,1)S(1)}, u32[]{:S(2)}, u32[]{:S(2)}) %collective-permute-start.10) | collective-permute-done | bytes 131104 | tf_op jit(solution)/shard_map/ppermute | solution.py:22
  93.9 1.0 collective-permute-start.13
  94.8 0.2 collective-permute-done.11.refs_4_
  95.1 2.9 %collective-permute-start.14 = (bf16[128,512]{1,0:T(8,128)(2,1)S(1)}, bf16[128,512]{1,0:T(8,128)(2,1)S(1)}, u32[]{:S(2)}, u32[]{:S(2)}) collective-permute-start(bf16[128,512]{1,0:T(8,128)(2,1)S(1)} %collective-permute-done.8.refs_1_), channel_id=1, source_target_pairs={{0,96},{32,0},{64,32},{96,64},{1,97},{33,1},{65,33},{97,65},{2,98}... | collective-permute-start | bytes 393224 | tf_op jit(solution)/shard_map/ppermute | solution.py:22
  98.0 3.9 %collective-permute-done.12.refs_5_ = bf16[128,512]{1,0:T(8,128)(2,1)S(1)} collective-permute-done((bf16[128,512]{1,0:T(8,128)(2,1)S(1)}, bf16[128,512]{1,0:T(8,128)(2,1)S(1)}, u32[]{:S(2)}, u32[]{:S(2)}) %collective-permute-start.12) | collective-permute-done | bytes 131104 | tf_op jit(solution)/shard_map/ppermute | solution.py:22
  101.9 2.4 %gram.2 = bf16[512,512]{1,0:T(8,128)(2,1)} custom-call(s32[17]{0:T(128)S(1)} %stack.71.place_ref, bf16[128,512]{1,0:T(8,128)(2,1)S(1)} %collective-permute-done.4.same_ref, bf16[128,512]{1,0:T(8,128)(2,1)S(1)} %collective-permute-done.5.cross_ref, bf16[256,512]{1,0:T(8,128)(2,1)S(1)} %collective-permute-done.6.across_ref, ...), custom_call_target="tpu_custom_call" | custom-call | tf_op jit(solution)/shard_map/gram/pallas_call | solution.py:217
  104.3 3.9 %all-to-all-start.2 = ((bf16[8,64,512]{2,1,0:T(8,128)(2,1)}), bf16[8,64,512]{2,1,0:T(8,128)(2,1)S(1)}, u32[]{:S(2)}, u32[]{:S(2)}) async-start(bf16[8,64,512]{2,1,0:T(8,128)(2,1)} %bitcast.28), calls=%async_computation.2 | async-start | bytes 1048576 | tf_op jit(solution)/shard_map/all_to_all | solution.py:26
  108.2 1.8 %collective-permute-start.15 = (bf16[128,512]{1,0:T(8,128)(2,1)S(1)}, bf16[128,512]{1,0:T(8,128)(2,1)S(1)}, u32[]{:S(2)}, u32[]{:S(2)}) collective-permute-start(bf16[128,512]{1,0:T(8,128)(2,1)S(1)} %get-tuple-element.44.refs_0_), channel_id=1, source_target_pairs={{0,128},{128,0},{1,129},{129,1},{2,130},{130,2},{3,131},{131,3},{4... | collective-permute-start | bytes 393224 | tf_op jit(solution)/shard_map/ppermute | solution.py:22
  110.0 1.0 collective-permute-start.16
  111.0 3.5 %collective-permute-start.17 = (bf16[128,512]{1,0:T(8,128)(2,1)S(1)}, bf16[128,512]{1,0:T(8,128)(2,1)S(1)}, u32[]{:S(2)}, u32[]{:S(2)}) collective-permute-start(bf16[128,512]{1,0:T(8,128)(2,1)S(1)} %get-tuple-element.44.refs_0_), channel_id=1, source_target_pairs={{0,64},{32,96},{64,0},{96,32},{1,65},{33,97},{65,1},{97,33},{2,66}... | collective-permute-start | bytes 393224 | tf_op jit(solution)/shard_map/ppermute | solution.py:22
  114.5 2.0 %collective-permute-start.19 = (bf16[128,512]{1,0:T(8,128)(2,1)S(1)}, bf16[128,512]{1,0:T(8,128)(2,1)S(1)}, u32[]{:S(2)}, u32[]{:S(2)}) collective-permute-start(bf16[128,512]{1,0:T(8,128)(2,1)S(1)} %collective-permute-done.15.refs_1_), channel_id=1, source_target_pairs={{0,32},{32,64},{64,96},{96,0},{1,33},{33,65},{65,97},{97,1},{2,34}... | collective-permute-start | bytes 393224 | tf_op jit(solution)/shard_map/ppermute | solution.py:22
  116.5 1.6 %collective-permute-start.20 = (bf16[128,512]{1,0:T(8,128)(2,1)S(1)}, bf16[128,512]{1,0:T(8,128)(2,1)S(1)}, u32[]{:S(2)}, u32[]{:S(2)}) collective-permute-start(bf16[128,512]{1,0:T(8,128)(2,1)S(1)} %collective-permute-done.15.refs_1_), channel_id=1, source_target_pairs={{0,64},{32,96},{64,0},{96,32},{1,65},{33,97},{65,1},{97,33},{2,66}... | collective-permute-start | bytes 393224 | tf_op jit(solution)/shard_map/ppermute | solution.py:22
  118.1 1.3 collective-permute-start.21
  119.4 2.2 %collective-permute-done.17.refs_3_ = bf16[128,512]{1,0:T(8,128)(2,1)S(1)} collective-permute-done((bf16[128,512]{1,0:T(8,128)(2,1)S(1)}, bf16[128,512]{1,0:T(8,128)(2,1)S(1)}, u32[]{:S(2)}, u32[]{:S(2)}) %collective-permute-start.17) | collective-permute-done | bytes 131104 | tf_op jit(solution)/shard_map/ppermute | solution.py:22
  121.7 1.4 collective-permute-done.19.refs_5_
  123.0 2.9 %collective-permute-done.20.refs_6_ = bf16[128,512]{1,0:T(8,128)(2,1)S(1)} collective-permute-done((bf16[128,512]{1,0:T(8,128)(2,1)S(1)}, bf16[128,512]{1,0:T(8,128)(2,1)S(1)}, u32[]{:S(2)}, u32[]{:S(2)}) %collective-permute-start.20) | collective-permute-done | bytes 131104 | tf_op jit(solution)/shard_map/ppermute | solution.py:22
  126.0 1.7 %gram.3 = (f32[64,512]{1,0:T(8,128)S(1)}, bf16[64,512]{1,0:T(8,128)(2,1)S(1)}, bf16[64,512]{1,0:T(8,128)(2,1)S(1)}, bf16[64,512]{1,0:T(8,128)(2,1)S(1)}, bf16[64...) custom-call(s32[17]{0:T(128)S(1)} %stack.71.place_ref, ...), custom_call_target="tpu_custom_call" | custom-call | tf_op jit(solution)/shard_map/gram/pallas_call | solution.py:217
  127.7 5.6 %collective-permute-start.22 = (bf16[64,512]{1,0:T(8,128)(2,1)S(1)}, bf16[64,512]{1,0:T(8,128)(2,1)S(1)}, u32[]{:S(2)}, u32[]{:S(2)}) collective-permute-start(bf16[64,512]{1,0:T(8,128)(2,1)S(1)} %get-tuple-element.30), channel_id=1, source_target_pairs={{0,16},{4,20},{8,24},{12,28},{16,0},{20,4},{24,8},{28,12},{1,17},{... | collective-permute-start | bytes 196616 | tf_op jit(solution)/shard_map/ppermute | solution.py:22
  133.3 0.6 collective-permute-start.23
  133.8 4.5 %collective-permute-start.24 = (bf16[64,512]{1,0:T(8,128)(2,1)S(1)}, bf16[64,512]{1,0:T(8,128)(2,1)S(1)}, u32[]{:S(2)}, u32[]{:S(2)}) collective-permute-start(bf16[64,512]{1,0:T(8,128)(2,1)S(1)} %get-tuple-element.32), channel_id=1, source_target_pairs={{0,20},{4,24},{8,28},{12,0},{16,4},{20,8},{24,12},{28,16},{1,21},{... | collective-permute-start | bytes 196616 | tf_op jit(solution)/shard_map/ppermute | solution.py:22
  138.3 0.6 collective-permute-start.25
  138.9 3.6 %collective-permute-start.26 = (bf16[64,512]{1,0:T(8,128)(2,1)S(1)}, bf16[64,512]{1,0:T(8,128)(2,1)S(1)}, u32[]{:S(2)}, u32[]{:S(2)}) collective-permute-start(bf16[64,512]{1,0:T(8,128)(2,1)S(1)} %get-tuple-element.34), channel_id=1, source_target_pairs={{0,24},{4,28},{8,0},{12,4},{16,8},{20,12},{24,16},{28,20},{1,25},{... | collective-permute-start | bytes 196616 | tf_op jit(solution)/shard_map/ppermute | solution.py:22
  142.4 0.6 collective-permute-start.27
  143.0 0.8 collective-permute-done.23
  143.7 1.9 %collective-permute-start.28 = (bf16[64,512]{1,0:T(8,128)(2,1)S(1)}, bf16[64,512]{1,0:T(8,128)(2,1)S(1)}, u32[]{:S(2)}, u32[]{:S(2)}) collective-permute-start(bf16[64,512]{1,0:T(8,128)(2,1)S(1)} %get-tuple-element.36), channel_id=1, source_target_pairs={{0,28},{4,0},{8,4},{12,8},{16,12},{20,16},{24,20},{28,24},{1,29},{... | collective-permute-start | bytes 196616 | tf_op jit(solution)/shard_map/ppermute | solution.py:22
  145.7 2.2 %collective-permute-done.27 = bf16[64,512]{1,0:T(8,128)(2,1)S(1)} collective-permute-done((bf16[64,512]{1,0:T(8,128)(2,1)S(1)}, bf16[64,512]{1,0:T(8,128)(2,1)S(1)}, u32[]{:S(2)}, u32[]{:S(2)}) %collective-permute-start.27) | collective-permute-done | bytes 65568 | tf_op jit(solution)/shard_map/ppermute | solution.py:22
  147.9 0.1 collective-permute-done.28
  148.0 0.1 convert_add_fusion
  148.1 0.1 convert_reduce_fusion
  148.2 0.7 pad_maximum_fusion.2
  (32 shorter events, 0.1 us)
Async XLA Ops:
  0.0 12.0 %copy-start.3 = (s32[128,1]{0,1:T(1,128)S(1)}, s32[128,1]{0,1:T(1,128)}, u32[]{:S(2)}) copy-start(s32[128,1]{0,1:T(1,128)} %param.9) | copy-start | bytes 1540
  0.0 12.1 %copy-start.2 = (bf16[128,512]{1,0:T(8,128)(2,1)S(1)}, bf16[128,512]{1,0:T(8,128)(2,1)}, u32[]{:S(2)}) copy-start(bf16[128,512]{1,0:T(8,128)(2,1)} %param.10) | copy-start | bytes 393220
  0.0 27.0 %copy-start.4 = (bf16[128]{0:T(256)(128)(2,1)S(1)}, bf16[128]{0:T(256)(128)(2,1)}, u32[]{:S(2)}) copy-start(bf16[128]{0:T(256)(128)(2,1)} %param.11) | copy-start | bytes 772
  0.0 29.4 %copy-start = (f32[4,128]{1,0:T(4,128)S(1)}, f32[4,128]{1,0:T(4,128)}, u32[]{:S(2)}) copy-start(f32[4,128]{1,0:T(4,128)} %wind_x_ref.5) | copy-start | bytes 6148
  0.0 29.4 %copy-start.1 = (f32[4,128]{1,0:T(4,128)S(1)}, f32[4,128]{1,0:T(4,128)}, u32[]{:S(2)}) copy-start(f32[4,128]{1,0:T(4,128)} %wind_y_ref.5) | copy-start | bytes 6148
  3.0 24.1 %collective-permute-start.2 = (bf16[2320,128]{1,0:T(8,128)(2,1)}, bf16[2320,128]{1,0:T(8,128)(2,1)S(1)}, u32[]{:S(2)}, u32[]{:S(2)}) collective-permute-start(bf16[2320,128]{1,0:T(8,128)(2,1)} %get-tuple-element.23), channel_id=1, source_target_pairs={{0,4},{4,8},{8,12},{12,16},{16,20},{20,24},{24,28},{28,32},{32,36}... | collective-permute-start | bytes 1781768 | tf_op jit(solution)/shard_map/ppermute | solution.py:22
  4.9 24.5 %collective-permute-start.3 = (bf16[2320,128]{1,0:T(8,128)(2,1)}, bf16[2320,128]{1,0:T(8,128)(2,1)S(1)}, u32[]{:S(2)}, u32[]{:S(2)}) collective-permute-start(bf16[2320,128]{1,0:T(8,128)(2,1)} %get-tuple-element.24), channel_id=1, source_target_pairs={{0,252},{4,0},{8,4},{12,8},{16,12},{20,16},{24,20},{28,24},{32,28}... | collective-permute-start | bytes 1781768 | tf_op jit(solution)/shard_map/ppermute | solution.py:22
  13.6 24.7 %all-to-all-start = ((bf16[64,8,256]{2,1,0:T(8,128)(2,1)}), bf16[64,8,256]{2,1,0:T(8,128)(2,1)S(1)}, u32[]{:S(2)}, u32[]{:S(2)}) async-start(bf16[64,8,256]{2,1,0:T(8,128)(2,1)} %fusion), calls=%async_computation | async-start | bytes 524288 | tf_op jit(solution)/shard_map/all_to_all | solution.py:26
  20.6 15.4 %collective-permute-start = (bf16[784,128]{1,0:T(8,128)(2,1)}, bf16[784,128]{1,0:T(8,128)(2,1)S(1)}, u32[]{:S(2)}, u32[]{:S(2)}) collective-permute-start(bf16[784,128]{1,0:T(8,128)(2,1)} %get-tuple-element.21), channel_id=1, source_target_pairs={{0,4},{4,8},{8,12},{12,16},{16,20},{20,24},{24,28},{28,32},{32,36}... | collective-permute-start | bytes 602120 | tf_op jit(solution)/shard_map/ppermute | solution.py:22
  22.3 13.8 %collective-permute-start.1 = (bf16[784,128]{1,0:T(8,128)(2,1)}, bf16[784,128]{1,0:T(8,128)(2,1)S(1)}, u32[]{:S(2)}, u32[]{:S(2)}) collective-permute-start(bf16[784,128]{1,0:T(8,128)(2,1)} %get-tuple-element.22), channel_id=1, source_target_pairs={{0,252},{4,0},{8,4},{12,8},{16,12},{20,16},{24,20},{28,24},{32,28}... | collective-permute-start | bytes 602120 | tf_op jit(solution)/shard_map/ppermute | solution.py:22
  65.4 7.8 %collective-permute-start.4 = (bf16[128,512]{1,0:T(8,128)(2,1)S(1)}, bf16[128,512]{1,0:T(8,128)(2,1)S(1)}, u32[]{:S(2)}, u32[]{:S(2)}) collective-permute-start(bf16[128,512]{1,0:T(8,128)(2,1)S(1)} %get-tuple-element.38), channel_id=1, source_target_pairs={{0,0},{1,64},{2,128},{3,192},{32,32},{33,96},{34,160},{35,224},{64... | collective-permute-start | bytes 393224 | tf_op jit(solution)/shard_map/ppermute | solution.py:295
  68.3 7.4 %collective-permute-start.5 = (bf16[128,512]{1,0:T(8,128)(2,1)S(1)}, bf16[128,512]{1,0:T(8,128)(2,1)S(1)}, u32[]{:S(2)}, u32[]{:S(2)}) collective-permute-start(bf16[128,512]{1,0:T(8,128)(2,1)S(1)} %get-tuple-element.37), channel_id=1, source_target_pairs={{0,32},{1,96},{2,160},{3,224},{32,0},{33,64},{34,128},{35,192},{64... | collective-permute-start | bytes 393224 | tf_op jit(solution)/shard_map/ppermute | solution.py:296
  75.7 8.7 %collective-permute-start.6 = (bf16[256,512]{1,0:T(8,128)(2,1)S(1)}, bf16[256,512]{1,0:T(8,128)(2,1)S(1)}, u32[]{:S(2)}, u32[]{:S(2)}) collective-permute-start(bf16[256,512]{1,0:T(8,128)(2,1)S(1)} %pad_maximum_fusion.1), channel_id=1, source_target_pairs={{0,2},{2,0},{1,3},{3,1},{4,6},{6,4},{5,7},{7,5},{8,10},{10,8},{9,1... | collective-permute-start | bytes 786440 | tf_op jit(solution)/shard_map/ppermute | solution.py:22
  84.5 17.5 %collective-permute-start.7 = (bf16[512,512]{1,0:T(8,128)(2,1)S(1)}, bf16[512,512]{1,0:T(8,128)(2,1)S(1)}, u32[]{:S(2)}, u32[]{:S(2)}) collective-permute-start(bf16[512,512]{1,0:T(8,128)(2,1)S(1)} %pad_maximum_fusion), channel_id=1, source_target_pairs={{0,1},{1,0},{2,3},{3,2},{4,5},{5,4},{6,7},{7,6},{8,9},{9,8},{10,11... | collective-permute-start | bytes 1572872 | tf_op jit(solution)/shard_map/ppermute | solution.py:22
  84.7 6.0 %collective-permute-start.8 = (bf16[128,512]{1,0:T(8,128)(2,1)S(1)}, bf16[128,512]{1,0:T(8,128)(2,1)S(1)}, u32[]{:S(2)}, u32[]{:S(2)}) collective-permute-start(bf16[128,512]{1,0:T(8,128)(2,1)S(1)} %get-tuple-element.43.refs_0_), channel_id=1, source_target_pairs={{0,128},{128,0},{1,129},{129,1},{2,130},{130,2},{3,131},{131,3},{4... | collective-permute-start | bytes 393224 | tf_op jit(solution)/shard_map/ppermute | solution.py:22
  86.0 7.9 %collective-permute-start.10 = (bf16[128,512]{1,0:T(8,128)(2,1)S(1)}, bf16[128,512]{1,0:T(8,128)(2,1)S(1)}, u32[]{:S(2)}, u32[]{:S(2)}) collective-permute-start(bf16[128,512]{1,0:T(8,128)(2,1)S(1)} %get-tuple-element.43.refs_0_), channel_id=1, source_target_pairs={{0,64},{32,96},{64,0},{96,32},{1,65},{33,97},{65,1},{97,33},{2,66}... | collective-permute-start | bytes 393224 | tf_op jit(solution)/shard_map/ppermute | solution.py:22
  87.0 8.1 %collective-permute-start.11 = (bf16[128,512]{1,0:T(8,128)(2,1)S(1)}, bf16[128,512]{1,0:T(8,128)(2,1)S(1)}, u32[]{:S(2)}, u32[]{:S(2)}) collective-permute-start(bf16[128,512]{1,0:T(8,128)(2,1)S(1)} %get-tuple-element.43.refs_0_), channel_id=1, source_target_pairs={{0,96},{32,0},{64,32},{96,64},{1,97},{33,1},{65,33},{97,65},{2,98}... | collective-permute-start | bytes 393224 | tf_op jit(solution)/shard_map/ppermute | solution.py:22
  90.1 7.9 %collective-permute-start.9 = (bf16[128,512]{1,0:T(8,128)(2,1)S(1)}, bf16[128,512]{1,0:T(8,128)(2,1)S(1)}, u32[]{:S(2)}, u32[]{:S(2)}) collective-permute-start(bf16[128,512]{1,0:T(8,128)(2,1)S(1)} %get-tuple-element.43.refs_0_), channel_id=1, source_target_pairs={{0,32},{32,64},{64,96},{96,0},{1,33},{33,65},{65,97},{97,1},{2,34}... | collective-permute-start | bytes 393224 | tf_op jit(solution)/shard_map/ppermute | solution.py:22
  90.6 11.3 %collective-permute-start.12 = (bf16[128,512]{1,0:T(8,128)(2,1)S(1)}, bf16[128,512]{1,0:T(8,128)(2,1)S(1)}, u32[]{:S(2)}, u32[]{:S(2)}) collective-permute-start(bf16[128,512]{1,0:T(8,128)(2,1)S(1)} %collective-permute-done.8.refs_1_), channel_id=1, source_target_pairs={{0,32},{32,64},{64,96},{96,0},{1,33},{33,65},{65,97},{97,1},{2,34}... | collective-permute-start | bytes 393224 | tf_op jit(solution)/shard_map/ppermute | solution.py:22
  93.9 8.0 %collective-permute-start.13 = (bf16[128,512]{1,0:T(8,128)(2,1)S(1)}, bf16[128,512]{1,0:T(8,128)(2,1)S(1)}, u32[]{:S(2)}, u32[]{:S(2)}) collective-permute-start(bf16[128,512]{1,0:T(8,128)(2,1)S(1)} %collective-permute-done.8.refs_1_), channel_id=1, source_target_pairs={{0,64},{32,96},{64,0},{96,32},{1,65},{33,97},{65,1},{97,33},{2,66}... | collective-permute-start | bytes 393224 | tf_op jit(solution)/shard_map/ppermute | solution.py:22
  95.1 6.8 %collective-permute-start.14 = (bf16[128,512]{1,0:T(8,128)(2,1)S(1)}, bf16[128,512]{1,0:T(8,128)(2,1)S(1)}, u32[]{:S(2)}, u32[]{:S(2)}) collective-permute-start(bf16[128,512]{1,0:T(8,128)(2,1)S(1)} %collective-permute-done.8.refs_1_), channel_id=1, source_target_pairs={{0,96},{32,0},{64,32},{96,64},{1,97},{33,1},{65,33},{97,65},{2,98}... | collective-permute-start | bytes 393224 | tf_op jit(solution)/shard_map/ppermute | solution.py:22
  104.3 43.7 %all-to-all-start.2 = ((bf16[8,64,512]{2,1,0:T(8,128)(2,1)}), bf16[8,64,512]{2,1,0:T(8,128)(2,1)S(1)}, u32[]{:S(2)}, u32[]{:S(2)}) async-start(bf16[8,64,512]{2,1,0:T(8,128)(2,1)} %bitcast.28), calls=%async_computation.2 | async-start | bytes 1048576 | tf_op jit(solution)/shard_map/all_to_all | solution.py:26
  108.2 6.3 %collective-permute-start.15 = (bf16[128,512]{1,0:T(8,128)(2,1)S(1)}, bf16[128,512]{1,0:T(8,128)(2,1)S(1)}, u32[]{:S(2)}, u32[]{:S(2)}) collective-permute-start(bf16[128,512]{1,0:T(8,128)(2,1)S(1)} %get-tuple-element.44.refs_0_), channel_id=1, source_target_pairs={{0,128},{128,0},{1,129},{129,1},{2,130},{130,2},{3,131},{131,3},{4... | collective-permute-start | bytes 393224 | tf_op jit(solution)/shard_map/ppermute | solution.py:22
  110.0 8.1 %collective-permute-start.16 = (bf16[128,512]{1,0:T(8,128)(2,1)S(1)}, bf16[128,512]{1,0:T(8,128)(2,1)S(1)}, u32[]{:S(2)}, u32[]{:S(2)}) collective-permute-start(bf16[128,512]{1,0:T(8,128)(2,1)S(1)} %get-tuple-element.44.refs_0_), channel_id=1, source_target_pairs={{0,32},{32,64},{64,96},{96,0},{1,33},{33,65},{65,97},{97,1},{2,34}... | collective-permute-start | bytes 393224 | tf_op jit(solution)/shard_map/ppermute | solution.py:22
  111.0 10.7 %collective-permute-start.17 = (bf16[128,512]{1,0:T(8,128)(2,1)S(1)}, bf16[128,512]{1,0:T(8,128)(2,1)S(1)}, u32[]{:S(2)}, u32[]{:S(2)}) collective-permute-start(bf16[128,512]{1,0:T(8,128)(2,1)S(1)} %get-tuple-element.44.refs_0_), channel_id=1, source_target_pairs={{0,64},{32,96},{64,0},{96,32},{1,65},{33,97},{65,1},{97,33},{2,66}... | collective-permute-start | bytes 393224 | tf_op jit(solution)/shard_map/ppermute | solution.py:22
  114.5 7.2 %collective-permute-start.18 = (bf16[128,512]{1,0:T(8,128)(2,1)S(1)}, bf16[128,512]{1,0:T(8,128)(2,1)S(1)}, u32[]{:S(2)}, u32[]{:S(2)}) collective-permute-start(bf16[128,512]{1,0:T(8,128)(2,1)S(1)} %get-tuple-element.44.refs_0_), channel_id=1, source_target_pairs={{0,96},{32,0},{64,32},{96,64},{1,97},{33,1},{65,33},{97,65},{2,98}... | collective-permute-start | bytes 393224 | tf_op jit(solution)/shard_map/ppermute | solution.py:22
  114.5 8.5 %collective-permute-start.19 = (bf16[128,512]{1,0:T(8,128)(2,1)S(1)}, bf16[128,512]{1,0:T(8,128)(2,1)S(1)}, u32[]{:S(2)}, u32[]{:S(2)}) collective-permute-start(bf16[128,512]{1,0:T(8,128)(2,1)S(1)} %collective-permute-done.15.refs_1_), channel_id=1, source_target_pairs={{0,32},{32,64},{64,96},{96,0},{1,33},{33,65},{65,97},{97,1},{2,34}... | collective-permute-start | bytes 393224 | tf_op jit(solution)/shard_map/ppermute | solution.py:22
  116.5 9.5 %collective-permute-start.20 = (bf16[128,512]{1,0:T(8,128)(2,1)S(1)}, bf16[128,512]{1,0:T(8,128)(2,1)S(1)}, u32[]{:S(2)}, u32[]{:S(2)}) collective-permute-start(bf16[128,512]{1,0:T(8,128)(2,1)S(1)} %collective-permute-done.15.refs_1_), channel_id=1, source_target_pairs={{0,64},{32,96},{64,0},{96,32},{1,65},{33,97},{65,1},{97,33},{2,66}... | collective-permute-start | bytes 393224 | tf_op jit(solution)/shard_map/ppermute | solution.py:22
  118.1 7.9 %collective-permute-start.21 = (bf16[128,512]{1,0:T(8,128)(2,1)S(1)}, bf16[128,512]{1,0:T(8,128)(2,1)S(1)}, u32[]{:S(2)}, u32[]{:S(2)}) collective-permute-start(bf16[128,512]{1,0:T(8,128)(2,1)S(1)} %collective-permute-done.15.refs_1_), channel_id=1, source_target_pairs={{0,96},{32,0},{64,32},{96,64},{1,97},{33,1},{65,33},{97,65},{2,98}... | collective-permute-start | bytes 393224 | tf_op jit(solution)/shard_map/ppermute | solution.py:22
  127.7 14.7 %collective-permute-start.22 = (bf16[64,512]{1,0:T(8,128)(2,1)S(1)}, bf16[64,512]{1,0:T(8,128)(2,1)S(1)}, u32[]{:S(2)}, u32[]{:S(2)}) collective-permute-start(bf16[64,512]{1,0:T(8,128)(2,1)S(1)} %get-tuple-element.30), channel_id=1, source_target_pairs={{0,16},{4,20},{8,24},{12,28},{16,0},{20,4},{24,8},{28,12},{1,17},{... | collective-permute-start | bytes 196616 | tf_op jit(solution)/shard_map/ppermute | solution.py:22
  133.3 10.5 %collective-permute-start.23 = (bf16[64,512]{1,0:T(8,128)(2,1)S(1)}, bf16[64,512]{1,0:T(8,128)(2,1)S(1)}, u32[]{:S(2)}, u32[]{:S(2)}) collective-permute-start(bf16[64,512]{1,0:T(8,128)(2,1)S(1)} %get-tuple-element.31), channel_id=1, source_target_pairs={{0,12},{4,16},{8,20},{12,24},{16,28},{20,0},{24,4},{28,8},{1,13},{... | collective-permute-start | bytes 196616 | tf_op jit(solution)/shard_map/ppermute | solution.py:22
  133.8 11.8 %collective-permute-start.24 = (bf16[64,512]{1,0:T(8,128)(2,1)S(1)}, bf16[64,512]{1,0:T(8,128)(2,1)S(1)}, u32[]{:S(2)}, u32[]{:S(2)}) collective-permute-start(bf16[64,512]{1,0:T(8,128)(2,1)S(1)} %get-tuple-element.32), channel_id=1, source_target_pairs={{0,20},{4,24},{8,28},{12,0},{16,4},{20,8},{24,12},{28,16},{1,21},{... | collective-permute-start | bytes 196616 | tf_op jit(solution)/shard_map/ppermute | solution.py:22
  138.3 7.4 %collective-permute-start.25 = (bf16[64,512]{1,0:T(8,128)(2,1)S(1)}, bf16[64,512]{1,0:T(8,128)(2,1)S(1)}, u32[]{:S(2)}, u32[]{:S(2)}) collective-permute-start(bf16[64,512]{1,0:T(8,128)(2,1)S(1)} %get-tuple-element.33), channel_id=1, source_target_pairs={{0,8},{4,12},{8,16},{12,20},{16,24},{20,28},{24,0},{28,4},{1,9},{5... | collective-permute-start | bytes 196616 | tf_op jit(solution)/shard_map/ppermute | solution.py:22
  138.9 6.8 %collective-permute-start.26 = (bf16[64,512]{1,0:T(8,128)(2,1)S(1)}, bf16[64,512]{1,0:T(8,128)(2,1)S(1)}, u32[]{:S(2)}, u32[]{:S(2)}) collective-permute-start(bf16[64,512]{1,0:T(8,128)(2,1)S(1)} %get-tuple-element.34), channel_id=1, source_target_pairs={{0,24},{4,28},{8,0},{12,4},{16,8},{20,12},{24,16},{28,20},{1,25},{... | collective-permute-start | bytes 196616 | tf_op jit(solution)/shard_map/ppermute | solution.py:22
  142.4 5.5 %collective-permute-start.27 = (bf16[64,512]{1,0:T(8,128)(2,1)S(1)}, bf16[64,512]{1,0:T(8,128)(2,1)S(1)}, u32[]{:S(2)}, u32[]{:S(2)}) collective-permute-start(bf16[64,512]{1,0:T(8,128)(2,1)S(1)} %get-tuple-element.35), channel_id=1, source_target_pairs={{0,4},{4,8},{8,12},{12,16},{16,20},{20,24},{24,28},{28,0},{1,5},{5... | collective-permute-start | bytes 196616 | tf_op jit(solution)/shard_map/ppermute | solution.py:22
  143.7 4.3 %collective-permute-start.28 = (bf16[64,512]{1,0:T(8,128)(2,1)S(1)}, bf16[64,512]{1,0:T(8,128)(2,1)S(1)}, u32[]{:S(2)}, u32[]{:S(2)}) collective-permute-start(bf16[64,512]{1,0:T(8,128)(2,1)S(1)} %get-tuple-element.36), channel_id=1, source_target_pairs={{0,28},{4,0},{8,4},{12,8},{16,12},{20,16},{24,20},{28,24},{1,29},{... | collective-permute-start | bytes 196616 | tf_op jit(solution)/shard_map/ppermute | solution.py:22
